TPU v7x, 32 devices: a whole 2x2x4 slice. The times are simulated.
32 devices in a mesh: dp: 8 (over z, x), tensor: 4 (over y, core).
Axes of the slice: x: 2, y: 2, z: 4, core: 2. Of those that a mesh axis runs over, the one named last changes fastest.
Arguments:
- hidden_in: bfloat16 [16384, 1024], P('dp'), may hold values from -6 to 6
- doc_ids: int32 [8, 2048], P('dp'), may hold values from 0 to 4, never falling along the last dimension, each value on 1 to 800 neighbouring positions
- cotangent: bfloat16 [16384, 1024], P('dp'), may hold values from -6 to 6
- norm_gain: float32 [1024], replicated, may hold values from 0.5 to 1.5
- in_weight: bfloat16 [1024, 4384], P('dp'), may hold values from -0.1875 to 0.1875
- conv_weight: bfloat16 [4, 2304], replicated, may hold values from -3 to 3
- conv_bias: float32 [2304], replicated, may hold values from -1.5 to 1.5
- dt_bias: float32 [32], replicated, may hold values from -6.9 to -2.3
- log_decay: float32 [32], replicated, may hold values from 0 to 2.77
- skip_gain: float32 [32], replicated, may hold values from 0.5 to 1.5
- gate_gain: float32 [2048], replicated, may hold values from 0.5 to 1.5
- out_weight: bfloat16 [1024, 2048], P('dp', 'tensor'), may hold values from -0.125 to 0.125
Outputs:
- layer_out: bfloat16 [16384, 1024], P('dp')
- grad_input: float32 [16384, 1024], P('dp')
- grad_norm_gain: float32 [1024], replicated
- grad_in_weight: float32 [1024, 4384], P('dp')
- grad_conv_weight: float32 [4, 2304], replicated
- grad_conv_bias: float32 [2304], replicated
- grad_dt_bias: float32 [32], replicated
- grad_log_decay: float32 [32], replicated
- grad_skip_gain: float32 [32], replicated
- grad_gate_gain: float32 [2048], replicated
- grad_out_weight: float32 [1024, 2048], P('dp', 'tensor')
Inputs may be any that keep to these rules, and one draw needn't show every extreme that they name: `doc_ids`: within each sequence the ids start at 0 and never fall; each document has 1 to 800 tokens, and one has exactly 800.
All inputs are finite; a program needn't handle non-finite values.
Results may differ from a plain program's by a relative error of at most 0.0065.
Values may be sent and summed in bfloat16 or wider, within the bound.
A program may use at most 256 MiB of HBM per device.

v0:
```python
import jax
import jax.numpy as jnp
from jax import lax
from jax.experimental import pallas as pl
from jax.experimental.pallas import tpu as pltpu
from jax.sharding import PartitionSpec as P

SPAN = 256
LANES = 128
EPS = 1e-05
FAR = -1e30
VMEM_MOST = 60 * 2**20
F32 = jnp.float32
BF16 = jnp.bfloat16


def cost(micros):
    return pl.CostEstimate(flops=int(micros * 1.15e9), bytes_accessed=1 << 20, transcendentals=0)


def nn(a, b):
    return lax.dot_general(a, b, (((1,), (0,)), ((), ())), preferred_element_type=F32)


def nt(a, b):
    return lax.dot_general(a, b, (((1,), (1,)), ((), ())), preferred_element_type=F32)


def tn(a, b):
    return lax.dot_general(a, b, (((0,), (0,)), ((), ())), preferred_element_type=F32)


def iota(shape, dim):
    return lax.broadcasted_iota(jnp.int32, shape, dim)


def as_column(row, rows=SPAN):
    return jnp.transpose(jnp.broadcast_to(row, (LANES, rows)))


def as_row(block):
    return jnp.sum(jnp.transpose(block), axis=0, keepdims=True)


def split3(v):
    hi = v.astype(BF16)
    rest = v - hi.astype(F32)
    mid = rest.astype(BF16)
    low = (rest - mid.astype(F32)).astype(BF16)
    return hi, mid, low


def tri_sum(tri, v, heads):
    lane = iota(v.shape, 1)
    v = jnp.where(lane < heads, v, 0.0)
    hi = v.astype(BF16).astype(F32)
    rest = v - hi
    mid = rest.astype(BF16).astype(F32)
    low = rest - mid
    packed = hi + pltpu.roll(mid, heads, 1) + pltpu.roll(low, 2 * heads, 1)
    out = nn(tri, packed.astype(BF16))
    return out + pltpu.roll(out, LANES - heads, 1) + pltpu.roll(out, LANES - 2 * heads, 1)


def pair_lanes(cols, pair, low_half):
    rows = cols.shape[0]
    first = jnp.broadcast_to(cols[:, 2 * pair : 2 * pair + 1], (rows, LANES))
    second = jnp.broadcast_to(cols[:, 2 * pair + 1 : 2 * pair + 2], (rows, LANES))
    return jnp.where(low_half, first, second)


def exact_nt(a, b):
    a_hi, b_hi = a.astype(BF16), b.astype(BF16)
    a_lo = (a - a_hi.astype(F32)).astype(BF16)
    b_lo = (b - b_hi.astype(F32)).astype(BF16)
    return nt(a_hi, b_hi) + (nt(a_hi, b_lo) + nt(a_lo, b_hi))


def softplus(v):
    return jnp.maximum(v, 0.0) + jnp.log1p(jnp.exp(-jnp.abs(v)))


def own_lanes(row, rank, heads):
    total = row.shape[1]
    pick = (iota((total, LANES), 0) == rank * heads + iota((total, LANES), 1)) & (
        iota((total, LANES), 1) < heads
    )
    wide = jnp.broadcast_to(row, (8, total))
    out = lax.dot_general(
        wide, pick.astype(F32), (((1,), (0,)), ((), ())),
        precision=lax.Precision.HIGHEST, preferred_element_type=F32,
    )
    return out[0:1]


def fold(v):
    return jnp.sum(v.reshape(SPAN // 8, 8, v.shape[1]), axis=0)


def own_params(rank, heads, inner, inner_all, dtb_ref, dec_ref, skip_ref, cw_ref, cb_ref, par, cwb):
    chan = inner + 2 * LANES
    off = pl.multiple_of(rank * inner, LANES)
    taps = cw_ref.shape[0]
    par[0:1] = own_lanes(dtb_ref[...], rank, heads)
    par[1:2] = -jnp.exp(own_lanes(dec_ref[...], rank, heads))
    par[2:3] = own_lanes(skip_ref[...], rank, heads)
    cwb[0:taps, 0:inner] = cw_ref[:, pl.ds(off, inner)].astype(F32)
    cwb[0:taps, inner:chan] = cw_ref[:, inner_all:].astype(F32)
    cwb[taps : taps + 1, 0:inner] = cb_ref[:, pl.ds(off, inner)]
    cwb[taps : taps + 1, inner:chan] = cb_ref[:, inner_all:]


MESH_IDS = pl.DeviceIdType.MESH


def forward_kernel(
    dims, docs_ref, normed_ref, cot_ref, win_ref, wout_ref, cw_ref, cb_ref,
    dtb_ref, dec_ref, skip_ref, ggain_ref,
    gate_ref, mixed_ref, pre_ref, ssd_ref, stp_ref, state_ref, dn_ref,
    sums_ref, mine_ref, far_ref,
    xbuf, dbuf, state, par, cwb, gain, gg_ref,
    own_sums, h_out, h_in, kept, mine, far, h_sem, y_sem, s_in, s_sem, put_sem,
):
    inner, heads, early = dims
    pairs = heads // 2
    chan = inner + 2 * LANES
    i = pl.program_id(0)
    spans = pl.num_programs(0)
    rank = lax.axis_index("tensor")
    core = rank % 2
    inner_all = ggain_ref.shape[1]
    half = SPAN // 2
    across = {"tensor": rank + 1 - 2 * core}
    beyond = {"tensor": (rank + 2) % 4}
    crossed = {"tensor": (rank + 3 - 2 * core) % 4}

    @pl.when(i == 0)
    def _():
        barrier = pltpu.get_barrier_semaphore()
        for device in (across, beyond, crossed):
            pl.semaphore_signal(barrier, inc=1, device_id=device, device_id_type=MESH_IDS)
        pl.semaphore_wait(barrier, 3)
        xbuf[0:8] = jnp.zeros((8, chan), F32)
        dbuf[0:8] = jnp.full((8, LANES), -1.0, F32)
        state[...] = jnp.zeros(state.shape, F32)
        own_params(rank, heads, inner, inner_all, dtb_ref, dec_ref, skip_ref, cw_ref, cb_ref, par, cwb)
        gain[0:1] = ggain_ref[:, pl.ds(pl.multiple_of(rank * inner, LANES), inner)]

    def slot(k):
        return pl.ds(pl.multiple_of(k * half, half), half)

    def h_copy(k):
        return pltpu.make_async_remote_copy(
            src_ref=h_out.at[slot(k)], dst_ref=h_in.at[slot(k)], send_sem=h_sem.at[0, k],
            recv_sem=h_sem.at[1, k], device_id=across, device_id_type=MESH_IDS,
        )

    def y_copy(k):
        return pltpu.make_async_remote_copy(
            src_ref=mine.at[slot(k)], dst_ref=far.at[slot(k)], send_sem=y_sem.at[0, k],
            recv_sem=y_sem.at[1, k], device_id=beyond, device_id_type=MESH_IDS,
        )

    def join(k):
        h_copy(k).wait_recv()
        mine[slot(k)] = (kept[...] + h_in[slot(k)].astype(F32)).astype(BF16)

    @pl.when(i > 0)
    def _():
        join(i - 1)

        @pl.when(i - 1 < early)
        def _():
            y_copy(i - 1).start()

    nb = normed_ref[...]
    xbuf[8 : 8 + SPAN] = nn(nb, win_ref[:, inner : inner + chan])
    gate_ref[...] = nn(nb, win_ref[:, 0:inner])
    stp = nn(nb, win_ref[:, inner + chan : inner + chan + LANES])
    stp_ref[...] = stp
    mixed_ref[...] = xbuf[8 : 8 + SPAN]
    dn_ref[...] = nn(cot_ref[...], wout_ref[...])

    drow = docs_ref[:, pl.ds(pl.multiple_of(i * SPAN, SPAN), SPAN)].astype(F32)
    dcol = as_column(drow)
    enter = dbuf[7:8]
    dbuf[8 : 8 + SPAN] = dcol
    keeps = [None] + [dbuf[8 - k : 8 - k + SPAN] == dcol for k in range(1, 4)]

    def conv(group):
        lanes = slice(group * LANES, (group + 1) * LANES)
        acc = cwb[4:5, lanes] + cwb[3:4, lanes] * xbuf[8 : 8 + SPAN, lanes]
        for k in range(1, 4):
            acc = acc + cwb[3 - k : 4 - k, lanes] * jnp.where(
                keeps[k], xbuf[8 - k : 8 - k + SPAN, lanes], 0.0
            )
        pre_ref[:, lanes] = acc
        return acc * jax.nn.sigmoid(acc)

    b_act, c_act = conv(pairs), conv(pairs + 1)
    b_rows, c_rows = b_act.astype(BF16), c_act.astype(BF16)

    step = softplus(stp + par[0:1])
    row_i, col_i = iota((SPAN, SPAN), 0), iota((SPAN, SPAN), 1)
    tril = (row_i >= col_i).astype(BF16)
    running = tri_sum(tril, step * par[1:2], heads)
    run_rows = jnp.transpose(running)
    ending = running[SPAN - 1 : SPAN]
    tail = jnp.where(dcol == dcol[SPAN - 1 : SPAN], jnp.exp(ending - running), 0.0)
    reach = jnp.where(dcol == enter, jnp.exp(running), 0.0)
    same = jnp.concatenate([dcol, dcol], 1) == drow
    bias = jnp.where(same & (row_i >= col_i), 0.0, FAR)
    scores = exact_nt(c_act, b_act)
    b_turned = jnp.transpose(b_act).astype(BF16)
    low_half = iota((SPAN, LANES), 1) < LANES // 2
    square = jnp.zeros((SPAN, LANES), F32)
    cross = jnp.zeros((SPAN, LANES), F32)
    for pair in range(pairs):
        lanes = slice(pair * LANES, (pair + 1) * LANES)
        act = conv(pair)
        scaled = act * pair_lanes(step, pair, low_half)
        xb = scaled.astype(BF16)
        tail_l = pair_lanes(tail, pair, low_half)
        reach_l = pair_lanes(reach, pair, low_half)
        held = state[:, lanes]
        held_b = held.astype(BF16)
        state_ref[0, :, lanes] = held_b
        state[:, lanes] = nn(b_turned, (scaled * tail_l).astype(BF16)) + reach_l[SPAN - 1 : SPAN] * held
        out = reach_l * nn(c_rows, held_b)
        parts = []
        for sub in range(2):
            head = 2 * pair + sub
            blocks = []
            for blk in range(2):
                rows = slice(blk * half, (blk + 1) * half)
                width = (blk + 1) * half
                gap = running[rows, head : head + 1] - run_rows[head : head + 1, 0:width]
                weight = jnp.exp(gap + bias[rows, 0:width]) * scores[rows, 0:width]
                blocks.append(nn(weight.astype(BF16), xb[0:width]))
            parts.append(jnp.concatenate(blocks, 0))
        out = out + jnp.where(low_half, parts[0], parts[1])
        skip_l = pair_lanes(par[2:3], pair, low_half[0:1])
        ssd = out + skip_l * act
        ssd_ref[:, lanes] = ssd
        gate = gate_ref[:, lanes]
        gated = ssd * (gate * jax.nn.sigmoid(gate))
        square = square + gated * gated
        gained = gain[0:1, lanes] * gated
        gg_ref[:, lanes] = gained.astype(BF16)
        cross = cross + dn_ref[:, lanes] * gained
    own_sums[0, pl.ds(i, 1), :] = as_row(square)
    own_sums[1, pl.ds(i, 1), :] = as_row(cross)
    xbuf[0:8] = xbuf[SPAN : SPAN + 8]
    dbuf[0:8] = dbuf[SPAN : SPAN + 8]
    h_out[slot(i)] = nt(gg_ref[slot(1 - core)], wout_ref[...]).astype(BF16)
    h_copy(i).start()
    kept[...] = nt(gg_ref[slot(core)], wout_ref[...])

    @pl.when(i == spans - 1)
    def _():
        def s_copy(k, device):
            return pltpu.make_async_remote_copy(
                src_ref=own_sums, dst_ref=s_in.at[k], send_sem=s_sem.at[0, k],
                recv_sem=s_sem.at[1, k], device_id=device, device_id_type=MESH_IDS,
            )

        sent = [s_copy(0, across), s_copy(1, beyond), s_copy(2, crossed)]
        for copy in sent:
            copy.start()
        join(i)
        mine_put = pltpu.make_async_copy(mine, mine_ref, put_sem.at[0])
        mine_put.start()
        for copy in sent:
            copy.wait_recv()
        near = own_sums[...] + s_in[0]
        sums_ref[...] = near + (s_in[1] + s_in[2])
        for k in range(early):
            y_copy(k).wait_recv()
        far_put = pltpu.make_async_copy(far, far_ref, put_sem.at[1])
        far_put.start()
        for copy in sent:
            copy.wait_send()

        def drain(k, carry):
            h_copy(k).wait_send()
            return carry

        lax.fori_loop(0, spans, drain, 0)
        for k in range(early):
            y_copy(k).wait_send()
        mine_put.wait()
        far_put.wait()


def mixer_forward(docs, normed, cotangent, w_in, w_out, params, ggain, heads, early):
    tokens, model = normed.shape
    inner = w_out.shape[1]
    chan = inner + 2 * LANES
    spans = tokens // SPAN

    def tok(width):
        return pl.BlockSpec((SPAN, width), lambda i: (i, 0))

    def full(shape):
        return pl.BlockSpec(shape, lambda i: (0,) * len(shape))

    anywhere = pl.BlockSpec(memory_space=pl.ANY)
    sums = (2, spans, SPAN)
    outs = (
        jax.ShapeDtypeStruct((tokens, inner), F32),
        jax.ShapeDtypeStruct((tokens, chan), F32),
        jax.ShapeDtypeStruct((tokens, chan), F32),
        jax.ShapeDtypeStruct((tokens, inner), F32),
        jax.ShapeDtypeStruct((tokens, LANES), F32),
        jax.ShapeDtypeStruct((spans, LANES, inner), BF16),
        jax.ShapeDtypeStruct((tokens, inner), F32),
        jax.ShapeDtypeStruct(sums, F32),
        jax.ShapeDtypeStruct((tokens // 2, model), BF16),
        jax.ShapeDtypeStruct((early * SPAN // 2, model), BF16),
    )
    out_specs = (
        tok(inner), tok(chan), tok(chan), tok(inner), tok(LANES),
        pl.BlockSpec((1, LANES, inner), lambda i: (i, 0, 0)),
        tok(inner), full(sums), anywhere, anywhere,
    )
    consts = (w_in, w_out) + params + (ggain,)
    dma, vmem = pltpu.SemaphoreType.DMA, pltpu.VMEM
    return pl.pallas_call(
        lambda *refs: forward_kernel((inner, heads, early), *refs),
        out_shape=outs,
        grid=(spans,),
        in_specs=[full(docs.shape), tok(model), tok(model)] + [full(v.shape) for v in consts],
        out_specs=out_specs,
        scratch_shapes=[
            vmem((SPAN + 8, chan), F32), vmem((SPAN + 8, LANES), F32), vmem((LANES, inner), F32),
            vmem((8, LANES), F32), vmem((8, chan), F32), vmem((8, inner), F32),
            vmem((SPAN, inner), BF16), vmem(sums, F32),
            vmem((tokens // 2, model), BF16), vmem((tokens // 2, model), BF16),
            vmem((SPAN // 2, model), F32), vmem((tokens // 2, model), BF16),
            vmem((early * SPAN // 2, model), BF16),
            dma((2, spans)), dma((2, early)), vmem((3,) + sums, F32), dma((2, 3)), dma((2,)),
        ],
        compiler_params=pltpu.CompilerParams(
            dimension_semantics=("arbitrary",), vmem_limit_bytes=VMEM_MOST,
            collective_id=2, has_side_effects=True,
        ),
        cost_estimate=cost(40.0),
        name="mixer_forward",
    )(docs, normed, cotangent, *consts)


def backward_kernel(
    dims,
    docs_ref, hid_ref, gate_ref, dn_ref, gate_low_ref, ssd_low_ref, dn_low_ref,
    ssd_ref, mixed_ref, pre_ref, stp_ref, state_ref, sums_ref,
    cw_ref, cb_ref, dtb_ref, dec_ref, skip_ref, ggain_ref, ngain_ref,
    naway_ref, nhere_ref, caway_ref, chere_ref, w_ref, mine_ref, far_ref,
    delta_ref, layer_ref, gin_ref, gout_ref, flatout_ref,
    naway, nhere, caway, chere, w, loads,
    pbuf, dbuf, dstate, par, cwb, gain,
    gconv, gskip, ghead, ggain, gnorm,
    nout_all, dgate_all, dall, dssd_low, inv_now, inv_own, hid_own,
    h_out, mine, y_in, kept, h_sem, y_sem, d_sem, d_put,
    omine, ofar, oy_sem, o_sem, o_put,
    ax_out, ax_in, ax_sem, az_in, az_sem, atotal,
    bx_out, bx_in, bx_sem, bz_in, bz_sem, btotal,
    gates, g_sem, values, v_sem, shared, s_sem, put_sem, flat, flat_in, f_sem,
):
    inner, heads, inner_all, lines, depth, early = dims
    pairs = heads // 2
    chan = inner + 2 * LANES
    width = inner + chan + LANES
    i = pl.program_id(0)
    spans = pl.num_programs(0)
    tokens = nout_all.shape[0]
    count = tokens // SPAN
    mid = count // 2
    c = count - 1 - i
    half = SPAN // 2
    model = w.shape[0]
    blocks = lines * depth // LANES
    rank, drank = lax.axis_index("tensor"), lax.axis_index("dp")
    line, side = drank // 2, drank % 2
    core = rank % 2
    off = pl.multiple_of(rank * inner, LANES)
    across = {"tensor": rank + 1 - 2 * core}
    beyond = {"tensor": (rank + 2) % 4}
    partner = {"dp": line * 2 + 1 - side}

    def peer(step):
        return {"dp": lax.rem(line + step, lines) * 2 + side}

    def remote(src, dst, sems, index, device):
        return pltpu.make_async_remote_copy(
            src_ref=src, dst_ref=dst, send_sem=sems.at[0, index], recv_sem=sems.at[1, index],
            device_id=device, device_id_type=MESH_IDS,
        )

    def lot(k, size):
        return pl.ds(pl.multiple_of(k * size, size), size)

    fetch = [
        pltpu.make_async_copy(src, dst, loads.at[k])
        for k, (src, dst) in enumerate(
            (
                (mine_ref, omine), (w_ref, w), (far_ref, ofar.at[pl.ds(0, early * half)]),
                (caway_ref, caway), (naway_ref, naway), (chere_ref, chere), (nhere_ref, nhere),
            )
        )
    ]

    def oy_copy(k):
        return remote(omine.at[lot(k, half)], ofar.at[lot(k, half)], oy_sem, k - early, beyond)

    def my_rows(k):
        return pl.ds(pl.multiple_of(k * SPAN + core * half, half), half)

    def o_copy(k):
        return remote(omine.at[lot(k, half)], layer_ref.at[my_rows(k)], o_sem, k, across)

    def o_local(k):
        return pltpu.make_async_copy(omine.at[lot(k, half)], layer_ref.at[my_rows(k)], o_put.at[k])

    def d_copy(k):
        return remote(mine.at[lot(k, half)], delta_ref.at[my_rows(k)], d_sem, k, across)

    def d_local(k):
        return pltpu.make_async_copy(mine.at[lot(k, half)], delta_ref.at[my_rows(k)], d_put.at[k])

    def h_copy(k):
        return remote(h_out.at[lot(k, half)], mine.at[lot(k, half)], h_sem, k, across)

    def y_copy(k):
        return remote(mine.at[lot(k, half)], y_in.at[lot(k, half)], y_sem, k, beyond)

    def ax_copy(k):
        return remote(ax_out.at[lot(k, LANES)], ax_in.at[lot(k, LANES)], ax_sem, k, partner)

    def bx_copy(k):
        return remote(bx_out.at[lot(k, LANES)], bx_in.at[lot(k, LANES)], bx_sem, k, partner)

    def az_copy(step):
        return remote(ax_out.at[pl.ds(step * depth, depth)], az_in.at[step - 1], az_sem, step - 1, peer(step))

    def bz_copy(step):
        return remote(bx_out.at[pl.ds(step * depth, depth)], bz_in.at[step - 1], bz_sem, step - 1, peer(step))

    @pl.when(i == 0)
    def _():
        barrier = pltpu.get_barrier_semaphore()
        for device in [across, beyond, partner] + [peer(step) for step in range(1, lines)]:
            pl.semaphore_signal(barrier, inc=1, device_id=device, device_id_type=MESH_IDS)
        pl.semaphore_wait(barrier, lines + 2)
        for copy in fetch:
            copy.start()
        pbuf[SPAN : SPAN + 8] = jnp.zeros((8, chan), F32)
        dbuf[SPAN : SPAN + 8] = jnp.full((8, LANES), -2.0, F32)
        dstate[...] = jnp.zeros(dstate.shape, F32)
        own_params(rank, heads, inner, inner_all, dtb_ref, dec_ref, skip_ref, cw_ref, cb_ref, par, cwb)
        gain[0:1] = ggain_ref[:, pl.ds(off, inner)]
        for acc in (gconv, gskip, ghead, ggain, gnorm):
            acc[...] = jnp.zeros(acc.shape, F32)
        fetch[0].wait()
        for k in range(early, count):
            oy_copy(k).start()

    def join(k):
        h_copy(k).wait_recv()
        mine[lot(k, half)] = (kept[...] + mine[lot(k, half)].astype(F32)).astype(BF16)
        y_copy(k).start()

    @pl.when(i > 0)
    def _():
        join(c + 1)

    def out_grads(n_side, c_side, k):
        cols = lot(k, LANES)
        return jnp.concatenate(
            [tn(c_side[:, cols], nout_all[...]), tn(n_side[:, cols], dgate_all[...])], 1
        )

    def scan_grads(n_side, k):
        return tn(n_side[:, lot(k, LANES)], dall[...])

    per = LANES // depth

    def to_lines(k, joined, x_copy_of, x_out, z_copy_of, total):
        x_copy_of(k).wait_send()
        x_out[lot(k, LANES)] = joined.astype(BF16)
        if isinstance(k, int):
            if k == 0:
                total[...] = joined[0:depth]
            for step in range(max(1, k * per), (k + 1) * per):
                z_copy_of(step).start()

    def a_block(k):
        ax_copy(k).wait_recv()
        joined = out_grads(nhere, chere, k) + ax_in[lot(k, LANES)].astype(F32)
        to_lines(k, joined, ax_copy, ax_out, az_copy, atotal)

    def b_block(k):
        bx_copy(k).wait_recv()
        joined = scan_grads(nhere, k) + bx_in[lot(k, LANES)].astype(F32)
        to_lines(k, joined, bx_copy, bx_out, bz_copy, btotal)

    for k in range(blocks - 1):
        @pl.when(i == mid + 1 + k)
        def _():
            a_block(k)

    @pl.when(i == mid)
    def _():
        for copy in fetch[2:]:
            copy.wait()

    hid_own[lot(c, half)] = hid_ref[lot(core, half)]

    def inverse(k):
        inv = lax.rsqrt(as_column(sums_ref[0, pl.ds(k, 1), :]) * (1.0 / inner_all) + EPS)
        pull = as_column(sums_ref[1, pl.ds(k, 1), :]) * (inv * inv * inv) * (1.0 / inner_all)
        inv_now[...] = inv
        inv_own[lot(k, half)] = inv_now[lot(core, half)]
        return inv, pull

    def gating(k, scales, lanes, gate_in, ssd_in, dn_in):
        inv, pull = scales
        gate = gate_in[:, lanes]
        sig = jax.nn.sigmoid(gate)
        silu = gate * sig
        ssd = ssd_in[:, lanes]
        gated = ssd * silu
        dn = dn_in[:, lanes]
        g_l = gain[0:1, lanes]
        nout = gated * inv
        nout_all[lot(k, SPAN), lanes] = (nout * g_l).astype(BF16)
        ggain[:, lanes] += fold(dn * nout)
        d_gated = dn * g_l * inv - gated * pull
        dgate_all[lot(k, SPAN), lanes] = (d_gated * ssd * (sig * (1.0 + gate * (1.0 - sig)))).astype(BF16)
        return d_gated * silu

    def finish_out(k):
        total = omine[lot(k, half)].astype(F32) + ofar[lot(k, half)].astype(F32)
        inv = inv_own[lot(k, half)]
        value = hid_own[lot(k, half)].astype(F32)
        for group in range(model // LANES):
            lanes = slice(group * LANES, (group + 1) * LANES)
            omine[lot(k, half), lanes] = (value[:, lanes] + total[:, lanes] * inv).astype(BF16)
        o_copy(k).start()
        o_local(k).start()

    def scan_step(first):
        if first:
            scales, low_scales = inverse(c), inverse(c - mid)
        drow = docs_ref[:, lot(c, SPAN)].astype(F32)
        dcol = as_column(drow)
        before = docs_ref[:, lot(jnp.maximum(c - 1, 0), SPAN)].astype(F32)
        enter = as_column(before)[SPAN - 1 : SPAN]
        enter = jnp.where(c == 0, -1.0, enter)
        dbuf[0:SPAN] = dcol
        keeps = [None] + [dbuf[k : k + SPAN] == dcol for k in range(1, 4)]
        if not first:
            ax_out[lot(i - mid, LANES)] = out_grads(naway, caway, i - mid).astype(BF16)
        raw = stp_ref[...] + par[0:1]
        step = softplus(raw)
        row_i, col_i = iota((SPAN, SPAN), 0), iota((SPAN, SPAN), 1)
        tril = (row_i >= col_i).astype(BF16)
        log_step = step * par[1:2]
        running = tri_sum(tril, log_step, heads)
        run_rows = jnp.transpose(running)
        ending = running[SPAN - 1 : SPAN]
        tail = jnp.where(dcol == dcol[SPAN - 1 : SPAN], jnp.exp(ending - running), 0.0)
        reach = jnp.where(dcol == enter, jnp.exp(running), 0.0)
        same = jnp.concatenate([dcol, dcol], 1) == drow
        bias = jnp.where(same & (row_i <= col_i), 0.0, FAR)

        def activate(group):
            lanes = slice(group * LANES, (group + 1) * LANES)
            pre = pre_ref[:, lanes]
            sig = jax.nn.sigmoid(pre)
            return pre * sig, sig * (1.0 + pre * (1.0 - sig))

        b_act, b_slope = activate(pairs)
        c_act, c_slope = activate(pairs + 1)
        b_rows, c_rows = b_act.astype(BF16), c_act.astype(BF16)
        c_turned = jnp.transpose(c_act).astype(BF16)
        scores = exact_nt(b_act, c_act)
        low_half = iota((SPAN, LANES), 1) < LANES // 2
        d_scores = [jnp.zeros((half, SPAN), F32), jnp.zeros((half, half), F32)]
        d_b = jnp.zeros((SPAN, LANES), F32)
        d_c = jnp.zeros((SPAN, LANES), F32)
        head_up = jnp.zeros((SPAN, LANES), F32)
        head_down = jnp.zeros((SPAN, LANES), F32)
        head_step = jnp.zeros((SPAN, LANES), F32)
        head_hold = jnp.zeros((8, LANES), F32)
        for pair in range(pairs):
            lanes = slice(pair * LANES, (pair + 1) * LANES)
            ones_at = (iota((LANES, LANES), 1) == 2 * pair + iota((LANES, LANES), 0) // (LANES // 2)).astype(BF16)

            def head_sum(v):
                hi = v.astype(BF16)
                low = (v - hi.astype(F32)).astype(BF16)
                return nn(hi, ones_at) + nn(low, ones_at)

            act, slope = activate(pair)
            step_l = pair_lanes(step, pair, low_half)
            tail_l = pair_lanes(tail, pair, low_half)
            reach_l = pair_lanes(reach, pair, low_half)
            skip_l = pair_lanes(par[2:3], pair, low_half[0:1])
            ssd = ssd_ref[:, lanes]
            if first:
                d_ssd = gating(c, scales, lanes, gate_ref, ssd_ref, dn_ref)
                dssd_low[lot(c - mid, SPAN), lanes] = gating(
                    c - mid, low_scales, lanes, gate_low_ref, ssd_low_ref, dn_low_ref
                )
            else:
                d_ssd = dssd_low[lot(c, SPAN), lanes]
            gskip[:, lanes] += fold(d_ssd * act)
            dyb = d_ssd.astype(BF16)
            scaled = act * step_l
            xb = scaled.astype(BF16)
            held = state_ref[0, :, lanes]
            d_held = dstate[:, lanes]
            d_held_b = d_held.astype(BF16)
            ry = (d_ssd * reach_l).astype(BF16)
            xt = (scaled * tail_l).astype(BF16)
            parts = []
            for sub in range(2):
                head = 2 * pair + sub
                x_own = jnp.where(low_half if sub == 0 else ~low_half, scaled, 0.0).astype(BF16)
                blocks = []
                for blk in range(2):
                    rows = slice(blk * half, (blk + 1) * half)
                    cols = slice(blk * half, SPAN)
                    gap = run_rows[head : head + 1, cols] - running[rows, head : head + 1]
                    decay = jnp.exp(gap + bias[rows, cols])
                    blocks.append(nn((decay * scores[rows, cols]).astype(BF16), dyb[cols]))
                    d_scores[blk] = d_scores[blk] + decay * nt(x_own[rows], dyb[cols])
                parts.append(jnp.concatenate(blocks, 0))
            d_within = jnp.where(low_half, parts[0], parts[1])
            from_state = tail_l * nn(b_rows, d_held_b)
            d_scaled = d_within + from_state
            xf = xb.astype(F32)
            head_up += head_sum(dyb.astype(F32) * (ssd - skip_l * act) - xf * d_within)
            head_down += head_sum(xf * from_state)
            head_step += head_sum(d_scaled * act)
            hold = reach_l[SPAN - 1 : SPAN]
            hold_sum = jnp.sum((d_held * held.astype(F32)).reshape(LANES // 8, 8, LANES), axis=0) * hold
            head_hold += head_sum(hold_sum)
            d_b += nt(xt, d_held_b)
            d_c += nt(ry, held)
            dstate[:, lanes] = hold * d_held + nn(c_turned, ry)
            pbuf[0:SPAN, lanes] = (skip_l * d_ssd + step_l * d_scaled) * slope

        ds_b = jnp.concatenate(
            [
                d_scores[0],
                jnp.concatenate([jnp.zeros((half, half), F32), d_scores[1]], 1),
            ],
            0,
        )
        d_b += nn(ds_b.astype(BF16), c_rows)
        d_c += nn(jnp.transpose(ds_b).astype(BF16), b_rows)
        pbuf[0:SPAN, inner : inner + LANES] = d_b * b_slope
        pbuf[0:SPAN, inner + LANES : chan] = d_c * c_slope

        triu = (row_i <= col_i).astype(BF16)
        below = (row_i > col_i).astype(BF16)
        d_log = (
            tri_sum(triu, head_up, heads)
            + tri_sum(below, head_down, heads)
            + jnp.sum(head_hold, axis=0, keepdims=True)
        )
        d_step = d_log * par[1:2] + head_step
        d_raw = jnp.where(iota((SPAN, LANES), 1) < heads, d_step * jax.nn.sigmoid(raw), 0.0)
        dall[lot(c, SPAN), chan:] = d_raw.astype(BF16)
        ghead[0] += fold(d_raw)
        ghead[1] += fold(d_log * log_step)

        for group in range(chan // LANES):
            lanes = slice(group * LANES, (group + 1) * LANES)
            mixed = mixed_ref[:, lanes]
            own = pbuf[0:SPAN, lanes]
            acc = cwb[3:4, lanes] * own
            gconv[3, :, lanes] += fold(mixed * own)
            gconv[4, :, lanes] += fold(own)
            for k in range(1, 4):
                later = jnp.where(keeps[k], pbuf[k : k + SPAN, lanes], 0.0)
                acc = acc + cwb[3 - k : 4 - k, lanes] * later
                gconv[3 - k, :, lanes] += fold(mixed * later)
            dall[lot(c, SPAN), lanes] = acc.astype(BF16)
        pbuf[SPAN : SPAN + 8] = pbuf[0:8]
        dbuf[SPAN : SPAN + 8] = dbuf[0:8]

    @pl.when(i < mid)
    def _():
        scan_step(True)

    @pl.when(i >= mid)
    def _():
        for k in (c + mid, c):
            if k is not c:
                oy_copy(k).wait_recv()
                oy_copy(k).wait_send()
            finish_out(k)
        scan_step(False)
        ax_copy(i - mid).start()

    @pl.when(i == 0)
    def _():
        fetch[1].wait()

    def share(which):
        rows = pl.ds(pl.multiple_of(c * SPAN + which * half, half), half)
        made = nt(dgate_all[rows], w[:, 0:inner]) + nt(dall[rows], w[:, inner:])
        value = hid_ref[lot(which, half)].astype(F32)
        inv = lax.rsqrt(jnp.mean(value * value, -1, keepdims=True) + EPS)
        gnorm[...] += jnp.sum((made * (value * inv)).reshape(half // 8, 8, model), axis=0)
        return made

    h_out[lot(c, half)] = share(1 - core).astype(BF16)
    h_copy(c).start()
    kept[...] = share(core)

    @pl.when(i == count - 1)
    def _():
        def send_block(k, carry):
            bx_out[lot(k, LANES)] = scan_grads(naway, k).astype(BF16)
            bx_copy(k).start()
            return carry

        lax.fori_loop(0, blocks, send_block, 0)
        join(0)
        a_block(blocks - 1)

        chan_all = inner_all + 2 * LANES
        tap_rows, own_rows = chan_all // LANES, inner // LANES
        flat[...] = jnp.zeros(flat.shape, F32)
        norm = jnp.sum(gnorm[...], axis=0, keepdims=True)
        at = model // LANES
        for k in range(at):
            flat[k : k + 1] = norm[:, k * LANES : (k + 1) * LANES]
        for tap in range(gconv.shape[0]):
            row = jnp.sum(gconv[tap], axis=0, keepdims=True)
            for k in range(chan // LANES):
                place = at + k + (rank * own_rows if k < own_rows else (tap_rows - chan // LANES))
                flat[pl.ds(place, 1), :] = row[:, k * LANES : (k + 1) * LANES]
            at += tap_rows
        lane = iota((1, LANES), 1)
        spread = jnp.zeros((1, LANES), F32)
        for k in range(2):
            row = jnp.where(lane < heads, jnp.sum(ghead[k], axis=0, keepdims=True), 0.0)
            spread = spread + pltpu.roll(row, 4 * heads * k + rank * heads, 1)
        flat[at : at + 1] = spread
        at += 1
        for acc in (ggain, gskip):
            row = jnp.sum(acc[...], axis=0, keepdims=True)
            for k in range(own_rows):
                flat[pl.ds(at + rank * own_rows + k, 1), :] = row[:, k * LANES : (k + 1) * LANES]
            at += inner_all // LANES

        hops = [across, beyond, partner]
        bit = 1
        while bit < lines:
            hops.append({"dp": (line + bit * (1 - 2 * ((line // bit) % 2))) * 2 + side})
            bit *= 2
        last = flat_in.shape[0] - 1

        def flat_copy(k):
            return remote(
                flat.at[...] if k == 0 else flat_in.at[len(hops) + k], flat_in.at[k], f_sem, k, hops[k]
            )

        def flat_step(k):
            flat_copy(k).wait_recv()
            held = (flat[...] if k == 0 else flat_in[len(hops) + k]) + flat_in[k]
            if k + 1 < len(hops):
                flat_in[len(hops) + k + 1] = held
                flat_copy(k + 1).start()
            else:
                flat_in[last] = held

        flat_copy(0).start()

        for step in range(1, lines):
            az_copy(step).wait_recv()
            atotal[...] += az_in[step - 1].astype(F32)
        gates[0] = atotal[:, inner:]
        gout_put = pltpu.make_async_copy(atotal.at[:, pl.ds(0, inner)], gout_ref, put_sem.at[9])
        gout_put.start()
        gate_near = remote(gates.at[0], gates.at[1], g_sem, 0, across)
        gate_far = remote(gates.at[0], gates.at[2], g_sem, 1, beyond)
        gate_pass = remote(gates.at[2], gates.at[3], g_sem, 2, across)
        gate_near.start()
        gate_far.start()
        flat_step(0)

        gain_row = ngain_ref[...]

        def finish_hidden(k, carry):
            y_copy(k).wait_recv()
            y_copy(k).wait_send()
            d_hidden = mine[lot(k, half)].astype(F32) + y_in[lot(k, half)].astype(F32)
            value = hid_own[lot(k, half)].astype(F32)
            inv = lax.rsqrt(jnp.mean(value * value, -1, keepdims=True) + EPS)
            scaled = d_hidden * gain_row
            pull = jnp.mean(scaled * value, -1, keepdims=True)
            mine[lot(k, half)] = (inv * scaled - value * (inv * inv * inv) * pull).astype(BF16)
            d_copy(k).start()
            d_local(k).start()
            return carry

        def down(k, carry):
            return finish_hidden(count - 1 - k, carry)

        b_block(0)
        lax.fori_loop(0, 3, down, 0)
        flat_step(1)
        b_block(1)
        lax.fori_loop(3, 5, down, 0)
        flat_step(2)
        b_block(2)
        gate_far.wait_recv()
        gate_pass.start()
        b_block(3)
        for k in range(3, len(hops)):
            flat_step(k)
        flat_put = pltpu.make_async_copy(flat_in.at[last], flatout_ref, put_sem.at[10])
        flat_put.start()
        lax.fori_loop(5, count - 1, down, 0)

        for step in range(1, lines):
            bz_copy(step).wait_recv()
            btotal[...] += bz_in[step - 1].astype(F32)
        values[0] = btotal[:, 0:inner]
        value_near = remote(values.at[0], values.at[1], v_sem, 0, across)
        value_far = remote(values.at[0], values.at[2], v_sem, 1, beyond)
        value_pass = remote(values.at[2], values.at[3], v_sem, 2, across)
        shared_near = remote(shared.at[0], shared.at[1], s_sem, 0, across)
        shared_far = remote(shared.at[2], shared.at[3], s_sem, 1, beyond)
        shared[0, :, 0 : 2 * LANES] = btotal[:, inner : inner + 2 * LANES]
        steps = pltpu.roll(btotal[:, inner + 2 * LANES :], rank * heads, 1)
        place = iota(steps.shape, 1) - rank * heads
        shared[0, :, 2 * LANES :] = jnp.where((place >= 0) & (place < heads), steps, 0.0)
        shared_near.start()
        value_far.start()
        value_near.start()
        finish_hidden(0, 0)
        shared_near.wait_recv()
        shared[2] = shared[0] + shared[1]
        shared_far.start()

        def put(source, k, first, owner, index):
            column = pl.multiple_of(first + owner * inner, LANES)
            return pltpu.make_async_copy(source.at[k], gin_ref.at[:, pl.ds(column, inner)], put_sem.at[index])

        owners = (rank, rank + 1 - 2 * core, (rank + 2) % 4, (rank + 3 - 2 * core) % 4)
        puts = [put(gates, 0, 0, owners[0], 0), put(values, 0, inner_all, owners[0], 4)]
        gate_near.wait_recv()
        gate_pass.wait_recv()
        puts += [put(gates, k, 0, owners[k], k) for k in range(1, 4)]
        value_near.wait_recv()
        puts.append(put(values, 1, inner_all, owners[1], 5))
        for copy in puts:
            copy.start()
        value_far.wait_recv()
        value_pass.start()
        puts.append(put(values, 2, inner_all, owners[2], 6))
        puts[-1].start()
        shared_far.wait_recv()
        shared[1] = shared[2] + shared[3]
        puts.append(
            pltpu.make_async_copy(
                shared.at[1], gin_ref.at[:, pl.ds(2 * inner_all, 3 * LANES)], put_sem.at[8]
            )
        )
        puts[-1].start()
        value_pass.wait_recv()
        puts.append(put(values, 3, inner_all, owners[3], 7))
        puts[-1].start()

        def drain(k, carry):
            h_copy(k).wait_send()
            d_copy(k).wait()
            d_local(k).wait()
            o_copy(k).wait()
            o_local(k).wait()
            return carry

        lax.fori_loop(0, count, drain, 0)
        for step in range(1, lines):
            az_copy(step).wait_send()
            bz_copy(step).wait_send()
        for copy in (
            gate_near, gate_far, gate_pass, value_near, value_far, value_pass, shared_near, shared_far,
        ):
            copy.wait_send()
        for k in range(len(hops)):
            flat_copy(k).wait_send()
        for copy in puts + [gout_put, flat_put]:
            copy.wait()


def mixer_backward(
    docs, hidden, held, sums, params, ggain, ngain, sorted_parts, w_in, mine, far,
    heads, lines, depth, early,
):
    gate, mixed, pre, ssd, stp, states, dn = held
    tokens, inner = ssd.shape
    model = hidden.shape[1]
    chan = inner + 2 * LANES
    width = inner + chan + LANES
    wide = width - inner
    inner_all = ggain.shape[1]
    count = tokens // SPAN
    mid = count // 2
    half = SPAN // 2
    blocks, fars = lines * depth // LANES, max(1, lines - 1)
    hops = 3 + (lines - 1).bit_length()
    rows = (model + 5 * (inner_all + 2 * LANES) + LANES + 2 * inner_all) // LANES
    rows += -rows % 8

    def tok(size):
        return pl.BlockSpec((SPAN, size), lambda i: (count - 1 - i, 0))

    def early_tok(size, base):
        return pl.BlockSpec((SPAN, size), lambda i: (base + (mid - 1 - i) * (1 - i // mid), 0))

    def full(shape):
        return pl.BlockSpec(shape, lambda i: (0,) * len(shape))

    anywhere = pl.BlockSpec(memory_space=pl.ANY)
    dma, vmem = pltpu.SemaphoreType.DMA, pltpu.VMEM
    consts = params + (ggain, ngain)
    big = tuple(sorted_parts)[0:2] + tuple(sorted_parts)[2:4] + (w_in, mine, far)
    side_shape = (tokens, lines * depth)
    return pl.pallas_call(
        lambda *refs: backward_kernel((inner, heads, inner_all, lines, depth, early), *refs),
        out_shape=(
            jax.ShapeDtypeStruct((tokens, model), BF16),
            jax.ShapeDtypeStruct((tokens, model), BF16),
            jax.ShapeDtypeStruct((depth, 2 * inner_all + 3 * LANES), F32),
            jax.ShapeDtypeStruct((depth, inner), F32),
            jax.ShapeDtypeStruct((rows, LANES), F32),
        ),
        grid=(count,),
        in_specs=[
            full(docs.shape), tok(model), early_tok(inner, mid), early_tok(inner, mid),
            early_tok(inner, 0), early_tok(inner, 0), early_tok(inner, 0),
            tok(inner), tok(chan), tok(chan), tok(LANES),
            pl.BlockSpec((1, LANES, inner), lambda i: (count - 1 - i, 0, 0)),
            full(sums.shape),
        ]
        + [full(v.shape) for v in consts]
        + [anywhere] * len(big),
        out_specs=(anywhere,) * 5,
        scratch_shapes=[
            vmem(side_shape, BF16), vmem(side_shape, BF16), vmem(side_shape, BF16), vmem(side_shape, BF16),
            vmem(w_in.shape, BF16), dma((len(big),)),
            vmem((SPAN + 8, chan), F32), vmem((SPAN + 8, LANES), F32), vmem((LANES, inner), F32),
            vmem((8, LANES), F32), vmem((8, chan), F32), vmem((8, inner), F32),
            vmem((5, 8, chan), F32), vmem((8, inner), F32), vmem((2, 8, LANES), F32),
            vmem((8, inner), F32), vmem((8, model), F32),
            vmem((tokens, inner), BF16), vmem((tokens, inner), BF16), vmem((tokens, wide), BF16),
            vmem((tokens // 2, inner), F32), vmem((SPAN, LANES), F32), vmem((tokens // 2, LANES), F32),
            vmem((tokens // 2, model), BF16),
            vmem((tokens // 2, model), BF16), vmem((tokens // 2, model), BF16),
            vmem((tokens // 2, model), BF16), vmem((half, model), F32),
            dma((2, count)), dma((2, count)), dma((2, count)), dma((count,)),
            vmem((tokens // 2, model), BF16), vmem((tokens // 2, model), BF16),
            dma((2, count - early)), dma((2, count)), dma((count,)),
            vmem((blocks * LANES, 2 * inner), BF16), vmem((blocks * LANES, 2 * inner), BF16),
            dma((2, blocks)), vmem((fars, depth, 2 * inner), BF16), dma((2, fars)),
            vmem((depth, 2 * inner), F32),
            vmem((blocks * LANES, wide), BF16), vmem((blocks * LANES, wide), BF16),
            dma((2, blocks)), vmem((fars, depth, wide), BF16), dma((2, fars)), vmem((depth, wide), F32),
            vmem((4, depth, inner), F32), dma((2, 3)), vmem((4, depth, inner), F32), dma((2, 3)),
            vmem((4, depth, 3 * LANES), F32), dma((2, 2)), dma((11,)),
            vmem((rows, LANES), F32), vmem((2 * hops + 1, rows, LANES), F32), dma((2, hops)),
        ],
        compiler_params=pltpu.CompilerParams(
            dimension_semantics=("arbitrary",), vmem_limit_bytes=67043328,
            collective_id=1, has_side_effects=True,
        ),
        cost_estimate=cost(90.0),
        name="mixer_backward",
    )(
        docs, hidden, gate, dn, gate, ssd, dn, ssd, mixed, pre, stp, states, sums, *consts, *big
    )


def gather_kernel(
    dims, hid_ref, cot_ref, ngain_ref, w_ref, step_ref, wo_ref,
    win_ref, wout_ref, normed_ref, *refs,
):
    lines, depth, inner, inner_all, aligned = dims
    outs = refs[:4] if aligned else ()
    mine, zsend, zrecv, xsend, xrecv, takes, puts = refs[len(outs):]
    trank, drank = lax.axis_index("tensor"), lax.axis_index("dp")
    line, side = drank // 2, drank % 2
    model = hid_ref.shape[1]
    off = pl.multiple_of(trank * inner, LANES)
    pieces = (
        (w_ref, inner_all + off, win_ref, inner, inner),
        (w_ref, 2 * inner_all, win_ref, 2 * inner, 2 * LANES),
        (step_ref, 0, win_ref, 2 * inner + 2 * LANES, LANES),
        (w_ref, off, win_ref, 0, inner),
        (wo_ref, 0, wout_ref, 0, inner),
    )

    def peer(step):
        return {"dp": lax.rem(line + step, lines) * 2 + side}

    partner = {"dp": line * 2 + 1 - side}
    barrier = pltpu.get_barrier_semaphore()
    for step in range(1, lines):
        pl.semaphore_signal(barrier, inc=1, device_id=peer(step), device_id_type=MESH_IDS)
    pl.semaphore_signal(barrier, inc=1, device_id=partner, device_id_type=MESH_IDS)
    pl.semaphore_wait(barrier, lines)

    def rows(index):
        return pl.ds(pl.multiple_of(index * depth, depth), depth)

    def block(p, index):
        _, _, dst, at, width = pieces[p]
        return dst.at[rows(index), pl.ds(at, width)]

    def own(p):
        src, at, _, _, width = pieces[p]
        return src.at[:, pl.ds(at, width)]

    def z_copy(p, step, src, index):
        return pltpu.make_async_remote_copy(
            src_ref=src, dst_ref=block(p, index), send_sem=zsend.at[p, step - 1],
            recv_sem=zrecv.at[p, step - 1], device_id=peer(step), device_id_type=MESH_IDS,
        )

    def x_copy(p, step, src, index):
        return pltpu.make_async_remote_copy(
            src_ref=src, dst_ref=block(p, index), send_sem=xsend.at[p, step],
            recv_sem=xrecv.at[p, step], device_id=partner, device_id_type=MESH_IDS,
        )

    count = len(pieces)
    for p in range(count):
        for step in range(1, lines):
            z_copy(p, step, own(p), drank).start()
        x_copy(p, 0, own(p), drank).start()
    spots, at = [], 0
    for p in range(count):
        spots.append(mine.at[:, pl.ds(at, pieces[p][4])])
        at += pieces[p][4]
    fetched = [pltpu.make_async_copy(own(p), spots[p], takes.at[p]) for p in range(count)]
    for copy in fetched:
        copy.start()

    gain = ngain_ref[...]

    def normalize(hid, cot, normed, *sorted_refs):
        value = hid[...].astype(F32)
        inv = lax.rsqrt(jnp.mean(value * value, -1, keepdims=True) + EPS)
        normed[...] = (value * inv * gain).astype(BF16)
        if aligned:
            for src, away, here in (
                (normed, sorted_refs[0], sorted_refs[1]), (cot, sorted_refs[2], sorted_refs[3]),
            ):
                for j in range(lines):
                    first = lax.rem(line + j, lines) * 2
                    lanes = slice(j * depth, (j + 1) * depth)
                    away[:, lanes] = src[:, pl.ds(pl.multiple_of((first + 1 - side) * depth, depth), depth)]
                    here[:, lanes] = src[:, pl.ds(pl.multiple_of((first + side) * depth, depth), depth)]

    full = pl.BlockSpec((SPAN, model), lambda i: (i, 0))
    half = pl.BlockSpec((SPAN, lines * depth), lambda i: (i, 0))
    pltpu.emit_pipeline(
        normalize, grid=(hid_ref.shape[0] // SPAN,), in_specs=[full, full],
        out_specs=[full] + [half] * len(outs),
    )(hid_ref, cot_ref, normed_ref, *outs)

    stored = [pltpu.make_async_copy(spots[p], block(p, drank), puts.at[p]) for p in range(count)]
    for p in range(count):
        fetched[p].wait()
        stored[p].start()
    for p in range(count):
        for step in range(1, lines):
            source = lax.rem(line - step + lines, lines) * 2 + side
            got = block(p, source)
            z_copy(p, step, got, source).wait_recv()
            x_copy(p, step, got, source).start()
    for p in range(count):
        for step in range(lines):
            source = lax.rem(line - step + lines, lines) * 2 + 1 - side
            x_copy(p, step, block(p, source), source).wait_recv()
    for p in range(count):
        for step in range(1, lines):
            z_copy(p, step, own(p), drank).wait_send()
        for step in range(lines):
            x_copy(p, step, own(p), drank).wait_send()
        stored[p].wait()


def gather_weights(hidden, cotangent, norm_gain, in_weight, own_step, out_weight, lines, inner_all):
    tokens, model = hidden.shape
    depth, inner = out_weight.shape
    aligned = depth % LANES == 0
    width = 2 * inner + 3 * LANES
    half = jax.ShapeDtypeStruct((tokens, lines * depth), BF16)
    anywhere = pl.BlockSpec(memory_space=pl.ANY)
    outs = (
        jax.ShapeDtypeStruct((model, width), BF16),
        jax.ShapeDtypeStruct((model, inner), BF16),
        jax.ShapeDtypeStruct((tokens, model), BF16),
    ) + (half,) * (4 if aligned else 0)
    dma = pltpu.SemaphoreType.DMA
    return pl.pallas_call(
        lambda *refs: gather_kernel((lines, depth, inner, inner_all, aligned), *refs),
        out_shape=outs,
        in_specs=[anywhere, anywhere, pl.BlockSpec(memory_space=pltpu.VMEM)] + [anywhere] * 3,
        out_specs=(anywhere,) * len(outs),
        scratch_shapes=[
            pltpu.VMEM((depth, width + inner), BF16),
            dma((5, max(1, lines - 1))), dma((5, max(1, lines - 1))), dma((5, lines)), dma((5, lines)),
            dma((5,)), dma((5,)),
        ],
        compiler_params=pltpu.CompilerParams(collective_id=0, has_side_effects=True),
        cost_estimate=cost(45.0),
        name="gather_weights",
    )(hidden, cotangent, norm_gain, in_weight, own_step, out_weight)


def body(
    hidden_in, doc_ids, cotangent, norm_gain, in_weight, conv_weight, conv_bias,
    dt_bias, log_decay, skip_gain, gate_gain, out_weight,
):
    tcount, dcount = lax.axis_size("tensor"), lax.axis_size("dp")
    trank, drank = lax.axis_index("tensor"), lax.axis_index("dp")
    lines = dcount // 2
    line, side = drank // 2, drank % 2
    inner_all, head_all = gate_gain.shape[0], dt_bias.shape[0]
    inner, heads = inner_all // tcount, head_all // tcount
    tokens, model = hidden_in.shape
    base_bc = 2 * inner_all
    base_dt = base_bc + 2 * LANES
    depth = in_weight.shape[0]

    def line_to(step):
        return lambda k: ((k // 2 + step) % lines) * 2 + k % 2

    own_step = jnp.pad(
        lax.dynamic_slice_in_dim(in_weight, base_dt + trank * heads, heads, 1),
        ((0, 0), (0, LANES - heads)),
    )
    w_in, w_out, normed, *sorted_parts = gather_weights(
        hidden_in, cotangent, norm_gain.reshape(1, -1), in_weight, own_step, out_weight,
        lines, inner_all,
    )
    if not sorted_parts:

        def features(v, which):
            return jnp.concatenate(
                [
                    lax.dynamic_slice_in_dim(v, (((line + j) % lines) * 2 + which) * depth, depth, 1)
                    for j in range(lines)
                ],
                1,
            )

        sorted_parts = [features(v, which) for v in (normed, cotangent) for which in (1 - side, side)]
    n_away, n_here, c_away, c_here = sorted_parts

    def row(v):
        return v.reshape(1, -1)

    params = (conv_weight, row(conv_bias), row(dt_bias), row(log_decay), row(skip_gain))

    early = 4
    *held, sums, mine, far = mixer_forward(
        doc_ids, normed, cotangent, w_in, w_out, params, row(gate_gain), heads, early
    )
    delta, layer_out, grad_in, g_out, flat = mixer_backward(
        doc_ids, hidden_in, held, sums, params, row(gate_gain), row(norm_gain), sorted_parts, w_in,
        mine, far, heads, lines, depth, early,
    )
    grad_input = cotangent.astype(F32) + delta.astype(F32)
    chan_all = inner_all + 2 * LANES
    flat = flat.reshape(-1)
    cuts, at = [], 0
    for size in (model, 5 * chan_all, LANES, inner_all, inner_all):
        cuts.append(flat[at : at + size])
        at += size
    conv_all = cuts[1].reshape(5, chan_all)
    return (
        layer_out, grad_input, cuts[0], grad_in[:, : in_weight.shape[1]], conv_all[:4], conv_all[4],
        cuts[2][:head_all], cuts[2][head_all : 2 * head_all],
        jnp.sum(cuts[4].reshape(head_all, -1), 1), cuts[3], g_out,
    )


def solution(mesh):
    rows, whole = P("dp", None), P()
    return jax.shard_map(
        body,
        mesh=mesh,
        in_specs=(rows, rows, rows, whole, rows, whole, whole, whole, whole, whole, whole, P("dp", "tensor")),
        out_specs=(rows, rows, whole, rows, whole, whole, whole, whole, whole, whole, P("dp", "tensor")),
        check_vma=False,
    )
```

profile of v0, /device:TPU:0, one launch (start us, length us, event | category | flops | bytes accessed | tf_op | source)
XLA Modules:
  0.0 277.3 jit_solution(17023416829677864178)
XLA Ops:
  0.6 1.3 reshape.60.refs_6_.refs_14_
  2.0 1.7 copy.24.refs_3_
  3.7 0.0 copy-start.1
  3.7 0.1 constant_dynamic-slice_fusion
  3.8 0.8 pad.4.refs_4_
  4.5 0.2 copy-done.1
  4.7 59.0 %gather_weights.1 = (bf16[1024,1408]{1,0:T(8,128)(2,1)}, bf16[1024,512]{1,0:T(8,128)(2,1)}, bf16[2048,1024]{1,0:T(8,128)(2,1)}, bf16[2048,512]{1,0:T(8,128)(2,1)...) custom-call(bf16[2048,1024]{1,0:T(8,128)(2,1)} %refs_1_.3, ...), custom_call_target="tpu_custom_call" | custom-call | flops 51749998592 | bytes 1048576 | tf_op jit(solution)/shard_map/gather_weights/pallas_call | solution.py:1114
  63.6 49.0 %mixer_forward.1 = (f32[2048,512]{1,0:T(8,128)}, f32[2048,768]{1,0:T(8,128)}, f32[2048,768]{1,0:T(8,128)}, f32[2048,512]{1,0:T(8,128)}, f32[2048,128]{1,0:T(8,12...) custom-call(s32[1,2048]{1,0:T(1,128)} %refs_0_.5, ...), custom_call_target="tpu_custom_call" | custom-call | flops 46000001024 | bytes 1048576 | tf_op jit(solution)/shard_map/mixer_forward/pallas_call | solution.py:328
  112.7 142.5 %mixer_backward.1 = (bf16[2048,1024]{1,0:T(8,128)(2,1)}, bf16[2048,1024]{1,0:T(8,128)(2,1)}, f32[128,4480]{1,0:T(8,128)}, f32[128,512]{1,0:T(8,128)}, f32[136,128]{1,0:T(8,128)}) custom-call(s32[1,2048]{1,0:T(1,128)} %refs_0_.5, bf16[2048,1024]{1,0:T(8,128)(2,1)} %refs_1_.3, f32[2048,512]{1,0:T(8,128)} %get-tuple-element.36.refs_2_.refs_4_, ...), custom_call_target="tpu_custom_call" | custom-call | flops 103499997184 | bytes 1048576 | tf_op jit(solution)/shard_map/mixer_backward/pallas_call | solution.py:936
  255.2 1.3 slice_bitcast_fusion.3
  256.6 1.3 slice_bitcast_fusion.2
  257.8 1.3 slice_bitcast_fusion
  259.1 1.4 slice_bitcast_fusion.1
  260.5 0.8 slice.52
  261.3 0.6 slice.53
  261.9 0.1 reshape.65
  262.0 0.6 reduce_sum.9
  262.6 3.0 %copy.25 = f32[128,4384]{0,1:T(8,128)} copy(f32[128,4384]{1,0:T(8,128)} %bitcast.16) | data formatting | bytes 4489216
  265.6 0.0 copy-start
  265.6 9.0 %convert_add_fusion = f32[2048,1024]{1,0:T(8,128)} fusion(bf16[2048,1024]{1,0:T(8,128)(2,1)} %get-tuple-element.51, bf16[2048,1024]{1,0:T(8,128)(2,1)} %refs_2_.1), kind=kLoop, calls=%fused_computation | loop fusion | flops 6291456 | bytes 16777216 | tf_op jit(solution)/shard_map/add | solution.py:1183
  274.6 0.0 copy-done
  274.6 0.0 copy-start.2
  274.6 2.0 copy.28
  276.6 0.0 copy-done.2
  276.6 0.7 copy.29
Async XLA Ops:
  3.7 1.0 copy-start.1
  265.6 9.0 %copy-start = (bf16[2048,1024]{1,0:T(8,128)(2,1)S(1)}, bf16[2048,1024]{1,0:T(8,128)(2,1)}, u32[]{:S(2)}) copy-start(bf16[2048,1024]{1,0:T(8,128)(2,1)} %get-tuple-element.81) | copy-start | bytes 12582916
  274.6 2.0 copy-start.2
where the time goes:
time: 278 us; the launch traced here: 277 us
  Pallas kernels  251 us (90%)
  local copies, waits for them, and re-layouts  16.5 us (6%)
  other arithmetic  9.63 us (3%)
    pallas_call x1, Pallas kernels, mixer_backward(): pl.pallas_call(lambda *refs: backward_kernel((inner, heads, inner_all, li...  143 us
    pallas_call x1, Pallas kernels, gather_weights(): pl.pallas_call(lambda *refs: gather_kernel((lines, depth, inner, inner_al...  59 us
    pallas_call x1, Pallas kernels, mixer_forward(): pl.pallas_call(lambda *refs: forward_kernel((inner, heads, early), *refs)...  49 us
    add x1, other arithmetic, body(): grad_input = cotangent.astype(F32) + delta.astype(F32)  9 us
    unnamed x10, local copies, waits for them, and re-layouts  7.58 us

commit v1 on v0

--- a/solution.py
+++ b/solution.py
@@ -163,15 +163,7 @@
 
     def join(k):
         h_copy(k).wait_recv()
-        mine[slot(k)] = (kept[...] + h_in[slot(k)].astype(F32)).astype(BF16)
-
-    @pl.when(i > 0)
-    def _():
-        join(i - 1)
-
-        @pl.when(i - 1 < early)
-        def _():
-            y_copy(i - 1).start()
+        mine[slot(k)] = (kept[slot(core)] + h_in[slot(k)].astype(F32)).astype(BF16)
 
     nb = normed_ref[...]
     xbuf[8 : 8 + SPAN] = nn(nb, win_ref[:, inner : inner + chan])
@@ -252,9 +244,17 @@
     own_sums[1, pl.ds(i, 1), :] = as_row(cross)
     xbuf[0:8] = xbuf[SPAN : SPAN + 8]
     dbuf[0:8] = dbuf[SPAN : SPAN + 8]
-    h_out[slot(i)] = nt(gg_ref[slot(1 - core)], wout_ref[...]).astype(BF16)
+    @pl.when(i > 0)
+    def _():
+        join(i - 1)
+
+        @pl.when(i - 1 < early)
+        def _():
+            y_copy(i - 1).start()
+
+    kept[...] = nt(gg_ref[...], wout_ref[...])
+    h_out[slot(i)] = kept[slot(1 - core)].astype(BF16)
     h_copy(i).start()
-    kept[...] = nt(gg_ref[slot(core)], wout_ref[...])
 
     @pl.when(i == spans - 1)
     def _():
@@ -336,7 +336,7 @@
             vmem((8, LANES), F32), vmem((8, chan), F32), vmem((8, inner), F32),
             vmem((SPAN, inner), BF16), vmem(sums, F32),
             vmem((tokens // 2, model), BF16), vmem((tokens // 2, model), BF16),
-            vmem((SPAN // 2, model), F32), vmem((tokens // 2, model), BF16),
+            vmem((SPAN, model), F32), vmem((tokens // 2, model), BF16),
             vmem((early * SPAN // 2, model), BF16),
             dma((2, spans)), dma((2, early)), vmem((3,) + sums, F32), dma((2, 3)), dma((2,)),
         ],
@@ -363,7 +363,8 @@
     h_out, mine, y_in, kept, h_sem, y_sem, d_sem, d_put,
     omine, ofar, oy_sem, o_sem, o_put,
     ax_out, ax_in, ax_sem, az_in, az_sem, atotal,
-    bx_out, bx_in, bx_sem, bz_in, bz_sem, btotal,
+    sx_out, sx_in, sx_sem, sz_in, sz_sem, stotal, shere,
+    vx_out, vx_in, vx_sem, vz_in, vz_sem, vtotal, vhere, vbuf,
     gates, g_sem, values, v_sem, shared, s_sem, put_sem, flat, flat_in, f_sem,
 ):
     inner, heads, inner_all, lines, depth, early = dims
@@ -436,14 +437,20 @@
     def ax_copy(k):
         return remote(ax_out.at[lot(k, LANES)], ax_in.at[lot(k, LANES)], ax_sem, k, partner)
 
-    def bx_copy(k):
-        return remote(bx_out.at[lot(k, LANES)], bx_in.at[lot(k, LANES)], bx_sem, k, partner)
+    def sx_copy(k):
+        return remote(sx_out.at[lot(k, LANES)], sx_in.at[lot(k, LANES)], sx_sem, k, partner)
+
+    def vx_copy(k):
+        return remote(vx_out.at[lot(k, LANES)], vx_in.at[lot(k, LANES)], vx_sem, k, partner)
 
     def az_copy(step):
         return remote(ax_out.at[pl.ds(step * depth, depth)], az_in.at[step - 1], az_sem, step - 1, peer(step))
 
-    def bz_copy(step):
-        return remote(bx_out.at[pl.ds(step * depth, depth)], bz_in.at[step - 1], bz_sem, step - 1, peer(step))
+    def sz_copy(step):
+        return remote(sx_out.at[pl.ds(step * depth, depth)], sz_in.at[step - 1], sz_sem, step - 1, peer(step))
+
+    def vz_copy(step):
+        return remote(vx_out.at[pl.ds(step * depth, depth)], vz_in.at[step - 1], vz_sem, step - 1, peer(step))
 
     @pl.when(i == 0)
     def _():
@@ -466,21 +473,14 @@
 
     def join(k):
         h_copy(k).wait_recv()
-        mine[lot(k, half)] = (kept[...] + mine[lot(k, half)].astype(F32)).astype(BF16)
+        mine[lot(k, half)] = (kept[lot(core, half)] + mine[lot(k, half)].astype(F32)).astype(BF16)
         y_copy(k).start()
-
-    @pl.when(i > 0)
-    def _():
-        join(c + 1)
 
     def out_grads(n_side, c_side, k):
         cols = lot(k, LANES)
         return jnp.concatenate(
             [tn(c_side[:, cols], nout_all[...]), tn(n_side[:, cols], dgate_all[...])], 1
         )
-
-    def scan_grads(n_side, k):
-        return tn(n_side[:, lot(k, LANES)], dall[...])
 
     per = LANES // depth
 
@@ -498,15 +498,15 @@
         joined = out_grads(nhere, chere, k) + ax_in[lot(k, LANES)].astype(F32)
         to_lines(k, joined, ax_copy, ax_out, az_copy, atotal)
 
-    def b_block(k):
-        bx_copy(k).wait_recv()
-        joined = scan_grads(nhere, k) + bx_in[lot(k, LANES)].astype(F32)
-        to_lines(k, joined, bx_copy, bx_out, bz_copy, btotal)
-
-    for k in range(blocks - 1):
-        @pl.when(i == mid + 1 + k)
-        def _():
-            a_block(k)
+    def s_block(k):
+        sx_copy(k).wait_recv()
+        joined = shere[lot(k, LANES)] + sx_in[lot(k, LANES)].astype(F32)
+        to_lines(k, joined, sx_copy, sx_out, sz_copy, stotal)
+
+    def v_block(k):
+        vx_copy(k).wait_recv()
+        joined = vhere[lot(k, LANES)] + vx_in[lot(k, LANES)].astype(F32)
+        to_lines(k, joined, vx_copy, vx_out, vz_copy, vtotal)
 
     @pl.when(i == mid)
     def _():
@@ -559,7 +559,8 @@
         dbuf[0:SPAN] = dcol
         keeps = [None] + [dbuf[k : k + SPAN] == dcol for k in range(1, 4)]
         if not first:
-            ax_out[lot(i - mid, LANES)] = out_grads(naway, caway, i - mid).astype(BF16)
+            block = lax.rem(i - mid + 1, blocks)
+            ax_out[lot(block, LANES)] = out_grads(naway, caway, block).astype(BF16)
         raw = stp_ref[...] + par[0:1]
         step = softplus(raw)
         row_i, col_i = iota((SPAN, SPAN), 0), iota((SPAN, SPAN), 1)
@@ -627,15 +628,15 @@
             for sub in range(2):
                 head = 2 * pair + sub
                 x_own = jnp.where(low_half if sub == 0 else ~low_half, scaled, 0.0).astype(BF16)
-                blocks = []
+                tiles = []
                 for blk in range(2):
                     rows = slice(blk * half, (blk + 1) * half)
                     cols = slice(blk * half, SPAN)
                     gap = run_rows[head : head + 1, cols] - running[rows, head : head + 1]
                     decay = jnp.exp(gap + bias[rows, cols])
-                    blocks.append(nn((decay * scores[rows, cols]).astype(BF16), dyb[cols]))
+                    tiles.append(nn((decay * scores[rows, cols]).astype(BF16), dyb[cols]))
                     d_scores[blk] = d_scores[blk] + decay * nt(x_own[rows], dyb[cols])
-                parts.append(jnp.concatenate(blocks, 0))
+                parts.append(jnp.concatenate(tiles, 0))
             d_within = jnp.where(low_half, parts[0], parts[1])
             from_state = tail_l * nn(b_rows, d_held_b)
             d_scaled = d_within + from_state
@@ -703,34 +704,41 @@
                 oy_copy(k).wait_send()
             finish_out(k)
         scan_step(False)
-        ax_copy(i - mid).start()
+        ax_copy(lax.rem(i - mid + 1, blocks)).start()
+
+    @pl.when(i > 0)
+    def _():
+        join(c + 1)
+
+    order = tuple(range(1, blocks)) + (0,)
+    for k in range(blocks - 1):
+        @pl.when(i == mid + 1 + k)
+        def _():
+            a_block(order[k])
 
     @pl.when(i == 0)
     def _():
         fetch[1].wait()
 
-    def share(which):
-        rows = pl.ds(pl.multiple_of(c * SPAN + which * half, half), half)
-        made = nt(dgate_all[rows], w[:, 0:inner]) + nt(dall[rows], w[:, inner:])
-        value = hid_ref[lot(which, half)].astype(F32)
-        inv = lax.rsqrt(jnp.mean(value * value, -1, keepdims=True) + EPS)
-        gnorm[...] += jnp.sum((made * (value * inv)).reshape(half // 8, 8, model), axis=0)
-        return made
-
-    h_out[lot(c, half)] = share(1 - core).astype(BF16)
+    rows_now = lot(c, SPAN)
+    kept[...] = nt(dgate_all[rows_now], w[:, 0:inner]) + nt(dall[rows_now], w[:, inner:])
+    h_out[lot(c, half)] = kept[lot(1 - core, half)].astype(BF16)
     h_copy(c).start()
-    kept[...] = share(core)
+    value = hid_ref[...].astype(F32)
+    unit = value * lax.rsqrt(jnp.mean(value * value, -1, keepdims=True) + EPS)
+    gnorm[...] += fold(kept[...] * unit)
 
     @pl.when(i == count - 1)
     def _():
-        def send_block(k, carry):
-            bx_out[lot(k, LANES)] = scan_grads(naway, k).astype(BF16)
-            bx_copy(k).start()
-            return carry
-
-        lax.fori_loop(0, blocks, send_block, 0)
+        sx_out[...] = tn(naway[...], dall[:, inner:]).astype(BF16)
+        for k in order:
+            sx_copy(k).start()
+        vx_out[LANES:] = tn(naway[:, LANES:], dall[:, 0:inner]).astype(BF16)
+        for k in order[:-1]:
+            vx_copy(k).start()
+        vx_out[0:LANES] = tn(naway[:, 0:LANES], dall[:, 0:inner]).astype(BF16)
+        vx_copy(0).start()
         join(0)
-        a_block(blocks - 1)
 
         chan_all = inner_all + 2 * LANES
         tap_rows, own_rows = chan_all // LANES, inner // LANES
@@ -781,19 +789,7 @@
 
         flat_copy(0).start()
 
-        for step in range(1, lines):
-            az_copy(step).wait_recv()
-            atotal[...] += az_in[step - 1].astype(F32)
-        gates[0] = atotal[:, inner:]
-        gout_put = pltpu.make_async_copy(atotal.at[:, pl.ds(0, inner)], gout_ref, put_sem.at[9])
-        gout_put.start()
-        gate_near = remote(gates.at[0], gates.at[1], g_sem, 0, across)
-        gate_far = remote(gates.at[0], gates.at[2], g_sem, 1, beyond)
-        gate_pass = remote(gates.at[2], gates.at[3], g_sem, 2, across)
-        gate_near.start()
-        gate_far.start()
-        flat_step(0)
-
+        a_block(order[-1])
         gain_row = ngain_ref[...]
 
         def finish_hidden(k, carry):
@@ -812,60 +808,68 @@
         def down(k, carry):
             return finish_hidden(count - 1 - k, carry)
 
-        b_block(0)
+        shere[...] = tn(nhere[...], dall[:, inner:])
+        for k in order:
+            s_block(k)
+        vhere[...] = tn(nhere[...], dall[:, 0:inner])
+        flat_step(0)
         lax.fori_loop(0, 3, down, 0)
+        for k in order[:-1]:
+            v_block(k)
         flat_step(1)
-        b_block(1)
-        lax.fori_loop(3, 5, down, 0)
+        for step in range(1, lines):
+            az_copy(step).wait_recv()
+            atotal[...] += az_in[step - 1].astype(F32)
+        gates[0] = atotal[:, inner:]
+        gout_put = pltpu.make_async_copy(atotal.at[:, pl.ds(0, inner)], gout_ref, put_sem.at[9])
+        gout_put.start()
+        gate_near = remote(gates.at[0], gates.at[1], g_sem, 0, across)
+        gate_far = remote(gates.at[0], gates.at[2], g_sem, 1, beyond)
+        gate_pass = remote(gates.at[2], gates.at[3], g_sem, 2, across)
+        gate_near.start()
+        gate_far.start()
+        for step in range(1, lines):
+            sz_copy(step).wait_recv()
+            stotal[...] += sz_in[step - 1].astype(F32)
+        shared_near = remote(shared.at[0], shared.at[1], s_sem, 0, across)
+        shared_far = remote(shared.at[2], shared.at[3], s_sem, 1, beyond)
+        shared[0, :, 0 : 2 * LANES] = stotal[:, 0 : 2 * LANES]
+        steps = pltpu.roll(stotal[:, 2 * LANES :], rank * heads, 1)
+        place = iota(steps.shape, 1) - rank * heads
+        shared[0, :, 2 * LANES :] = jnp.where((place >= 0) & (place < heads), steps, 0.0)
+        shared_near.start()
         flat_step(2)
-        b_block(2)
+        v_block(order[-1])
+        lax.fori_loop(3, 6, down, 0)
+        shared_near.wait_recv()
+        shared[2] = shared[0] + shared[1]
+        shared_far.start()
         gate_far.wait_recv()
         gate_pass.start()
-        b_block(3)
         for k in range(3, len(hops)):
             flat_step(k)
         flat_put = pltpu.make_async_copy(flat_in.at[last], flatout_ref, put_sem.at[10])
         flat_put.start()
-        lax.fori_loop(5, count - 1, down, 0)
+        lax.fori_loop(6, count, down, 0)
 
         for step in range(1, lines):
-            bz_copy(step).wait_recv()
-            btotal[...] += bz_in[step - 1].astype(F32)
-        values[0] = btotal[:, 0:inner]
+            vz_copy(step).wait_recv()
+            vtotal[...] += vz_in[step - 1].astype(F32)
+        values[0] = vtotal[...].astype(BF16)
         value_near = remote(values.at[0], values.at[1], v_sem, 0, across)
         value_far = remote(values.at[0], values.at[2], v_sem, 1, beyond)
         value_pass = remote(values.at[2], values.at[3], v_sem, 2, across)
-        shared_near = remote(shared.at[0], shared.at[1], s_sem, 0, across)
-        shared_far = remote(shared.at[2], shared.at[3], s_sem, 1, beyond)
-        shared[0, :, 0 : 2 * LANES] = btotal[:, inner : inner + 2 * LANES]
-        steps = pltpu.roll(btotal[:, inner + 2 * LANES :], rank * heads, 1)
-        place = iota(steps.shape, 1) - rank * heads
-        shared[0, :, 2 * LANES :] = jnp.where((place >= 0) & (place < heads), steps, 0.0)
-        shared_near.start()
         value_far.start()
         value_near.start()
-        finish_hidden(0, 0)
-        shared_near.wait_recv()
-        shared[2] = shared[0] + shared[1]
-        shared_far.start()
 
         def put(source, k, first, owner, index):
             column = pl.multiple_of(first + owner * inner, LANES)
             return pltpu.make_async_copy(source.at[k], gin_ref.at[:, pl.ds(column, inner)], put_sem.at[index])
 
         owners = (rank, rank + 1 - 2 * core, (rank + 2) % 4, (rank + 3 - 2 * core) % 4)
-        puts = [put(gates, 0, 0, owners[0], 0), put(values, 0, inner_all, owners[0], 4)]
         gate_near.wait_recv()
         gate_pass.wait_recv()
-        puts += [put(gates, k, 0, owners[k], k) for k in range(1, 4)]
-        value_near.wait_recv()
-        puts.append(put(values, 1, inner_all, owners[1], 5))
-        for copy in puts:
-            copy.start()
-        value_far.wait_recv()
-        value_pass.start()
-        puts.append(put(values, 2, inner_all, owners[2], 6))
-        puts[-1].start()
+        puts = [put(gates, k, 0, owners[k], k) for k in range(4)]
         shared_far.wait_recv()
         shared[1] = shared[2] + shared[3]
         puts.append(
@@ -873,10 +877,22 @@
                 shared.at[1], gin_ref.at[:, pl.ds(2 * inner_all, 3 * LANES)], put_sem.at[8]
             )
         )
-        puts[-1].start()
+        for copy in puts:
+            copy.start()
+
+        def put_values(k):
+            vbuf[k] = values[k].astype(F32)
+            puts.append(put(vbuf, k, inner_all, owners[k], 4 + k))
+            puts[-1].start()
+
+        put_values(0)
+        value_near.wait_recv()
+        put_values(1)
+        value_far.wait_recv()
+        value_pass.start()
+        put_values(2)
         value_pass.wait_recv()
-        puts.append(put(values, 3, inner_all, owners[3], 7))
-        puts[-1].start()
+        put_values(3)
 
         def drain(k, carry):
             h_copy(k).wait_send()
@@ -889,7 +905,8 @@
         lax.fori_loop(0, count, drain, 0)
         for step in range(1, lines):
             az_copy(step).wait_send()
-            bz_copy(step).wait_send()
+            sz_copy(step).wait_send()
+            vz_copy(step).wait_send()
         for copy in (
             gate_near, gate_far, gate_pass, value_near, value_far, value_pass, shared_near, shared_far,
         ):
@@ -964,16 +981,20 @@
             vmem((tokens // 2, inner), F32), vmem((SPAN, LANES), F32), vmem((tokens // 2, LANES), F32),
             vmem((tokens // 2, model), BF16),
             vmem((tokens // 2, model), BF16), vmem((tokens // 2, model), BF16),
-            vmem((tokens // 2, model), BF16), vmem((half, model), F32),
+            vmem((tokens // 2, model), BF16), vmem((SPAN, model), F32),
             dma((2, count)), dma((2, count)), dma((2, count)), dma((count,)),
             vmem((tokens // 2, model), BF16), vmem((tokens // 2, model), BF16),
             dma((2, count - early)), dma((2, count)), dma((count,)),
             vmem((blocks * LANES, 2 * inner), BF16), vmem((blocks * LANES, 2 * inner), BF16),
             dma((2, blocks)), vmem((fars, depth, 2 * inner), BF16), dma((2, fars)),
             vmem((depth, 2 * inner), F32),
-            vmem((blocks * LANES, wide), BF16), vmem((blocks * LANES, wide), BF16),
-            dma((2, blocks)), vmem((fars, depth, wide), BF16), dma((2, fars)), vmem((depth, wide), F32),
-            vmem((4, depth, inner), F32), dma((2, 3)), vmem((4, depth, inner), F32), dma((2, 3)),
+            vmem((blocks * LANES, 3 * LANES), BF16), vmem((blocks * LANES, 3 * LANES), BF16),
+            dma((2, blocks)), vmem((fars, depth, 3 * LANES), BF16), dma((2, fars)),
+            vmem((depth, 3 * LANES), F32), vmem((blocks * LANES, 3 * LANES), F32),
+            vmem((blocks * LANES, inner), BF16), vmem((blocks * LANES, inner), BF16),
+            dma((2, blocks)), vmem((fars, depth, inner), BF16), dma((2, fars)), vmem((depth, inner), F32),
+            vmem((blocks * LANES, inner), F32), vmem((4, depth, inner), F32),
+            vmem((4, depth, inner), F32), dma((2, 3)), vmem((4, depth, inner), BF16), dma((2, 3)),
             vmem((4, depth, 3 * LANES), F32), dma((2, 2)), dma((11,)),
             vmem((rows, LANES), F32), vmem((2 * hops + 1, rows, LANES), F32), dma((2, hops)),
         ],
@@ -986,6 +1007,82 @@
     )(
         docs, hidden, gate, dn, gate, ssd, dn, ssd, mixed, pre, stp, states, sums, *consts, *big
     )
+
+
+def finish_kernel(
+    dims, cot_ref, delta_ref, layer_ref, gin_ref, flat_ref,
+    out_ref, grad_ref, norm_ref, win_ref, taps_ref, bias_ref, dt_ref, decay_ref, skip_ref, gain_ref,
+):
+    inner_all, heads = dims
+    grad_ref[...] = cot_ref[...].astype(F32) + delta_ref[...].astype(F32)
+    out_ref[...] = layer_ref[...]
+    win_ref[...] = gin_ref[:, 0 : win_ref.shape[1]]
+
+    @pl.when(pl.program_id(0) == 0)
+    def _():
+        at = norm_ref.shape[1] // LANES
+
+        def spread(dst, row, first, count):
+            for k in range(count):
+                dst[row : row + 1, k * LANES : (k + 1) * LANES] = flat_ref[first + k : first + k + 1]
+
+        spread(norm_ref, 0, 0, at)
+        wide = taps_ref.shape[1] // LANES
+        for tap in range(taps_ref.shape[0]):
+            spread(taps_ref, tap, at + tap * wide, wide)
+        at += taps_ref.shape[0] * wide
+        spread(bias_ref, 0, at, wide)
+        at += wide
+        dt_ref[...] = flat_ref[at : at + 1, 0:heads]
+        decay_ref[...] = flat_ref[at : at + 1, heads : 2 * heads]
+        at += 1
+        spread(gain_ref, 0, at, inner_all // LANES)
+        at += inner_all // LANES
+        per = inner_all // heads
+        lane = iota((1, LANES), 1)
+        found = jnp.zeros((1, LANES), F32)
+        for k in range(inner_all // LANES):
+            row = flat_ref[at + k : at + k + 1]
+            for part in range(LANES // per):
+                inside = (lane >= part * per) & (lane < (part + 1) * per)
+                total = jnp.sum(jnp.where(inside, row, 0.0), axis=1, keepdims=True)
+                found = jnp.where(lane == k * (LANES // per) + part, total, found)
+        skip_ref[...] = found[:, 0:heads]
+
+
+def finish(cotangent, delta, layer_out, grad_in, flat, columns, inner_all, heads):
+    tokens, model = cotangent.shape
+    depth = grad_in.shape[0]
+    steps = 8
+    chan_all = inner_all + 2 * LANES
+
+    def tok(v, size):
+        return pl.BlockSpec((v // steps, size), lambda i: (i, 0))
+
+    def full(shape):
+        return pl.BlockSpec(shape, lambda i: (0,) * len(shape))
+
+    small = [(1, model), (4, chan_all), (1, chan_all), (1, heads), (1, heads), (1, heads), (1, inner_all)]
+    if depth % (8 * steps) == 0:
+        rows, shown = tok(depth, grad_in.shape[1]), tok(depth, columns)
+    else:
+        rows, shown = full(grad_in.shape), full((depth, columns))
+    return pl.pallas_call(
+        lambda *refs: finish_kernel((inner_all, heads), *refs),
+        out_shape=[
+            jax.ShapeDtypeStruct((tokens, model), BF16),
+            jax.ShapeDtypeStruct((tokens, model), F32),
+            jax.ShapeDtypeStruct(small[0], F32),
+            jax.ShapeDtypeStruct((depth, columns), F32),
+        ]
+        + [jax.ShapeDtypeStruct(v, F32) for v in small[1:]],
+        grid=(steps,),
+        in_specs=[tok(tokens, model)] * 3 + [rows, full(flat.shape)],
+        out_specs=[tok(tokens, model)] * 2 + [full(small[0]), shown] + [full(v) for v in small[1:]],
+        compiler_params=pltpu.CompilerParams(dimension_semantics=("arbitrary",)),
+        cost_estimate=cost(9.0),
+        name="finish",
+    )(cotangent, delta, layer_out, grad_in, flat)
 
 
 def gather_kernel(
@@ -1180,18 +1277,12 @@
         doc_ids, hidden_in, held, sums, params, row(gate_gain), row(norm_gain), sorted_parts, w_in,
         mine, far, heads, lines, depth, early,
     )
-    grad_input = cotangent.astype(F32) + delta.astype(F32)
-    chan_all = inner_all + 2 * LANES
-    flat = flat.reshape(-1)
-    cuts, at = [], 0
-    for size in (model, 5 * chan_all, LANES, inner_all, inner_all):
-        cuts.append(flat[at : at + size])
-        at += size
-    conv_all = cuts[1].reshape(5, chan_all)
+    layer_out, grad_input, g_norm, grad_in_weight, taps, bias, dt, decay, skip, gain = finish(
+        cotangent, delta, layer_out, grad_in, flat, in_weight.shape[1], inner_all, head_all
+    )
     return (
-        layer_out, grad_input, cuts[0], grad_in[:, : in_weight.shape[1]], conv_all[:4], conv_all[4],
-        cuts[2][:head_all], cuts[2][head_all : 2 * head_all],
-        jnp.sum(cuts[4].reshape(head_all, -1), 1), cuts[3], g_out,
+        layer_out, grad_input, g_norm.reshape(-1), grad_in_weight, taps, bias.reshape(-1),
+        dt.reshape(-1), decay.reshape(-1), skip.reshape(-1), gain.reshape(-1), g_out,
     )
 
 

time: 278 us -> 231 us (0.83)
  Pallas kernels: 251 us -> 220 us
  local copies, waits for them, and re-layouts: 16.5 us -> 7.72 us
  other arithmetic: 9.63 us -> 1.37 us
    pallas_call x1, Pallas kernels: 143 us -> 105 us  [mixer_backward(): pl.pallas_call(lambda *refs: backward_kernel((inner, heads, inner_all, li...]
    pallas_call x0 -> x1, Pallas kernels: none -> 12.9 us  [finish(): pl.pallas_call(lambda *refs: finish_kernel((inner_all, heads), *refs), ou...]
    add x1 -> x0, other arithmetic: 9 us -> none  [body(): grad_input = cotangent.astype(F32) + delta.astype(F32)]
    pallas_call x1, Pallas kernels: 49 us -> 43.1 us  [mixer_forward(): pl.pallas_call(lambda *refs: forward_kernel((inner, heads, early), *refs)...]
    slice x5 -> x0, local copies, waits for them, and re-layouts: 5.39 us -> none  [the longest x2 2.65 us: body(): cuts.append(flat[at:at + size])]
    unnamed x10 -> x7, local copies, waits for them, and re-layouts: 7.58 us -> 5.57 us
where the time goes in v1:
time: 231 us; the launch traced here: 229 us
  Pallas kernels  220 us (95%)
  local copies, waits for them, and re-layouts  7.72 us (3%)
    pallas_call x1, Pallas kernels, mixer_backward(): pl.pallas_call(lambda *refs: backward_kernel((inner, heads, inner_all, li...  105 us
    pallas_call x1, Pallas kernels, gather_weights(): pl.pallas_call(lambda *refs: gather_kernel((lines, depth, inner, inner_al...  59 us
    pallas_call x1, Pallas kernels, mixer_forward(): pl.pallas_call(lambda *refs: forward_kernel((inner, heads, early), *refs)...  43.1 us
    pallas_call x1, Pallas kernels, finish(): pl.pallas_call(lambda *refs: finish_kernel((inner_all, heads), *refs), ou...  12.9 us
    unnamed x7, local copies, waits for them, and re-layouts  5.57 us

profile of v1, /device:TPU:0, one launch (start us, length us, event | category | flops | bytes accessed | tf_op | source)
XLA Modules:
  0.0 229.3 jit_solution(12085154974499855830)
XLA Ops:
  0.6 1.3 reshape.61.refs_6_.refs_14_
  2.0 1.7 copy.24.refs_3_
  3.7 0.0 copy-start
  3.7 0.1 constant_dynamic-slice_fusion
  3.8 0.8 pad.4.refs_4_
  4.5 0.2 copy-done
  4.7 59.0 %gather_weights.1 = (bf16[1024,1408]{1,0:T(8,128)(2,1)}, bf16[1024,512]{1,0:T(8,128)(2,1)}, bf16[2048,1024]{1,0:T(8,128)(2,1)}, bf16[2048,512]{1,0:T(8,128)(2,1)...) custom-call(bf16[2048,1024]{1,0:T(8,128)(2,1)} %refs_1_.3, ...), custom_call_target="tpu_custom_call" | custom-call | flops 51749998592 | bytes 1048576 | tf_op jit(solution)/shard_map/gather_weights/pallas_call | solution.py:1211
  63.6 43.1 %mixer_forward.1 = (f32[2048,512]{1,0:T(8,128)}, f32[2048,768]{1,0:T(8,128)}, f32[2048,768]{1,0:T(8,128)}, f32[2048,512]{1,0:T(8,128)}, f32[2048,128]{1,0:T(8,12...) custom-call(s32[1,2048]{1,0:T(1,128)} %refs_0_.6, ...), custom_call_target="tpu_custom_call" | custom-call | flops 46000001024 | bytes 1048576 | tf_op jit(solution)/shard_map/mixer_forward/pallas_call | solution.py:328
  106.7 104.6 %mixer_backward.1 = (bf16[2048,1024]{1,0:T(8,128)(2,1)}, bf16[2048,1024]{1,0:T(8,128)(2,1)}, f32[128,4480]{1,0:T(8,128)}, f32[128,512]{1,0:T(8,128)}, f32[136,128]{1,0:T(8,128)}) custom-call(s32[1,2048]{1,0:T(1,128)} %refs_0_.6, bf16[2048,1024]{1,0:T(8,128)(2,1)} %refs_1_.3, f32[2048,512]{1,0:T(8,128)} %get-tuple-element.46.refs_2_.refs_4_, ...), custom_call_target="tpu_custom_call" | custom-call | flops 103499997184 | bytes 1048576 | tf_op jit(solution)/shard_map/mixer_backward/pallas_call | solution.py:953
  211.3 12.9 %finish.1 = (bf16[2048,1024]{1,0:T(8,128)(2,1)}, f32[2048,1024]{1,0:T(8,128)}, f32[1,1024]{1,0:T(1,128)}, f32[128,4384]{1,0:T(8,128)}, f32[4,2304]{1,0:T(4,128)}...) custom-call(bf16[2048,1024]{1,0:T(8,128)(2,1)} %refs_0_.7, ...), custom_call_target="tpu_custom_call" | custom-call | flops 10350000128 | bytes 1048576 | tf_op jit(solution)/shard_map/finish/pallas_call | solution.py:1070
  224.3 0.0 copy-start.1
  224.3 1.4 reduce
  225.6 3.0 %copy.25 = f32[128,4384]{0,1:T(8,128)} copy(f32[128,4384]{1,0:T(8,128)} %get-tuple-element.78) | data formatting | bytes 4489216
  228.6 0.0 copy-done.1
  228.6 0.7 copy.27
Async XLA Ops:
  3.7 1.0 copy-start
  224.3 4.4 %copy-start.1 = (f32[128,512]{1,0:T(8,128)S(1)}, f32[128,512]{1,0:T(8,128)}, u32[]{:S(2)}) copy-start(f32[128,512]{1,0:T(8,128)} %get-tuple-element.107) | copy-start | bytes 786436

commit v2 on v1

--- a/solution.py
+++ b/solution.py
@@ -9,6 +9,7 @@
 LANES = 128
 EPS = 1e-05
 FAR = -1e30
+LOG2_E = 1.4426950408889634
 VMEM_MOST = 60 * 2**20
 F32 = jnp.float32
 BF16 = jnp.bfloat16
@@ -39,34 +40,30 @@
 
 
 def as_row(block):
-    return jnp.sum(jnp.transpose(block), axis=0, keepdims=True)
-
-
-def split3(v):
-    hi = v.astype(BF16)
-    rest = v - hi.astype(F32)
-    mid = rest.astype(BF16)
-    low = (rest - mid.astype(F32)).astype(BF16)
-    return hi, mid, low
-
-
-def tri_sum(tri, v, heads):
-    lane = iota(v.shape, 1)
-    v = jnp.where(lane < heads, v, 0.0)
+    ones = jnp.ones((16, LANES), BF16)
+    hi = block.astype(BF16)
+    low = (block - hi.astype(F32)).astype(BF16)
+    return (nt(ones, hi) + nt(ones, low))[0:1]
+
+
+def sigmoid(v):
+    return 0.5 * jnp.tanh(0.5 * v) + 0.5
+
+
+def row_sum(v, tri):
     hi = v.astype(BF16).astype(F32)
     rest = v - hi
     mid = rest.astype(BF16).astype(F32)
-    low = rest - mid
-    packed = hi + pltpu.roll(mid, heads, 1) + pltpu.roll(low, 2 * heads, 1)
-    out = nn(tri, packed.astype(BF16))
-    return out + pltpu.roll(out, LANES - heads, 1) + pltpu.roll(out, LANES - 2 * heads, 1)
-
-
-def pair_lanes(cols, pair, low_half):
+    count = v.shape[0]
+    out = nn(jnp.concatenate([hi, mid, rest - mid], 0).astype(BF16), tri)
+    return out[0:count] + out[count : 2 * count] + out[2 * count :]
+
+
+def pair_lanes(cols, first, low_half):
     rows = cols.shape[0]
-    first = jnp.broadcast_to(cols[:, 2 * pair : 2 * pair + 1], (rows, LANES))
-    second = jnp.broadcast_to(cols[:, 2 * pair + 1 : 2 * pair + 2], (rows, LANES))
-    return jnp.where(low_half, first, second)
+    left = jnp.broadcast_to(cols[:, first : first + 1], (rows, LANES))
+    right = jnp.broadcast_to(cols[:, first + 1 : first + 2], (rows, LANES))
+    return jnp.where(low_half, left, right)
 
 
 def exact_nt(a, b):
@@ -93,21 +90,45 @@
     return out[0:1]
 
 
+def own_rows_of(row, rank, heads):
+    total = row.shape[1]
+    place = iota((heads, total), 1) == rank * heads + iota((heads, total), 0)
+    picked = jnp.where(place, jnp.broadcast_to(row, (heads, total)), 0.0)
+    return jnp.broadcast_to(jnp.sum(picked, axis=1, keepdims=True), (heads, SPAN))
+
+
+def head_scales(raw, rate, doc, enter, extra):
+    step = softplus(raw)
+    log_step = step * rate
+    row_i, col_i = iota((SPAN, SPAN), 0), iota((SPAN, SPAN), 1)
+    running = row_sum(log_step, (row_i <= col_i).astype(BF16))
+    ending = jnp.broadcast_to(running[:, SPAN - 1 :], running.shape)
+    last = jnp.broadcast_to(doc[:, SPAN - 1 :], doc.shape)
+    tail = jnp.where(doc == last, jnp.exp(ending - running), 0.0)
+    reach = jnp.where(doc == enter, jnp.exp(running), 0.0)
+    scaled = running * LOG2_E
+    rows = [scaled, step, tail, reach, doc] + extra
+    used = sum(v.shape[0] for v in rows)
+    packed = jnp.concatenate(rows + [jnp.zeros((LANES - used, SPAN), F32)], 0)
+    return log_step, scaled, jnp.transpose(packed)
+
+
 def fold(v):
     return jnp.sum(v.reshape(SPAN // 8, 8, v.shape[1]), axis=0)
 
 
-def own_params(rank, heads, inner, inner_all, dtb_ref, dec_ref, skip_ref, cw_ref, cb_ref, par, cwb):
+def own_params(rank, heads, inner, inner_all, dtb_ref, dec_ref, skip_ref, cw_ref, cb_ref, par, skips, cwb):
     chan = inner + 2 * LANES
     off = pl.multiple_of(rank * inner, LANES)
     taps = cw_ref.shape[0]
-    par[0:1] = own_lanes(dtb_ref[...], rank, heads)
-    par[1:2] = -jnp.exp(own_lanes(dec_ref[...], rank, heads))
-    par[2:3] = own_lanes(skip_ref[...], rank, heads)
+    par[0] = own_rows_of(dtb_ref[...], rank, heads)
+    par[1] = -jnp.exp(own_rows_of(dec_ref[...], rank, heads))
+    skips[0:1] = own_lanes(skip_ref[...], rank, heads)
     cwb[0:taps, 0:inner] = cw_ref[:, pl.ds(off, inner)].astype(F32)
     cwb[0:taps, inner:chan] = cw_ref[:, inner_all:].astype(F32)
-    cwb[taps : taps + 1, 0:inner] = cb_ref[:, pl.ds(off, inner)]
-    cwb[taps : taps + 1, inner:chan] = cb_ref[:, inner_all:]
+    for k in range(chan // LANES):
+        row = rank * (inner // LANES) + k if k < inner // LANES else (inner_all - inner) // LANES + k
+        cwb[taps : taps + 1, k * LANES : (k + 1) * LANES] = cb_ref[pl.ds(row, 1), :]
 
 
 MESH_IDS = pl.DeviceIdType.MESH
@@ -118,7 +139,7 @@
     dtb_ref, dec_ref, skip_ref, ggain_ref,
     gate_ref, mixed_ref, pre_ref, ssd_ref, stp_ref, state_ref, dn_ref,
     sums_ref, mine_ref, far_ref,
-    xbuf, dbuf, state, par, cwb, gain, gg_ref,
+    xbuf, dbuf, state, par, skips, cwb, gain, gg_ref,
     own_sums, h_out, h_in, kept, mine, far, h_sem, y_sem, s_in, s_sem, put_sem,
 ):
     inner, heads, early = dims
@@ -143,7 +164,7 @@
         xbuf[0:8] = jnp.zeros((8, chan), F32)
         dbuf[0:8] = jnp.full((8, LANES), -1.0, F32)
         state[...] = jnp.zeros(state.shape, F32)
-        own_params(rank, heads, inner, inner_all, dtb_ref, dec_ref, skip_ref, cw_ref, cb_ref, par, cwb)
+        own_params(rank, heads, inner, inner_all, dtb_ref, dec_ref, skip_ref, cw_ref, cb_ref, par, skips, cwb)
         gain[0:1] = ggain_ref[:, pl.ds(pl.multiple_of(rank * inner, LANES), inner)]
 
     def slot(k):
@@ -166,16 +187,19 @@
         mine[slot(k)] = (kept[slot(core)] + h_in[slot(k)].astype(F32)).astype(BF16)
 
     nb = normed_ref[...]
-    xbuf[8 : 8 + SPAN] = nn(nb, win_ref[:, inner : inner + chan])
-    gate_ref[...] = nn(nb, win_ref[:, 0:inner])
-    stp = nn(nb, win_ref[:, inner + chan : inner + chan + LANES])
+    xbuf[8 : 8 + SPAN] = nt(nb, win_ref[inner : inner + chan])
+    gate_ref[...] = nt(nb, win_ref[0:inner])
+    both_cores = nt(win_ref[inner + chan : inner + chan + 2 * heads], nb)
+    stp = jnp.where(core == 0, both_cores[0:heads], both_cores[heads:])
     stp_ref[...] = stp
     mixed_ref[...] = xbuf[8 : 8 + SPAN]
     dn_ref[...] = nn(cot_ref[...], wout_ref[...])
 
     drow = docs_ref[:, pl.ds(pl.multiple_of(i * SPAN, SPAN), SPAN)].astype(F32)
-    dcol = as_column(drow)
-    enter = dbuf[7:8]
+    doc = jnp.broadcast_to(drow, (heads, SPAN))
+    enter = jnp.broadcast_to(dbuf[7:8, 0:1], (heads, SPAN))
+    _, run_rows, cols = head_scales(stp + par[0], par[1], doc, enter, [])
+    dcol = jnp.broadcast_to(cols[:, 4 * heads : 4 * heads + 1], (SPAN, LANES))
     dbuf[8 : 8 + SPAN] = dcol
     keeps = [None] + [dbuf[8 - k : 8 - k + SPAN] == dcol for k in range(1, 4)]
 
@@ -187,19 +211,12 @@
                 keeps[k], xbuf[8 - k : 8 - k + SPAN, lanes], 0.0
             )
         pre_ref[:, lanes] = acc
-        return acc * jax.nn.sigmoid(acc)
+        return acc * sigmoid(acc)
 
     b_act, c_act = conv(pairs), conv(pairs + 1)
     b_rows, c_rows = b_act.astype(BF16), c_act.astype(BF16)
 
-    step = softplus(stp + par[0:1])
     row_i, col_i = iota((SPAN, SPAN), 0), iota((SPAN, SPAN), 1)
-    tril = (row_i >= col_i).astype(BF16)
-    running = tri_sum(tril, step * par[1:2], heads)
-    run_rows = jnp.transpose(running)
-    ending = running[SPAN - 1 : SPAN]
-    tail = jnp.where(dcol == dcol[SPAN - 1 : SPAN], jnp.exp(ending - running), 0.0)
-    reach = jnp.where(dcol == enter, jnp.exp(running), 0.0)
     same = jnp.concatenate([dcol, dcol], 1) == drow
     bias = jnp.where(same & (row_i >= col_i), 0.0, FAR)
     scores = exact_nt(c_act, b_act)
@@ -210,10 +227,10 @@
     for pair in range(pairs):
         lanes = slice(pair * LANES, (pair + 1) * LANES)
         act = conv(pair)
-        scaled = act * pair_lanes(step, pair, low_half)
+        scaled = act * pair_lanes(cols, heads + 2 * pair, low_half)
         xb = scaled.astype(BF16)
-        tail_l = pair_lanes(tail, pair, low_half)
-        reach_l = pair_lanes(reach, pair, low_half)
+        tail_l = pair_lanes(cols, 2 * heads + 2 * pair, low_half)
+        reach_l = pair_lanes(cols, 3 * heads + 2 * pair, low_half)
         held = state[:, lanes]
         held_b = held.astype(BF16)
         state_ref[0, :, lanes] = held_b
@@ -226,16 +243,16 @@
             for blk in range(2):
                 rows = slice(blk * half, (blk + 1) * half)
                 width = (blk + 1) * half
-                gap = running[rows, head : head + 1] - run_rows[head : head + 1, 0:width]
-                weight = jnp.exp(gap + bias[rows, 0:width]) * scores[rows, 0:width]
+                gap = cols[rows, head : head + 1] - run_rows[head : head + 1, 0:width]
+                weight = jnp.exp2(gap + bias[rows, 0:width]) * scores[rows, 0:width]
                 blocks.append(nn(weight.astype(BF16), xb[0:width]))
             parts.append(jnp.concatenate(blocks, 0))
         out = out + jnp.where(low_half, parts[0], parts[1])
-        skip_l = pair_lanes(par[2:3], pair, low_half[0:1])
+        skip_l = pair_lanes(skips[0:1], 2 * pair, low_half[0:1])
         ssd = out + skip_l * act
         ssd_ref[:, lanes] = ssd
         gate = gate_ref[:, lanes]
-        gated = ssd * (gate * jax.nn.sigmoid(gate))
+        gated = ssd * (gate * sigmoid(gate))
         square = square + gated * gated
         gained = gain[0:1, lanes] * gated
         gg_ref[:, lanes] = gained.astype(BF16)
@@ -311,7 +328,7 @@
         jax.ShapeDtypeStruct((tokens, chan), F32),
         jax.ShapeDtypeStruct((tokens, chan), F32),
         jax.ShapeDtypeStruct((tokens, inner), F32),
-        jax.ShapeDtypeStruct((tokens, LANES), F32),
+        jax.ShapeDtypeStruct((heads, tokens), F32),
         jax.ShapeDtypeStruct((spans, LANES, inner), BF16),
         jax.ShapeDtypeStruct((tokens, inner), F32),
         jax.ShapeDtypeStruct(sums, F32),
@@ -319,7 +336,7 @@
         jax.ShapeDtypeStruct((early * SPAN // 2, model), BF16),
     )
     out_specs = (
-        tok(inner), tok(chan), tok(chan), tok(inner), tok(LANES),
+        tok(inner), tok(chan), tok(chan), tok(inner), pl.BlockSpec((heads, SPAN), lambda i: (0, i)),
         pl.BlockSpec((1, LANES, inner), lambda i: (i, 0, 0)),
         tok(inner), full(sums), anywhere, anywhere,
     )
@@ -333,7 +350,7 @@
         out_specs=out_specs,
         scratch_shapes=[
             vmem((SPAN + 8, chan), F32), vmem((SPAN + 8, LANES), F32), vmem((LANES, inner), F32),
-            vmem((8, LANES), F32), vmem((8, chan), F32), vmem((8, inner), F32),
+            vmem((2, heads, SPAN), F32), vmem((8, LANES), F32), vmem((8, chan), F32), vmem((8, inner), F32),
             vmem((SPAN, inner), BF16), vmem(sums, F32),
             vmem((tokens // 2, model), BF16), vmem((tokens // 2, model), BF16),
             vmem((SPAN, model), F32), vmem((tokens // 2, model), BF16),
@@ -357,7 +374,7 @@
     naway_ref, nhere_ref, caway_ref, chere_ref, w_ref, mine_ref, far_ref,
     delta_ref, layer_ref, gin_ref, gout_ref, flatout_ref,
     naway, nhere, caway, chere, w, loads,
-    pbuf, dbuf, dstate, par, cwb, gain,
+    pbuf, dbuf, dstate, par, skips, cwb, gain, w_step, sumv,
     gconv, gskip, ghead, ggain, gnorm,
     nout_all, dgate_all, dall, dssd_low, inv_now, inv_own, hid_own,
     h_out, mine, y_in, kept, h_sem, y_sem, d_sem, d_put,
@@ -378,7 +395,7 @@
     mid = count // 2
     c = count - 1 - i
     half = SPAN // 2
-    model = w.shape[0]
+    model = w.shape[1]
     blocks = lines * depth // LANES
     rank, drank = lax.axis_index("tensor"), lax.axis_index("dp")
     line, side = drank // 2, drank % 2
@@ -463,7 +480,7 @@
         pbuf[SPAN : SPAN + 8] = jnp.zeros((8, chan), F32)
         dbuf[SPAN : SPAN + 8] = jnp.full((8, LANES), -2.0, F32)
         dstate[...] = jnp.zeros(dstate.shape, F32)
-        own_params(rank, heads, inner, inner_all, dtb_ref, dec_ref, skip_ref, cw_ref, cb_ref, par, cwb)
+        own_params(rank, heads, inner, inner_all, dtb_ref, dec_ref, skip_ref, cw_ref, cb_ref, par, skips, cwb)
         gain[0:1] = ggain_ref[:, pl.ds(off, inner)]
         for acc in (gconv, gskip, ghead, ggain, gnorm):
             acc[...] = jnp.zeros(acc.shape, F32)
@@ -516,16 +533,20 @@
     hid_own[lot(c, half)] = hid_ref[lot(core, half)]
 
     def inverse(k):
-        inv = lax.rsqrt(as_column(sums_ref[0, pl.ds(k, 1), :]) * (1.0 / inner_all) + EPS)
-        pull = as_column(sums_ref[1, pl.ds(k, 1), :]) * (inv * inv * inv) * (1.0 / inner_all)
+        inv = lax.rsqrt(sums_ref[0, pl.ds(k, 1), :] * (1.0 / inner_all) + EPS)
+        pull = sums_ref[1, pl.ds(k, 1), :] * (inv * inv * inv) * (1.0 / inner_all)
+        return inv, pull
+
+    def spread_inverse(k, cols, first):
+        inv = jnp.broadcast_to(cols[:, first : first + 1], (SPAN, LANES))
         inv_now[...] = inv
         inv_own[lot(k, half)] = inv_now[lot(core, half)]
-        return inv, pull
+        return inv, jnp.broadcast_to(cols[:, first + 1 : first + 2], (SPAN, LANES))
 
     def gating(k, scales, lanes, gate_in, ssd_in, dn_in):
         inv, pull = scales
         gate = gate_in[:, lanes]
-        sig = jax.nn.sigmoid(gate)
+        sig = sigmoid(gate)
         silu = gate * sig
         ssd = ssd_in[:, lanes]
         gated = ssd * silu
@@ -549,35 +570,37 @@
         o_local(k).start()
 
     def scan_step(first):
+        drow = docs_ref[:, lot(c, SPAN)].astype(F32)
+        before = docs_ref[:, lot(jnp.maximum(c - 1, 0), SPAN)].astype(F32)
+        doc = jnp.broadcast_to(drow, (heads, SPAN))
+        enter = jnp.broadcast_to(before[:, SPAN - 1 :], (heads, SPAN))
+        enter = jnp.where(c == 0, -1.0, enter)
+        extra = []
         if first:
-            scales, low_scales = inverse(c), inverse(c - mid)
-        drow = docs_ref[:, lot(c, SPAN)].astype(F32)
-        dcol = as_column(drow)
-        before = docs_ref[:, lot(jnp.maximum(c - 1, 0), SPAN)].astype(F32)
-        enter = as_column(before)[SPAN - 1 : SPAN]
-        enter = jnp.where(c == 0, -1.0, enter)
+            row = iota((8, SPAN), 0)
+            block = jnp.zeros((8, SPAN), F32)
+            for k, v in enumerate(inverse(c) + inverse(c - mid)):
+                block = jnp.where(row == k, jnp.broadcast_to(v, (8, SPAN)), block)
+            extra = [block]
+        raw = stp_ref[...] + par[0]
+        log_step, run_rows, cols = head_scales(raw, par[1], doc, enter, extra)
+        dcol = jnp.broadcast_to(cols[:, 4 * heads : 4 * heads + 1], (SPAN, LANES))
+        if first:
+            scales = spread_inverse(c, cols, 5 * heads)
+            low_scales = spread_inverse(c - mid, cols, 5 * heads + 2)
         dbuf[0:SPAN] = dcol
         keeps = [None] + [dbuf[k : k + SPAN] == dcol for k in range(1, 4)]
         if not first:
             block = lax.rem(i - mid + 1, blocks)
             ax_out[lot(block, LANES)] = out_grads(naway, caway, block).astype(BF16)
-        raw = stp_ref[...] + par[0:1]
-        step = softplus(raw)
         row_i, col_i = iota((SPAN, SPAN), 0), iota((SPAN, SPAN), 1)
-        tril = (row_i >= col_i).astype(BF16)
-        log_step = step * par[1:2]
-        running = tri_sum(tril, log_step, heads)
-        run_rows = jnp.transpose(running)
-        ending = running[SPAN - 1 : SPAN]
-        tail = jnp.where(dcol == dcol[SPAN - 1 : SPAN], jnp.exp(ending - running), 0.0)
-        reach = jnp.where(dcol == enter, jnp.exp(running), 0.0)
         same = jnp.concatenate([dcol, dcol], 1) == drow
         bias = jnp.where(same & (row_i <= col_i), 0.0, FAR)
 
         def activate(group):
             lanes = slice(group * LANES, (group + 1) * LANES)
             pre = pre_ref[:, lanes]
-            sig = jax.nn.sigmoid(pre)
+            sig = sigmoid(pre)
             return pre * sig, sig * (1.0 + pre * (1.0 - sig))
 
         b_act, b_slope = activate(pairs)
@@ -589,24 +612,14 @@
         d_scores = [jnp.zeros((half, SPAN), F32), jnp.zeros((half, half), F32)]
         d_b = jnp.zeros((SPAN, LANES), F32)
         d_c = jnp.zeros((SPAN, LANES), F32)
-        head_up = jnp.zeros((SPAN, LANES), F32)
-        head_down = jnp.zeros((SPAN, LANES), F32)
-        head_step = jnp.zeros((SPAN, LANES), F32)
-        head_hold = jnp.zeros((8, LANES), F32)
+        holds = []
         for pair in range(pairs):
             lanes = slice(pair * LANES, (pair + 1) * LANES)
-            ones_at = (iota((LANES, LANES), 1) == 2 * pair + iota((LANES, LANES), 0) // (LANES // 2)).astype(BF16)
-
-            def head_sum(v):
-                hi = v.astype(BF16)
-                low = (v - hi.astype(F32)).astype(BF16)
-                return nn(hi, ones_at) + nn(low, ones_at)
-
             act, slope = activate(pair)
-            step_l = pair_lanes(step, pair, low_half)
-            tail_l = pair_lanes(tail, pair, low_half)
-            reach_l = pair_lanes(reach, pair, low_half)
-            skip_l = pair_lanes(par[2:3], pair, low_half[0:1])
+            step_l = pair_lanes(cols, heads + 2 * pair, low_half)
+            tail_l = pair_lanes(cols, 2 * heads + 2 * pair, low_half)
+            reach_l = pair_lanes(cols, 3 * heads + 2 * pair, low_half)
+            skip_l = pair_lanes(skips[0:1], 2 * pair, low_half[0:1])
             ssd = ssd_ref[:, lanes]
             if first:
                 d_ssd = gating(c, scales, lanes, gate_ref, ssd_ref, dn_ref)
@@ -631,22 +644,25 @@
                 tiles = []
                 for blk in range(2):
                     rows = slice(blk * half, (blk + 1) * half)
-                    cols = slice(blk * half, SPAN)
-                    gap = run_rows[head : head + 1, cols] - running[rows, head : head + 1]
-                    decay = jnp.exp(gap + bias[rows, cols])
-                    tiles.append(nn((decay * scores[rows, cols]).astype(BF16), dyb[cols]))
-                    d_scores[blk] = d_scores[blk] + decay * nt(x_own[rows], dyb[cols])
+                    span = slice(blk * half, SPAN)
+                    gap = run_rows[head : head + 1, span] - cols[rows, head : head + 1]
+                    decay = jnp.exp2(gap + bias[rows, span])
+                    tiles.append(nn((decay * scores[rows, span]).astype(BF16), dyb[span]))
+                    d_scores[blk] = d_scores[blk] + decay * nt(x_own[rows], dyb[span])
                 parts.append(jnp.concatenate(tiles, 0))
             d_within = jnp.where(low_half, parts[0], parts[1])
             from_state = tail_l * nn(b_rows, d_held_b)
             d_scaled = d_within + from_state
             xf = xb.astype(F32)
-            head_up += head_sum(dyb.astype(F32) * (ssd - skip_l * act) - xf * d_within)
-            head_down += head_sum(xf * from_state)
-            head_step += head_sum(d_scaled * act)
+            up = dyb.astype(F32) * (ssd - skip_l * act) - xf * d_within
+            up_hi = up.astype(BF16)
+            sumv[0, :, lanes] = up_hi
+            sumv[1, :, lanes] = (up - up_hi.astype(F32)).astype(BF16)
+            sumv[2, :, lanes] = (xf * from_state).astype(BF16)
+            sumv[3, :, lanes] = (d_scaled * act).astype(BF16)
             hold = reach_l[SPAN - 1 : SPAN]
-            hold_sum = jnp.sum((d_held * held.astype(F32)).reshape(LANES // 8, 8, LANES), axis=0) * hold
-            head_hold += head_sum(hold_sum)
+            held_sum = jnp.sum((d_held * held.astype(F32)).reshape(LANES // 8, 8, LANES), axis=0)
+            holds.append(jnp.sum(held_sum, axis=0, keepdims=True) * hold)
             d_b += nt(xt, d_held_b)
             d_c += nt(ry, held)
             dstate[:, lanes] = hold * d_held + nn(c_turned, ry)
@@ -664,18 +680,24 @@
         pbuf[0:SPAN, inner : inner + LANES] = d_b * b_slope
         pbuf[0:SPAN, inner + LANES : chan] = d_c * c_slope
 
-        triu = (row_i <= col_i).astype(BF16)
-        below = (row_i > col_i).astype(BF16)
+        per_head = inner // heads
+        owner = (iota((2 * heads, inner), 0) == iota((2 * heads, inner), 1) // per_head).astype(BF16)
+        up = (nt(owner, sumv[0]) + nt(owner, sumv[1]))[0:heads]
+        down = nt(owner, sumv[2])[0:heads]
+        direct = nt(owner, sumv[3])[0:heads]
+        hold_row = jnp.broadcast_to(jnp.concatenate(holds, 1), (heads, inner))
+        inside = iota((heads, inner), 0) == iota((heads, inner), 1) // per_head
+        hold_sum = jnp.sum(jnp.where(inside, hold_row, 0.0), axis=1, keepdims=True)
         d_log = (
-            tri_sum(triu, head_up, heads)
-            + tri_sum(below, head_down, heads)
-            + jnp.sum(head_hold, axis=0, keepdims=True)
+            row_sum(up, (row_i >= col_i).astype(BF16))
+            + row_sum(down, (row_i < col_i).astype(BF16))
+            + jnp.broadcast_to(hold_sum, (heads, SPAN))
         )
-        d_step = d_log * par[1:2] + head_step
-        d_raw = jnp.where(iota((SPAN, LANES), 1) < heads, d_step * jax.nn.sigmoid(raw), 0.0)
-        dall[lot(c, SPAN), chan:] = d_raw.astype(BF16)
-        ghead[0] += fold(d_raw)
-        ghead[1] += fold(d_log * log_step)
+        d_raw = (d_log * par[1] + direct) * sigmoid(raw)
+        turned = jnp.transpose(jnp.concatenate([d_raw, jnp.zeros((LANES - heads, SPAN), F32)], 0))
+        dall[lot(c, SPAN), chan:] = turned.astype(BF16)
+        ghead[0] += d_raw
+        ghead[1] += d_log * log_step
 
         for group in range(chan // LANES):
             lanes = slice(group * LANES, (group + 1) * LANES)
@@ -719,9 +741,16 @@
     @pl.when(i == 0)
     def _():
         fetch[1].wait()
+        both_cores = w[inner + chan : inner + chan + 2 * heads].astype(F32)
+        own = jnp.where(core == 0, both_cores[0:heads], both_cores[heads:])
+        w_step[...] = jnp.concatenate([own, jnp.zeros((LANES - heads, model), F32)], 0).astype(BF16)
 
     rows_now = lot(c, SPAN)
-    kept[...] = nt(dgate_all[rows_now], w[:, 0:inner]) + nt(dall[rows_now], w[:, inner:])
+    kept[...] = (
+        nn(dgate_all[rows_now], w[0:inner])
+        + nn(dall[rows_now, 0:chan], w[inner : inner + chan])
+        + nn(dall[rows_now, chan:], w_step[...])
+    )
     h_out[lot(c, half)] = kept[lot(1 - core, half)].astype(BF16)
     h_copy(c).start()
     value = hid_ref[...].astype(F32)
@@ -753,11 +782,11 @@
                 place = at + k + (rank * own_rows if k < own_rows else (tap_rows - chan // LANES))
                 flat[pl.ds(place, 1), :] = row[:, k * LANES : (k + 1) * LANES]
             at += tap_rows
-        lane = iota((1, LANES), 1)
         spread = jnp.zeros((1, LANES), F32)
         for k in range(2):
-            row = jnp.where(lane < heads, jnp.sum(ghead[k], axis=0, keepdims=True), 0.0)
-            spread = spread + pltpu.roll(row, 4 * heads * k + rank * heads, 1)
+            total = jnp.broadcast_to(jnp.sum(ghead[k], axis=1, keepdims=True), (heads, LANES))
+            place = iota((heads, LANES), 1) == 4 * heads * k + rank * heads + iota((heads, LANES), 0)
+            spread = spread + jnp.sum(jnp.where(place, total, 0.0), axis=0, keepdims=True)
         flat[at : at + 1] = spread
         at += 1
         for acc in (ggain, gskip):
@@ -963,7 +992,7 @@
         in_specs=[
             full(docs.shape), tok(model), early_tok(inner, mid), early_tok(inner, mid),
             early_tok(inner, 0), early_tok(inner, 0), early_tok(inner, 0),
-            tok(inner), tok(chan), tok(chan), tok(LANES),
+            tok(inner), tok(chan), tok(chan), pl.BlockSpec((heads, SPAN), lambda i: (0, count - 1 - i)),
             pl.BlockSpec((1, LANES, inner), lambda i: (count - 1 - i, 0, 0)),
             full(sums.shape),
         ]
@@ -974,8 +1003,9 @@
             vmem(side_shape, BF16), vmem(side_shape, BF16), vmem(side_shape, BF16), vmem(side_shape, BF16),
             vmem(w_in.shape, BF16), dma((len(big),)),
             vmem((SPAN + 8, chan), F32), vmem((SPAN + 8, LANES), F32), vmem((LANES, inner), F32),
-            vmem((8, LANES), F32), vmem((8, chan), F32), vmem((8, inner), F32),
-            vmem((5, 8, chan), F32), vmem((8, inner), F32), vmem((2, 8, LANES), F32),
+            vmem((2, heads, SPAN), F32), vmem((8, LANES), F32), vmem((8, chan), F32), vmem((8, inner), F32),
+            vmem((LANES, model), BF16), vmem((4, SPAN, inner), BF16),
+            vmem((5, 8, chan), F32), vmem((8, inner), F32), vmem((2, heads, SPAN), F32),
             vmem((8, inner), F32), vmem((8, model), F32),
             vmem((tokens, inner), BF16), vmem((tokens, inner), BF16), vmem((tokens, wide), BF16),
             vmem((tokens // 2, inner), F32), vmem((SPAN, LANES), F32), vmem((tokens // 2, LANES), F32),
@@ -1013,10 +1043,13 @@
     dims, cot_ref, delta_ref, layer_ref, gin_ref, flat_ref,
     out_ref, grad_ref, norm_ref, win_ref, taps_ref, bias_ref, dt_ref, decay_ref, skip_ref, gain_ref,
 ):
-    inner_all, heads = dims
+    inner_all, heads, turned = dims
     grad_ref[...] = cot_ref[...].astype(F32) + delta_ref[...].astype(F32)
     out_ref[...] = layer_ref[...]
-    win_ref[...] = gin_ref[:, 0 : win_ref.shape[1]]
+    if turned:
+        win_ref[...] = jnp.transpose(gin_ref[...])
+    else:
+        win_ref[...] = gin_ref[:, 0 : win_ref.shape[1]]
 
     @pl.when(pl.program_id(0) == 0)
     def _():
@@ -1031,7 +1064,7 @@
         for tap in range(taps_ref.shape[0]):
             spread(taps_ref, tap, at + tap * wide, wide)
         at += taps_ref.shape[0] * wide
-        spread(bias_ref, 0, at, wide)
+        bias_ref[...] = flat_ref[at : at + wide]
         at += wide
         dt_ref[...] = flat_ref[at : at + 1, 0:heads]
         decay_ref[...] = flat_ref[at : at + 1, heads : 2 * heads]
@@ -1050,7 +1083,7 @@
         skip_ref[...] = found[:, 0:heads]
 
 
-def finish(cotangent, delta, layer_out, grad_in, flat, columns, inner_all, heads):
+def finish(cotangent, delta, layer_out, grad_in, flat, columns, inner_all, heads, turned):
     tokens, model = cotangent.shape
     depth = grad_in.shape[0]
     steps = 8
@@ -1062,18 +1095,20 @@
     def full(shape):
         return pl.BlockSpec(shape, lambda i: (0,) * len(shape))
 
-    small = [(1, model), (4, chan_all), (1, chan_all), (1, heads), (1, heads), (1, heads), (1, inner_all)]
-    if depth % (8 * steps) == 0:
-        rows, shown = tok(depth, grad_in.shape[1]), tok(depth, columns)
+    small = [(1, model), (4, chan_all), (chan_all // LANES, LANES), (1, heads), (1, heads), (1, heads), (1, inner_all)]
+    if turned:
+        cut = grad_in.shape[1] // (steps - 1)
+        rows = pl.BlockSpec((depth, cut), lambda i: (0, i - i // (steps - 1)))
+        shown = pl.BlockSpec((cut, depth), lambda i: (i - i // (steps - 1), 0))
     else:
         rows, shown = full(grad_in.shape), full((depth, columns))
     return pl.pallas_call(
-        lambda *refs: finish_kernel((inner_all, heads), *refs),
+        lambda *refs: finish_kernel((inner_all, heads, turned), *refs),
         out_shape=[
             jax.ShapeDtypeStruct((tokens, model), BF16),
             jax.ShapeDtypeStruct((tokens, model), F32),
             jax.ShapeDtypeStruct(small[0], F32),
-            jax.ShapeDtypeStruct((depth, columns), F32),
+            jax.ShapeDtypeStruct((columns, depth) if turned else (depth, columns), F32),
         ]
         + [jax.ShapeDtypeStruct(v, F32) for v in small[1:]],
         grid=(steps,),
@@ -1089,41 +1124,66 @@
     dims, hid_ref, cot_ref, ngain_ref, w_ref, step_ref, wo_ref,
     win_ref, wout_ref, normed_ref, *refs,
 ):
-    lines, depth, inner, inner_all, aligned = dims
-    outs = refs[:4] if aligned else ()
-    mine, zsend, zrecv, xsend, xrecv, takes, puts = refs[len(outs):]
+    lines, depth, inner, inner_all, heads, turned = dims
+    outs = refs[:4] if turned else ()
+    mine, zsend, zrecv, xsend, xrecv, takes, puts, qsend, qrecv = refs[len(outs):]
     trank, drank = lax.axis_index("tensor"), lax.axis_index("dp")
     line, side = drank // 2, drank % 2
+    core = trank % 2
     model = hid_ref.shape[1]
     off = pl.multiple_of(trank * inner, LANES)
-    pieces = (
-        (w_ref, inner_all + off, win_ref, inner, inner),
-        (w_ref, 2 * inner_all, win_ref, 2 * inner, 2 * LANES),
-        (step_ref, 0, win_ref, 2 * inner + 2 * LANES, LANES),
-        (w_ref, off, win_ref, 0, inner),
-        (wo_ref, 0, wout_ref, 0, inner),
-    )
+    base = 2 * inner_all
+    if turned:
+        quarter = 2 * LANES // 4
+        own_quarter = pl.multiple_of(trank * quarter, quarter)
+        chip = 2 * heads
+        steps = pl.multiple_of(base + 2 * LANES + (trank // 2) * chip, chip)
+        cut = inner // 2
+        pieces = [
+            (w_ref, base + own_quarter, win_ref, 2 * inner + own_quarter, quarter),
+            (w_ref, steps, win_ref, 2 * inner + 2 * LANES, chip),
+        ]
+        pieces += [(w_ref, inner_all + off + k * cut, win_ref, inner + k * cut, cut) for k in range(2)]
+        pieces += [(w_ref, off + k * cut, win_ref, k * cut, cut) for k in range(2)]
+        pieces += [(wo_ref, k * LANES, wout_ref, k * LANES, LANES) for k in range(inner // LANES)]
+    else:
+        pieces = [
+            (w_ref, inner_all + off, win_ref, inner, inner),
+            (w_ref, base, win_ref, 2 * inner, 2 * LANES),
+            (step_ref, 0, win_ref, 2 * inner + 2 * LANES, LANES),
+            (w_ref, off, win_ref, 0, inner),
+            (wo_ref, 0, wout_ref, 0, inner),
+        ]
 
     def peer(step):
         return {"dp": lax.rem(line + step, lines) * 2 + side}
 
     partner = {"dp": line * 2 + 1 - side}
+    family = (
+        {"tensor": trank + 1 - 2 * core}, {"tensor": (trank + 2) % 4},
+        {"tensor": (trank + 3 - 2 * core) % 4},
+    )
+    others = [partner] + [peer(step) for step in range(1, lines)] + (list(family) if turned else [])
     barrier = pltpu.get_barrier_semaphore()
-    for step in range(1, lines):
-        pl.semaphore_signal(barrier, inc=1, device_id=peer(step), device_id_type=MESH_IDS)
-    pl.semaphore_signal(barrier, inc=1, device_id=partner, device_id_type=MESH_IDS)
-    pl.semaphore_wait(barrier, lines)
-
-    def rows(index):
+    for device in others:
+        pl.semaphore_signal(barrier, inc=1, device_id=device, device_id_type=MESH_IDS)
+    pl.semaphore_wait(barrier, len(others))
+
+    def lanes_of(index):
         return pl.ds(pl.multiple_of(index * depth, depth), depth)
+
+    def in_rows(p):
+        return turned and pieces[p][0] is w_ref
 
     def block(p, index):
         _, _, dst, at, width = pieces[p]
-        return dst.at[rows(index), pl.ds(at, width)]
+        if in_rows(p):
+            return dst.at[pl.ds(at, width), lanes_of(index)]
+        return dst.at[lanes_of(index), pl.ds(at, width)]
 
     def own(p):
         src, at, _, _, width = pieces[p]
-        return src.at[:, pl.ds(at, width)]
+        return src.at[pl.ds(at, width)] if in_rows(p) else src.at[:, pl.ds(at, width)]
 
     def z_copy(p, step, src, index):
         return pltpu.make_async_remote_copy(
@@ -1144,8 +1204,16 @@
         x_copy(p, 0, own(p), drank).start()
     spots, at = [], 0
     for p in range(count):
-        spots.append(mine.at[:, pl.ds(at, pieces[p][4])])
-        at += pieces[p][4]
+        width = pieces[p][4]
+        if in_rows(p):
+            spots.append(mine.at[pl.ds(at, width), pl.ds(0, depth)])
+            at += width
+        elif turned:
+            spots.append(mine.at[pl.ds(at, depth), pl.ds(0, width)])
+            at += depth
+        else:
+            spots.append(mine.at[:, pl.ds(at, width)])
+            at += width
     fetched = [pltpu.make_async_copy(own(p), spots[p], takes.at[p]) for p in range(count)]
     for copy in fetched:
         copy.start()
@@ -1156,15 +1224,15 @@
         value = hid[...].astype(F32)
         inv = lax.rsqrt(jnp.mean(value * value, -1, keepdims=True) + EPS)
         normed[...] = (value * inv * gain).astype(BF16)
-        if aligned:
+        if turned:
             for src, away, here in (
                 (normed, sorted_refs[0], sorted_refs[1]), (cot, sorted_refs[2], sorted_refs[3]),
             ):
                 for j in range(lines):
                     first = lax.rem(line + j, lines) * 2
                     lanes = slice(j * depth, (j + 1) * depth)
-                    away[:, lanes] = src[:, pl.ds(pl.multiple_of((first + 1 - side) * depth, depth), depth)]
-                    here[:, lanes] = src[:, pl.ds(pl.multiple_of((first + side) * depth, depth), depth)]
+                    away[:, lanes] = src[:, lanes_of(first + 1 - side)]
+                    here[:, lanes] = src[:, lanes_of(first + side)]
 
     full = pl.BlockSpec((SPAN, model), lambda i: (i, 0))
     half = pl.BlockSpec((SPAN, lines * depth), lambda i: (i, 0))
@@ -1177,46 +1245,83 @@
     for p in range(count):
         fetched[p].wait()
         stored[p].start()
+
+    def source_line(step):
+        return lax.rem(line - step + lines, lines) * 2
+
+    def x_arrived(p):
+        for step in range(lines):
+            source = source_line(step) + 1 - side
+            x_copy(p, step, block(p, source), source).wait_recv()
+
+    def quarter_copy(k, device):
+        rows = win_ref.at[pl.ds(2 * inner + own_quarter, quarter)]
+        return pltpu.make_async_remote_copy(
+            src_ref=rows, dst_ref=rows, send_sem=qsend.at[k], recv_sem=qrecv.at[k],
+            device_id=device, device_id_type=MESH_IDS,
+        )
+
+    def quarter_from(k, owner):
+        rows = win_ref.at[pl.ds(pl.multiple_of(2 * inner + owner * quarter, quarter), quarter)]
+        return pltpu.make_async_remote_copy(
+            src_ref=rows, dst_ref=rows, send_sem=qsend.at[k], recv_sem=qrecv.at[k],
+            device_id=family[k], device_id_type=MESH_IDS,
+        )
+
     for p in range(count):
         for step in range(1, lines):
-            source = lax.rem(line - step + lines, lines) * 2 + side
+            source = source_line(step) + side
             got = block(p, source)
             z_copy(p, step, got, source).wait_recv()
             x_copy(p, step, got, source).start()
-    for p in range(count):
-        for step in range(lines):
-            source = lax.rem(line - step + lines, lines) * 2 + 1 - side
-            x_copy(p, step, block(p, source), source).wait_recv()
+        if turned and p == 3:
+            stored[0].wait()
+            x_arrived(0)
+            for k in range(3):
+                quarter_copy(k, family[k]).start()
+    for p in range(1 if turned else 0, count):
+        x_arrived(p)
+    if turned:
+        owners = (trank + 1 - 2 * core, (trank + 2) % 4, (trank + 3 - 2 * core) % 4)
+        for k in range(3):
+            quarter_from(k, owners[k]).wait_recv()
+            quarter_copy(k, family[k]).wait_send()
     for p in range(count):
         for step in range(1, lines):
             z_copy(p, step, own(p), drank).wait_send()
         for step in range(lines):
             x_copy(p, step, own(p), drank).wait_send()
-        stored[p].wait()
-
-
-def gather_weights(hidden, cotangent, norm_gain, in_weight, own_step, out_weight, lines, inner_all):
+        if not (turned and p == 0):
+            stored[p].wait()
+
+
+def gather_weights(
+    hidden, cotangent, norm_gain, in_weight, own_step, out_weight, lines, inner_all, heads, turned
+):
     tokens, model = hidden.shape
     depth, inner = out_weight.shape
-    aligned = depth % LANES == 0
-    width = 2 * inner + 3 * LANES
     half = jax.ShapeDtypeStruct((tokens, lines * depth), BF16)
     anywhere = pl.BlockSpec(memory_space=pl.ANY)
+    rows = 2 * inner + 2 * LANES + 2 * heads
+    width = 2 * inner + 3 * LANES
+    count = 6 + inner // LANES if turned else 5
     outs = (
-        jax.ShapeDtypeStruct((model, width), BF16),
+        jax.ShapeDtypeStruct((rows, model) if turned else (model, width), BF16),
         jax.ShapeDtypeStruct((model, inner), BF16),
         jax.ShapeDtypeStruct((tokens, model), BF16),
-    ) + (half,) * (4 if aligned else 0)
+    ) + (half,) * (4 if turned else 0)
     dma = pltpu.SemaphoreType.DMA
+    held = (rows + depth * (inner // LANES), LANES) if turned else (depth, width + inner)
+    fars = max(1, lines - 1)
     return pl.pallas_call(
-        lambda *refs: gather_kernel((lines, depth, inner, inner_all, aligned), *refs),
+        lambda *refs: gather_kernel((lines, depth, inner, inner_all, heads, turned), *refs),
         out_shape=outs,
         in_specs=[anywhere, anywhere, pl.BlockSpec(memory_space=pltpu.VMEM)] + [anywhere] * 3,
         out_specs=(anywhere,) * len(outs),
         scratch_shapes=[
-            pltpu.VMEM((depth, width + inner), BF16),
-            dma((5, max(1, lines - 1))), dma((5, max(1, lines - 1))), dma((5, lines)), dma((5, lines)),
-            dma((5,)), dma((5,)),
+            pltpu.VMEM(held, BF16),
+            dma((count, fars)), dma((count, fars)), dma((count, lines)), dma((count, lines)),
+            dma((count,)), dma((count,)), dma((3,)), dma((3,)),
         ],
         compiler_params=pltpu.CompilerParams(collective_id=0, has_side_effects=True),
         cost_estimate=cost(45.0),
@@ -1242,14 +1347,25 @@
     def line_to(step):
         return lambda k: ((k // 2 + step) % lines) * 2 + k % 2
 
-    own_step = jnp.pad(
-        lax.dynamic_slice_in_dim(in_weight, base_dt + trank * heads, heads, 1),
-        ((0, 0), (0, LANES - heads)),
+    turned = depth % LANES == 0
+    if turned:
+        weight_in = own_step = in_weight.T
+    else:
+        weight_in = in_weight
+        own_step = jnp.pad(
+            lax.dynamic_slice_in_dim(in_weight, base_dt + trank * heads, heads, 1),
+            ((0, 0), (0, LANES - heads)),
+        )
+    w_in, w_out, normed, *sorted_parts = gather_weights(
+        hidden_in, cotangent, norm_gain.reshape(1, -1), weight_in, own_step,
+        out_weight, lines, inner_all, heads, turned,
     )
-    w_in, w_out, normed, *sorted_parts = gather_weights(
-        hidden_in, cotangent, norm_gain.reshape(1, -1), in_weight, own_step, out_weight,
-        lines, inner_all,
-    )
+    if not turned:
+        pair = lax.dynamic_update_slice_in_dim(
+            jnp.zeros((2 * heads, model), BF16),
+            w_in[:, 2 * inner + 2 * LANES :][:, :heads].T, trank % 2 * heads, 0,
+        )
+        w_in = jnp.concatenate([w_in[:, : 2 * inner + 2 * LANES].T, pair], 0)
     if not sorted_parts:
 
         def features(v, which):
@@ -1267,7 +1383,7 @@
     def row(v):
         return v.reshape(1, -1)
 
-    params = (conv_weight, row(conv_bias), row(dt_bias), row(log_decay), row(skip_gain))
+    params = (conv_weight, conv_bias.reshape(-1, LANES), row(dt_bias), row(log_decay), row(skip_gain))
 
     early = 4
     *held, sums, mine, far = mixer_forward(
@@ -1278,10 +1394,10 @@
         mine, far, heads, lines, depth, early,
     )
     layer_out, grad_input, g_norm, grad_in_weight, taps, bias, dt, decay, skip, gain = finish(
-        cotangent, delta, layer_out, grad_in, flat, in_weight.shape[1], inner_all, head_all
+        cotangent, delta, layer_out, grad_in, flat, in_weight.shape[1], inner_all, head_all, turned
     )
     return (
-        layer_out, grad_input, g_norm.reshape(-1), grad_in_weight, taps, bias.reshape(-1),
+        layer_out, grad_input, g_norm.reshape(-1), grad_in_weight.T if turned else grad_in_weight, taps, bias.reshape(-1),
         dt.reshape(-1), decay.reshape(-1), skip.reshape(-1), gain.reshape(-1), g_out,
     )
 

time: 231 us -> 213 us (0.922)
  Pallas kernels: 220 us -> 211 us
  local copies, waits for them, and re-layouts: 7.72 us -> 0.71 us
    pallas_call x1, Pallas kernels: 59 us -> 51.1 us  [gather_weights(): pl.pallas_call(lambda *refs: gather_kernel((lines, depth, inner, inner_al...]
    unnamed x7 -> x3, local copies, waits for them, and re-layouts: 5.57 us -> 0.71 us
where the time goes in v2:
time: 213 us; the launch traced here: 212 us
  Pallas kernels  211 us (99%)
    pallas_call x1, Pallas kernels, mixer_backward(): pl.pallas_call(lambda *refs: backward_kernel((inner, heads, inner_all, li...  103 us
    pallas_call x1, Pallas kernels, gather_weights(): pl.pallas_call(lambda *refs: gather_kernel((lines, depth, inner, inner_al...  51.1 us
    pallas_call x1, Pallas kernels, mixer_forward(): pl.pallas_call(lambda *refs: forward_kernel((inner, heads, early), *refs)...  42.6 us
    pallas_call x1, Pallas kernels, finish(): pl.pallas_call(lambda *refs: finish_kernel((inner_all, heads, turned), *r...  13.6 us

profile of v2, /device:TPU:0, one launch (start us, length us, event | category | flops | bytes accessed | tf_op | source)
XLA Modules:
  0.0 212.0 jit_solution(3931192886127994828)
XLA Ops:
  0.6 51.1 %gather_weights.1 = (bf16[1296,1024]{1,0:T(8,128)(2,1)}, bf16[1024,512]{1,0:T(8,128)(2,1)}, bf16[2048,1024]{1,0:T(8,128)(2,1)}, bf16[2048,512]{1,0:T(8,128)(2,1)...) custom-call(bf16[2048,1024]{1,0:T(8,128)(2,1)} %refs_1_.3, ...), custom_call_target="tpu_custom_call" | custom-call | flops 51749998592 | bytes 1048576 | tf_op jit(solution)/shard_map/gather_weights/pallas_call | solution.py:1316
  51.8 42.6 %mixer_forward.1 = (f32[2048,512]{1,0:T(8,128)}, f32[2048,768]{1,0:T(8,128)}, f32[2048,768]{1,0:T(8,128)}, f32[2048,512]{1,0:T(8,128)}, f32[8,2048]{1,0:T(8,128)...) custom-call(s32[1,2048]{1,0:T(1,128)} %refs_0_.6, ...), custom_call_target="tpu_custom_call" | custom-call | flops 46000001024 | bytes 1048576 | tf_op jit(solution)/shard_map/mixer_forward/pallas_call | solution.py:345
  94.5 103.2 %mixer_backward.1 = (bf16[2048,1024]{1,0:T(8,128)(2,1)}, bf16[2048,1024]{1,0:T(8,128)(2,1)}, f32[128,4480]{1,0:T(8,128)}, f32[128,512]{1,0:T(8,128)}, f32[136,128]{1,0:T(8,128)}) custom-call(s32[1,2048]{1,0:T(1,128)} %refs_0_.6, bf16[2048,1024]{1,0:T(8,128)(2,1)} %refs_1_.3, f32[2048,512]{1,0:T(8,128)} %get-tuple-element.46.refs_2_.refs_4_, ...), custom_call_target="tpu_custom_call" | custom-call | flops 103499997184 | bytes 1048576 | tf_op jit(solution)/shard_map/mixer_backward/pallas_call | solution.py:982
  197.7 0.0 copy-start
  197.7 13.6 %finish.1 = (bf16[2048,1024]{1,0:T(8,128)(2,1)}, f32[2048,1024]{1,0:T(8,128)}, f32[1,1024]{1,0:T(1,128)}, f32[4384,128]{1,0:T(8,128)}, f32[4,2304]{1,0:T(4,128)}...) custom-call(bf16[2048,1024]{1,0:T(8,128)(2,1)} %refs_0_.7, ...), custom_call_target="tpu_custom_call" | custom-call | flops 10350000128 | bytes 1048576 | tf_op jit(solution)/shard_map/finish/pallas_call | solution.py:1105
  211.3 0.0 copy-done
  211.3 0.7 copy.24
Async XLA Ops:
  197.7 13.6 %copy-start = (f32[128,512]{1,0:T(8,128)S(1)}, f32[128,512]{1,0:T(8,128)}, u32[]{:S(2)}) copy-start(f32[128,512]{1,0:T(8,128)} %get-tuple-element.96) | copy-start | bytes 786436

commit v3 on v2

--- a/solution.py
+++ b/solution.py
@@ -135,18 +135,20 @@
 
 
 def forward_kernel(
-    dims, docs_ref, normed_ref, cot_ref, win_ref, wout_ref, cw_ref, cb_ref,
+    dims, docs_ref, normed_ref, cot_low_ref, cot_high_ref, win_ref, wo_ref, cw_ref, cb_ref,
     dtb_ref, dec_ref, skip_ref, ggain_ref,
-    gate_ref, mixed_ref, pre_ref, ssd_ref, stp_ref, state_ref, dn_ref,
-    sums_ref, mine_ref, far_ref,
-    xbuf, dbuf, state, par, skips, cwb, gain, gg_ref,
+    gate_ref, mixed_ref, pre_ref, ssd_ref, stp_ref, state_ref,
+    sums_ref, mine_ref, far_ref, wfull_ref,
+    xbuf, dbuf, state, par, skips, cwb, gain, gg_all,
     own_sums, h_out, h_in, kept, mine, far, h_sem, y_sem, s_in, s_sem, put_sem,
+    wout, oz_sem, ox_sem, own_sem,
 ):
-    inner, heads, early = dims
+    inner, heads, lines, depth, turned = dims
     pairs = heads // 2
     chan = inner + 2 * LANES
     i = pl.program_id(0)
-    spans = pl.num_programs(0)
+    spans = gg_all.shape[0] // SPAN
+    mid = spans // 2
     rank = lax.axis_index("tensor")
     core = rank % 2
     inner_all = ggain_ref.shape[1]
@@ -154,13 +156,58 @@
     across = {"tensor": rank + 1 - 2 * core}
     beyond = {"tensor": (rank + 2) % 4}
     crossed = {"tensor": (rank + 3 - 2 * core) % 4}
+    drank = lax.axis_index("dp")
+    line, side = drank // 2, drank % 2
+    partner = {"dp": line * 2 + 1 - side}
+    portions = 2 if turned else 0
+    cut = inner // 2
+
+    def peer(step):
+        return {"dp": lax.rem(line + step, lines) * 2 + side}
+
+    def o_block(p, index):
+        return wout.at[pl.ds(pl.multiple_of(index * depth, depth), depth), pl.ds(p * cut, cut)]
+
+    def own_block(p):
+        return wo_ref.at[:, pl.ds(p * cut, cut)]
+
+    def oz_copy(p, step, src, index):
+        return pltpu.make_async_remote_copy(
+            src_ref=src, dst_ref=o_block(p, index), send_sem=oz_sem.at[0, p, step - 1],
+            recv_sem=oz_sem.at[1, p, step - 1], device_id=peer(step), device_id_type=MESH_IDS,
+        )
+
+    def ox_copy(p, step, src, index):
+        return pltpu.make_async_remote_copy(
+            src_ref=src, dst_ref=o_block(p, index), send_sem=ox_sem.at[0, p, step],
+            recv_sem=ox_sem.at[1, p, step], device_id=partner, device_id_type=MESH_IDS,
+        )
+
+    def source(step):
+        return lax.rem(line - step + lines, lines) * 2
+
+    if turned:
+        own_copies = [
+            pltpu.make_async_copy(own_block(p), o_block(p, drank), own_sem.at[p]) for p in range(portions)
+        ]
+    else:
+        own_copies = [pltpu.make_async_copy(wo_ref, wout, own_sem.at[0])]
 
     @pl.when(i == 0)
     def _():
+        others = [across, beyond, crossed]
+        if turned:
+            others += [partner] + [peer(step) for step in range(1, lines)]
         barrier = pltpu.get_barrier_semaphore()
-        for device in (across, beyond, crossed):
+        for device in others:
             pl.semaphore_signal(barrier, inc=1, device_id=device, device_id_type=MESH_IDS)
-        pl.semaphore_wait(barrier, 3)
+        pl.semaphore_wait(barrier, len(others))
+        for p in range(portions):
+            for step in range(1, lines):
+                oz_copy(p, step, own_block(p), drank).start()
+            ox_copy(p, 0, own_block(p), drank).start()
+        for copy in own_copies:
+            copy.start()
         xbuf[0:8] = jnp.zeros((8, chan), F32)
         dbuf[0:8] = jnp.full((8, LANES), -1.0, F32)
         state[...] = jnp.zeros(state.shape, F32)
@@ -178,13 +225,15 @@
 
     def y_copy(k):
         return pltpu.make_async_remote_copy(
-            src_ref=mine.at[slot(k)], dst_ref=far.at[slot(k)], send_sem=y_sem.at[0, k],
-            recv_sem=y_sem.at[1, k], device_id=beyond, device_id_type=MESH_IDS,
+            src_ref=mine.at[slot(k)], dst_ref=far.at[slot(k // mid)], send_sem=y_sem.at[0, k // mid],
+            recv_sem=y_sem.at[1, k // mid], device_id=beyond, device_id_type=MESH_IDS,
         )
+
+    full_copy = pltpu.make_async_copy(wout, wfull_ref, put_sem.at[2])
 
     def join(k):
         h_copy(k).wait_recv()
-        mine[slot(k)] = (kept[slot(core)] + h_in[slot(k)].astype(F32)).astype(BF16)
+        mine[slot(k)] = (kept[k // mid, slot(core)] + h_in[slot(k)].astype(F32)).astype(BF16)
 
     nb = normed_ref[...]
     xbuf[8 : 8 + SPAN] = nt(nb, win_ref[inner : inner + chan])
@@ -193,7 +242,6 @@
     stp = jnp.where(core == 0, both_cores[0:heads], both_cores[heads:])
     stp_ref[...] = stp
     mixed_ref[...] = xbuf[8 : 8 + SPAN]
-    dn_ref[...] = nn(cot_ref[...], wout_ref[...])
 
     drow = docs_ref[:, pl.ds(pl.multiple_of(i * SPAN, SPAN), SPAN)].astype(F32)
     doc = jnp.broadcast_to(drow, (heads, SPAN))
@@ -223,7 +271,6 @@
     b_turned = jnp.transpose(b_act).astype(BF16)
     low_half = iota((SPAN, LANES), 1) < LANES // 2
     square = jnp.zeros((SPAN, LANES), F32)
-    cross = jnp.zeros((SPAN, LANES), F32)
     for pair in range(pairs):
         lanes = slice(pair * LANES, (pair + 1) * LANES)
         act = conv(pair)
@@ -255,23 +302,51 @@
         gated = ssd * (gate * sigmoid(gate))
         square = square + gated * gated
         gained = gain[0:1, lanes] * gated
-        gg_ref[:, lanes] = gained.astype(BF16)
-        cross = cross + dn_ref[:, lanes] * gained
+        gg_all[pl.ds(pl.multiple_of(i * SPAN, SPAN), SPAN), lanes] = gained.astype(BF16)
     own_sums[0, pl.ds(i, 1), :] = as_row(square)
-    own_sums[1, pl.ds(i, 1), :] = as_row(cross)
     xbuf[0:8] = xbuf[SPAN : SPAN + 8]
     dbuf[0:8] = dbuf[SPAN : SPAN + 8]
-    @pl.when(i > 0)
+
+    for p in range(portions):
+        @pl.when(i == p + 1)
+        def _():
+            for step in range(1, lines):
+                got = o_block(p, source(step) + side)
+                oz_copy(p, step, got, source(step) + side).wait_recv()
+                ox_copy(p, step, got, source(step) + side).start()
+
+    @pl.when(i == mid)
     def _():
+        for copy in own_copies:
+            copy.wait()
+        for p in range(portions):
+            for step in range(lines):
+                index = source(step) + 1 - side
+                ox_copy(p, step, o_block(p, index), index).wait_recv()
+        full_copy.start()
+
+    @pl.when(i > mid)
+    def _():
+        join(i - 1 - mid)
         join(i - 1)
 
-        @pl.when(i - 1 < early)
-        def _():
-            y_copy(i - 1).start()
-
-    kept[...] = nt(gg_ref[...], wout_ref[...])
-    h_out[slot(i)] = kept[slot(1 - core)].astype(BF16)
-    h_copy(i).start()
+    @pl.when(i == mid + 1)
+    def _():
+        y_copy(0).start()
+        y_copy(mid).start()
+
+    @pl.when(i >= mid)
+    def _():
+        for which, (k, cot_ref) in enumerate(((i - mid, cot_low_ref), (i, cot_high_ref))):
+            rows = gg_all[pl.ds(pl.multiple_of(k * SPAN, SPAN), SPAN)]
+            kept[which] = nt(rows, wout[...])
+            cross = jnp.zeros((SPAN, LANES), F32)
+            for group in range(wout.shape[0] // LANES):
+                lanes = slice(group * LANES, (group + 1) * LANES)
+                cross = cross + kept[which, :, lanes] * cot_ref[:, lanes].astype(F32)
+            own_sums[1, pl.ds(k, 1), :] = as_row(cross)
+            h_out[slot(k)] = kept[which, slot(1 - core)].astype(BF16)
+            h_copy(k).start()
 
     @pl.when(i == spans - 1)
     def _():
@@ -284,6 +359,7 @@
         sent = [s_copy(0, across), s_copy(1, beyond), s_copy(2, crossed)]
         for copy in sent:
             copy.start()
+        join(i - mid)
         join(i)
         mine_put = pltpu.make_async_copy(mine, mine_ref, put_sem.at[0])
         mine_put.start()
@@ -291,7 +367,7 @@
             copy.wait_recv()
         near = own_sums[...] + s_in[0]
         sums_ref[...] = near + (s_in[1] + s_in[2])
-        for k in range(early):
+        for k in (0, mid):
             y_copy(k).wait_recv()
         far_put = pltpu.make_async_copy(far, far_ref, put_sem.at[1])
         far_put.start()
@@ -303,20 +379,31 @@
             return carry
 
         lax.fori_loop(0, spans, drain, 0)
-        for k in range(early):
+        for k in (0, mid):
             y_copy(k).wait_send()
+        for p in range(portions):
+            for step in range(1, lines):
+                oz_copy(p, step, own_block(p), drank).wait_send()
+            for step in range(lines):
+                ox_copy(p, step, own_block(p), drank).wait_send()
         mine_put.wait()
         far_put.wait()
-
-
-def mixer_forward(docs, normed, cotangent, w_in, w_out, params, ggain, heads, early):
+        full_copy.wait()
+
+
+def mixer_forward(docs, normed, cotangent, w_in, w_out, params, ggain, heads, lines, turned):
     tokens, model = normed.shape
-    inner = w_out.shape[1]
+    depth, inner = w_out.shape
+    half = tokens // 2
+    mid = tokens // SPAN // 2
     chan = inner + 2 * LANES
     spans = tokens // SPAN
 
     def tok(width):
         return pl.BlockSpec((SPAN, width), lambda i: (i, 0))
+
+    def late(width, base):
+        return pl.BlockSpec((SPAN, width), lambda i: (base + (i - mid) * (i // mid), 0))
 
     def full(shape):
         return pl.BlockSpec(shape, lambda i: (0,) * len(shape))
@@ -330,32 +417,36 @@
         jax.ShapeDtypeStruct((tokens, inner), F32),
         jax.ShapeDtypeStruct((heads, tokens), F32),
         jax.ShapeDtypeStruct((spans, LANES, inner), BF16),
-        jax.ShapeDtypeStruct((tokens, inner), F32),
         jax.ShapeDtypeStruct(sums, F32),
         jax.ShapeDtypeStruct((tokens // 2, model), BF16),
-        jax.ShapeDtypeStruct((early * SPAN // 2, model), BF16),
+        jax.ShapeDtypeStruct((SPAN, model), BF16),
+        jax.ShapeDtypeStruct((model, inner), BF16),
     )
     out_specs = (
         tok(inner), tok(chan), tok(chan), tok(inner), pl.BlockSpec((heads, SPAN), lambda i: (0, i)),
         pl.BlockSpec((1, LANES, inner), lambda i: (i, 0, 0)),
-        tok(inner), full(sums), anywhere, anywhere,
+        full(sums), anywhere, anywhere, anywhere,
     )
-    consts = (w_in, w_out) + params + (ggain,)
+    consts = params + (ggain,)
     dma, vmem = pltpu.SemaphoreType.DMA, pltpu.VMEM
     return pl.pallas_call(
-        lambda *refs: forward_kernel((inner, heads, early), *refs),
+        lambda *refs: forward_kernel((inner, heads, lines, depth, turned), *refs),
         out_shape=outs,
         grid=(spans,),
-        in_specs=[full(docs.shape), tok(model), tok(model)] + [full(v.shape) for v in consts],
+        in_specs=[
+            full(docs.shape), tok(model), late(model, 0), late(model, mid), full(w_in.shape), anywhere,
+        ]
+        + [full(v.shape) for v in consts],
         out_specs=out_specs,
         scratch_shapes=[
             vmem((SPAN + 8, chan), F32), vmem((SPAN + 8, LANES), F32), vmem((LANES, inner), F32),
             vmem((2, heads, SPAN), F32), vmem((8, LANES), F32), vmem((8, chan), F32), vmem((8, inner), F32),
-            vmem((SPAN, inner), BF16), vmem(sums, F32),
+            vmem((tokens, inner), BF16), vmem(sums, F32),
             vmem((tokens // 2, model), BF16), vmem((tokens // 2, model), BF16),
-            vmem((SPAN, model), F32), vmem((tokens // 2, model), BF16),
-            vmem((early * SPAN // 2, model), BF16),
-            dma((2, spans)), dma((2, early)), vmem((3,) + sums, F32), dma((2, 3)), dma((2,)),
+            vmem((2, SPAN, model), F32), vmem((tokens // 2, model), BF16),
+            vmem((SPAN, model), BF16),
+            dma((2, spans)), dma((2, 2)), vmem((3,) + sums, F32), dma((2, 3)), dma((3,)),
+            vmem((model, inner), BF16), dma((2, 2, max(1, lines - 1))), dma((2, 2, lines)), dma((2,)),
         ],
         compiler_params=pltpu.CompilerParams(
             dimension_semantics=("arbitrary",), vmem_limit_bytes=VMEM_MOST,
@@ -363,28 +454,28 @@
         ),
         cost_estimate=cost(40.0),
         name="mixer_forward",
-    )(docs, normed, cotangent, *consts)
+    )(docs, normed, cotangent, cotangent, w_in, w_out, *consts)
 
 
 def backward_kernel(
     dims,
-    docs_ref, hid_ref, gate_ref, dn_ref, gate_low_ref, ssd_low_ref, dn_low_ref,
+    docs_ref, hid_ref, gate_ref, cot_ref, gate_low_ref, ssd_low_ref, cot_low_ref,
     ssd_ref, mixed_ref, pre_ref, stp_ref, state_ref, sums_ref,
     cw_ref, cb_ref, dtb_ref, dec_ref, skip_ref, ggain_ref, ngain_ref,
-    naway_ref, nhere_ref, caway_ref, chere_ref, w_ref, mine_ref, far_ref,
+    naway_ref, nhere_ref, caway_ref, chere_ref, w_ref, mine_ref, far_ref, wout_ref,
     delta_ref, layer_ref, gin_ref, gout_ref, flatout_ref,
-    naway, nhere, caway, chere, w, loads,
+    naway, nhere, caway, chere, w, wout, loads,
     pbuf, dbuf, dstate, par, skips, cwb, gain, w_step, sumv,
     gconv, gskip, ghead, ggain, gnorm,
-    nout_all, dgate_all, dall, dssd_low, inv_now, inv_own, hid_own,
+    nout_all, dgate_all, dall, dssd_low, inv_own, hid_own,
     h_out, mine, y_in, kept, h_sem, y_sem, d_sem, d_put,
     omine, ofar, oy_sem, o_sem, o_put,
     ax_out, ax_in, ax_sem, az_in, az_sem, atotal,
     sx_out, sx_in, sx_sem, sz_in, sz_sem, stotal, shere,
     vx_out, vx_in, vx_sem, vz_in, vz_sem, vtotal, vhere, vbuf,
-    gates, g_sem, values, v_sem, shared, s_sem, put_sem, flat, flat_in, f_sem,
+    gates, g_sem, values, v_sem, shared, shared_low, s_sem, put_sem, flat, flat_in, f_sem,
 ):
-    inner, heads, inner_all, lines, depth, early = dims
+    inner, heads, inner_all, lines, depth = dims
     pairs = heads // 2
     chan = inner + 2 * LANES
     width = inner + chan + LANES
@@ -421,14 +512,16 @@
         pltpu.make_async_copy(src, dst, loads.at[k])
         for k, (src, dst) in enumerate(
             (
-                (mine_ref, omine), (w_ref, w), (far_ref, ofar.at[pl.ds(0, early * half)]),
+                (mine_ref, omine), (w_ref, w), (far_ref.at[pl.ds(0, half)], ofar.at[pl.ds(0, half)]),
+                (far_ref.at[pl.ds(half, half)], ofar.at[pl.ds(mid * half, half)]),
                 (caway_ref, caway), (naway_ref, naway), (chere_ref, chere), (nhere_ref, nhere),
+                (wout_ref, wout),
             )
         )
     ]
 
     def oy_copy(k):
-        return remote(omine.at[lot(k, half)], ofar.at[lot(k, half)], oy_sem, k - early, beyond)
+        return remote(omine.at[lot(k, half)], ofar.at[lot(k, half)], oy_sem, k, beyond)
 
     def my_rows(k):
         return pl.ds(pl.multiple_of(k * SPAN + core * half, half), half)
@@ -446,7 +539,7 @@
         return pltpu.make_async_copy(mine.at[lot(k, half)], delta_ref.at[my_rows(k)], d_put.at[k])
 
     def h_copy(k):
-        return remote(h_out.at[lot(k, half)], mine.at[lot(k, half)], h_sem, k, across)
+        return remote(h_out.at[lot(k % 2, half)], mine.at[lot(k, half)], h_sem, k, across)
 
     def y_copy(k):
         return remote(mine.at[lot(k, half)], y_in.at[lot(k, half)], y_sem, k, beyond)
@@ -471,12 +564,13 @@
 
     @pl.when(i == 0)
     def _():
+        for copy in [fetch[-1]] + fetch[:-1]:
+            copy.start()
         barrier = pltpu.get_barrier_semaphore()
         for device in [across, beyond, partner] + [peer(step) for step in range(1, lines)]:
             pl.semaphore_signal(barrier, inc=1, device_id=device, device_id_type=MESH_IDS)
         pl.semaphore_wait(barrier, lines + 2)
-        for copy in fetch:
-            copy.start()
+        fetch[-1].wait()
         pbuf[SPAN : SPAN + 8] = jnp.zeros((8, chan), F32)
         dbuf[SPAN : SPAN + 8] = jnp.full((8, LANES), -2.0, F32)
         dstate[...] = jnp.zeros(dstate.shape, F32)
@@ -485,11 +579,12 @@
         for acc in (gconv, gskip, ghead, ggain, gnorm):
             acc[...] = jnp.zeros(acc.shape, F32)
         fetch[0].wait()
-        for k in range(early, count):
-            oy_copy(k).start()
+        for k in range(1, mid):
+            oy_copy(count - k).start()
+            oy_copy(mid - k).start()
 
     def join(k):
-        h_copy(k).wait_recv()
+        h_copy(k).wait()
         mine[lot(k, half)] = (kept[lot(core, half)] + mine[lot(k, half)].astype(F32)).astype(BF16)
         y_copy(k).start()
 
@@ -527,7 +622,7 @@
 
     @pl.when(i == mid)
     def _():
-        for copy in fetch[2:]:
+        for copy in fetch[2:-1]:
             copy.wait()
 
     hid_own[lot(c, half)] = hid_ref[lot(core, half)]
@@ -535,12 +630,11 @@
     def inverse(k):
         inv = lax.rsqrt(sums_ref[0, pl.ds(k, 1), :] * (1.0 / inner_all) + EPS)
         pull = sums_ref[1, pl.ds(k, 1), :] * (inv * inv * inv) * (1.0 / inner_all)
+        inv_own[pl.ds(k, 1), :] = jnp.where(core == 0, inv[:, 0:half], inv[:, half:])
         return inv, pull
 
-    def spread_inverse(k, cols, first):
+    def spread_inverse(cols, first):
         inv = jnp.broadcast_to(cols[:, first : first + 1], (SPAN, LANES))
-        inv_now[...] = inv
-        inv_own[lot(k, half)] = inv_now[lot(core, half)]
         return inv, jnp.broadcast_to(cols[:, first + 1 : first + 2], (SPAN, LANES))
 
     def gating(k, scales, lanes, gate_in, ssd_in, dn_in):
@@ -550,7 +644,7 @@
         silu = gate * sig
         ssd = ssd_in[:, lanes]
         gated = ssd * silu
-        dn = dn_in[:, lanes]
+        dn = dn_in
         g_l = gain[0:1, lanes]
         nout = gated * inv
         nout_all[lot(k, SPAN), lanes] = (nout * g_l).astype(BF16)
@@ -561,7 +655,7 @@
 
     def finish_out(k):
         total = omine[lot(k, half)].astype(F32) + ofar[lot(k, half)].astype(F32)
-        inv = inv_own[lot(k, half)]
+        inv = as_column(inv_own[pl.ds(k, 1), :], half)
         value = hid_own[lot(k, half)].astype(F32)
         for group in range(model // LANES):
             lanes = slice(group * LANES, (group + 1) * LANES)
@@ -586,13 +680,10 @@
         log_step, run_rows, cols = head_scales(raw, par[1], doc, enter, extra)
         dcol = jnp.broadcast_to(cols[:, 4 * heads : 4 * heads + 1], (SPAN, LANES))
         if first:
-            scales = spread_inverse(c, cols, 5 * heads)
-            low_scales = spread_inverse(c - mid, cols, 5 * heads + 2)
+            scales = spread_inverse(cols, 5 * heads)
+            low_scales = spread_inverse(cols, 5 * heads + 2)
         dbuf[0:SPAN] = dcol
         keeps = [None] + [dbuf[k : k + SPAN] == dcol for k in range(1, 4)]
-        if not first:
-            block = lax.rem(i - mid + 1, blocks)
-            ax_out[lot(block, LANES)] = out_grads(naway, caway, block).astype(BF16)
         row_i, col_i = iota((SPAN, SPAN), 0), iota((SPAN, SPAN), 1)
         same = jnp.concatenate([dcol, dcol], 1) == drow
         bias = jnp.where(same & (row_i <= col_i), 0.0, FAR)
@@ -622,9 +713,13 @@
             skip_l = pair_lanes(skips[0:1], 2 * pair, low_half[0:1])
             ssd = ssd_ref[:, lanes]
             if first:
-                d_ssd = gating(c, scales, lanes, gate_ref, ssd_ref, dn_ref)
+                if pair % 2 == 0:
+                    both = slice(pair * LANES, (pair + 2) * LANES)
+                    dn_both, dn_low_both = nn(cot_ref[...], wout[:, both]), nn(cot_low_ref[...], wout[:, both])
+                side_lanes = slice(pair % 2 * LANES, (pair % 2 + 1) * LANES)
+                d_ssd = gating(c, scales, lanes, gate_ref, ssd_ref, dn_both[:, side_lanes])
                 dssd_low[lot(c - mid, SPAN), lanes] = gating(
-                    c - mid, low_scales, lanes, gate_low_ref, ssd_low_ref, dn_low_ref
+                    c - mid, low_scales, lanes, gate_low_ref, ssd_low_ref, dn_low_both[:, side_lanes]
                 )
             else:
                 d_ssd = dssd_low[lot(c, SPAN), lanes]
@@ -720,13 +815,17 @@
 
     @pl.when(i >= mid)
     def _():
-        for k in (c + mid, c):
-            if k is not c:
-                oy_copy(k).wait_recv()
-                oy_copy(k).wait_send()
-            finish_out(k)
+        block = lax.rem(i - mid + 1, blocks)
+        ax_out[lot(block, LANES)] = out_grads(naway, caway, block).astype(BF16)
+        ax_copy(block).start()
+        @pl.when(i < count - 1)
+        def _():
+            for k in (c + mid, c):
+                oy_copy(k).wait()
+
+        finish_out(c + mid)
+        finish_out(c)
         scan_step(False)
-        ax_copy(lax.rem(i - mid + 1, blocks)).start()
 
     @pl.when(i > 0)
     def _():
@@ -751,7 +850,7 @@
         + nn(dall[rows_now, 0:chan], w[inner : inner + chan])
         + nn(dall[rows_now, chan:], w_step[...])
     )
-    h_out[lot(c, half)] = kept[lot(1 - core, half)].astype(BF16)
+    h_out[lot(c % 2, half)] = kept[lot(1 - core, half)].astype(BF16)
     h_copy(c).start()
     value = hid_ref[...].astype(F32)
     unit = value * lax.rsqrt(jnp.mean(value * value, -1, keepdims=True) + EPS)
@@ -759,16 +858,6 @@
 
     @pl.when(i == count - 1)
     def _():
-        sx_out[...] = tn(naway[...], dall[:, inner:]).astype(BF16)
-        for k in order:
-            sx_copy(k).start()
-        vx_out[LANES:] = tn(naway[:, LANES:], dall[:, 0:inner]).astype(BF16)
-        for k in order[:-1]:
-            vx_copy(k).start()
-        vx_out[0:LANES] = tn(naway[:, 0:LANES], dall[:, 0:inner]).astype(BF16)
-        vx_copy(0).start()
-        join(0)
-
         chan_all = inner_all + 2 * LANES
         tap_rows, own_rows = chan_all // LANES, inner // LANES
         flat[...] = jnp.zeros(flat.shape, F32)
@@ -795,11 +884,12 @@
                 flat[pl.ds(at + rank * own_rows + k, 1), :] = row[:, k * LANES : (k + 1) * LANES]
             at += inner_all // LANES
 
-        hops = [across, beyond, partner]
+        hops = [partner]
         bit = 1
         while bit < lines:
             hops.append({"dp": (line + bit * (1 - 2 * ((line // bit) % 2))) * 2 + side})
             bit *= 2
+        hops += [across, beyond]
         last = flat_in.shape[0] - 1
 
         def flat_copy(k):
@@ -817,8 +907,21 @@
                 flat_in[last] = held
 
         flat_copy(0).start()
+        sx_out[...] = tn(naway[...], dall[:, inner:]).astype(BF16)
+        for k in order:
+            sx_copy(k).start()
+        flat_step(0)
+        vx_out[LANES:] = tn(naway[:, LANES:], dall[:, 0:inner]).astype(BF16)
+        for k in order[:-1]:
+            vx_copy(k).start()
+        vx_out[0:LANES] = tn(naway[:, 0:LANES], dall[:, 0:inner]).astype(BF16)
+        vx_copy(0).start()
+        flat_step(1)
+        join(0)
 
         a_block(order[-1])
+        for k in range(2, len(hops) - 2):
+            flat_step(k)
         gain_row = ngain_ref[...]
 
         def finish_hidden(k, carry):
@@ -841,15 +944,14 @@
         for k in order:
             s_block(k)
         vhere[...] = tn(nhere[...], dall[:, 0:inner])
-        flat_step(0)
         lax.fori_loop(0, 3, down, 0)
         for k in order[:-1]:
             v_block(k)
-        flat_step(1)
+        flat_step(len(hops) - 2)
         for step in range(1, lines):
             az_copy(step).wait_recv()
             atotal[...] += az_in[step - 1].astype(F32)
-        gates[0] = atotal[:, inner:]
+        gates[0] = atotal[:, inner:].astype(BF16)
         gout_put = pltpu.make_async_copy(atotal.at[:, pl.ds(0, inner)], gout_ref, put_sem.at[9])
         gout_put.start()
         gate_near = remote(gates.at[0], gates.at[1], g_sem, 0, across)
@@ -861,22 +963,20 @@
             sz_copy(step).wait_recv()
             stotal[...] += sz_in[step - 1].astype(F32)
         shared_near = remote(shared.at[0], shared.at[1], s_sem, 0, across)
-        shared_far = remote(shared.at[2], shared.at[3], s_sem, 1, beyond)
+        shared_far = remote(shared_low.at[0], shared_low.at[1], s_sem, 1, beyond)
         shared[0, :, 0 : 2 * LANES] = stotal[:, 0 : 2 * LANES]
         steps = pltpu.roll(stotal[:, 2 * LANES :], rank * heads, 1)
         place = iota(steps.shape, 1) - rank * heads
         shared[0, :, 2 * LANES :] = jnp.where((place >= 0) & (place < heads), steps, 0.0)
         shared_near.start()
-        flat_step(2)
         v_block(order[-1])
         lax.fori_loop(3, 6, down, 0)
         shared_near.wait_recv()
-        shared[2] = shared[0] + shared[1]
+        shared_low[0] = (shared[0] + shared[1]).astype(BF16)
         shared_far.start()
         gate_far.wait_recv()
         gate_pass.start()
-        for k in range(3, len(hops)):
-            flat_step(k)
+        flat_step(len(hops) - 1)
         flat_put = pltpu.make_async_copy(flat_in.at[last], flatout_ref, put_sem.at[10])
         flat_put.start()
         lax.fori_loop(6, count, down, 0)
@@ -898,16 +998,20 @@
         owners = (rank, rank + 1 - 2 * core, (rank + 2) % 4, (rank + 3 - 2 * core) % 4)
         gate_near.wait_recv()
         gate_pass.wait_recv()
-        puts = [put(gates, k, 0, owners[k], k) for k in range(4)]
+        gate_puts = [put(vbuf, k, 0, owners[k], k) for k in range(4)]
+        for k in range(4):
+            vbuf[k] = gates[k].astype(F32)
+            gate_puts[k].start()
         shared_far.wait_recv()
-        shared[1] = shared[2] + shared[3]
-        puts.append(
+        shared[1] = shared_low[0].astype(F32) + shared_low[1].astype(F32)
+        puts = [
             pltpu.make_async_copy(
                 shared.at[1], gin_ref.at[:, pl.ds(2 * inner_all, 3 * LANES)], put_sem.at[8]
             )
-        )
-        for copy in puts:
-            copy.start()
+        ]
+        puts[0].start()
+        for copy in gate_puts:
+            copy.wait()
 
         def put_values(k):
             vbuf[k] = values[k].astype(F32)
@@ -924,7 +1028,6 @@
         put_values(3)
 
         def drain(k, carry):
-            h_copy(k).wait_send()
             d_copy(k).wait()
             d_local(k).wait()
             o_copy(k).wait()
@@ -947,10 +1050,10 @@
 
 
 def mixer_backward(
-    docs, hidden, held, sums, params, ggain, ngain, sorted_parts, w_in, mine, far,
-    heads, lines, depth, early,
+    docs, hidden, cotangent, held, sums, params, ggain, ngain, sorted_parts, w_in, mine, far, w_out,
+    heads, lines, depth,
 ):
-    gate, mixed, pre, ssd, stp, states, dn = held
+    gate, mixed, pre, ssd, stp, states = held
     tokens, inner = ssd.shape
     model = hidden.shape[1]
     chan = inner + 2 * LANES
@@ -977,10 +1080,10 @@
     anywhere = pl.BlockSpec(memory_space=pl.ANY)
     dma, vmem = pltpu.SemaphoreType.DMA, pltpu.VMEM
     consts = params + (ggain, ngain)
-    big = tuple(sorted_parts)[0:2] + tuple(sorted_parts)[2:4] + (w_in, mine, far)
+    big = tuple(sorted_parts)[0:2] + tuple(sorted_parts)[2:4] + (w_in, mine, far, w_out)
     side_shape = (tokens, lines * depth)
     return pl.pallas_call(
-        lambda *refs: backward_kernel((inner, heads, inner_all, lines, depth, early), *refs),
+        lambda *refs: backward_kernel((inner, heads, inner_all, lines, depth), *refs),
         out_shape=(
             jax.ShapeDtypeStruct((tokens, model), BF16),
             jax.ShapeDtypeStruct((tokens, model), BF16),
@@ -990,8 +1093,8 @@
         ),
         grid=(count,),
         in_specs=[
-            full(docs.shape), tok(model), early_tok(inner, mid), early_tok(inner, mid),
-            early_tok(inner, 0), early_tok(inner, 0), early_tok(inner, 0),
+            full(docs.shape), tok(model), early_tok(inner, mid), early_tok(model, mid),
+            early_tok(inner, 0), early_tok(inner, 0), early_tok(model, 0),
             tok(inner), tok(chan), tok(chan), pl.BlockSpec((heads, SPAN), lambda i: (0, count - 1 - i)),
             pl.BlockSpec((1, LANES, inner), lambda i: (count - 1 - i, 0, 0)),
             full(sums.shape),
@@ -1001,20 +1104,20 @@
         out_specs=(anywhere,) * 5,
         scratch_shapes=[
             vmem(side_shape, BF16), vmem(side_shape, BF16), vmem(side_shape, BF16), vmem(side_shape, BF16),
-            vmem(w_in.shape, BF16), dma((len(big),)),
+            vmem(w_in.shape, BF16), vmem(w_out.shape, BF16), dma((len(big) + 1,)),
             vmem((SPAN + 8, chan), F32), vmem((SPAN + 8, LANES), F32), vmem((LANES, inner), F32),
             vmem((2, heads, SPAN), F32), vmem((8, LANES), F32), vmem((8, chan), F32), vmem((8, inner), F32),
             vmem((LANES, model), BF16), vmem((4, SPAN, inner), BF16),
             vmem((5, 8, chan), F32), vmem((8, inner), F32), vmem((2, heads, SPAN), F32),
             vmem((8, inner), F32), vmem((8, model), F32),
             vmem((tokens, inner), BF16), vmem((tokens, inner), BF16), vmem((tokens, wide), BF16),
-            vmem((tokens // 2, inner), F32), vmem((SPAN, LANES), F32), vmem((tokens // 2, LANES), F32),
+            vmem((tokens // 2, inner), F32), vmem((count, LANES), F32),
             vmem((tokens // 2, model), BF16),
-            vmem((tokens // 2, model), BF16), vmem((tokens // 2, model), BF16),
+            vmem((SPAN, model), BF16), vmem((tokens // 2, model), BF16),
             vmem((tokens // 2, model), BF16), vmem((SPAN, model), F32),
             dma((2, count)), dma((2, count)), dma((2, count)), dma((count,)),
             vmem((tokens // 2, model), BF16), vmem((tokens // 2, model), BF16),
-            dma((2, count - early)), dma((2, count)), dma((count,)),
+            dma((2, count)), dma((2, count)), dma((count,)),
             vmem((blocks * LANES, 2 * inner), BF16), vmem((blocks * LANES, 2 * inner), BF16),
             dma((2, blocks)), vmem((fars, depth, 2 * inner), BF16), dma((2, fars)),
             vmem((depth, 2 * inner), F32),
@@ -1024,8 +1127,8 @@
             vmem((blocks * LANES, inner), BF16), vmem((blocks * LANES, inner), BF16),
             dma((2, blocks)), vmem((fars, depth, inner), BF16), dma((2, fars)), vmem((depth, inner), F32),
             vmem((blocks * LANES, inner), F32), vmem((4, depth, inner), F32),
-            vmem((4, depth, inner), F32), dma((2, 3)), vmem((4, depth, inner), BF16), dma((2, 3)),
-            vmem((4, depth, 3 * LANES), F32), dma((2, 2)), dma((11,)),
+            vmem((4, depth, inner), BF16), dma((2, 3)), vmem((4, depth, inner), BF16), dma((2, 3)),
+            vmem((2, depth, 3 * LANES), F32), vmem((2, depth, 3 * LANES), BF16), dma((2, 2)), dma((11,)),
             vmem((rows, LANES), F32), vmem((2 * hops + 1, rows, LANES), F32), dma((2, hops)),
         ],
         compiler_params=pltpu.CompilerParams(
@@ -1035,7 +1138,7 @@
         cost_estimate=cost(90.0),
         name="mixer_backward",
     )(
-        docs, hidden, gate, dn, gate, ssd, dn, ssd, mixed, pre, stp, states, sums, *consts, *big
+        docs, hidden, gate, cotangent, gate, ssd, cotangent, ssd, mixed, pre, stp, states, sums, *consts, *big
     )
 
 
@@ -1122,9 +1225,12 @@
 
 def gather_kernel(
     dims, hid_ref, cot_ref, ngain_ref, w_ref, step_ref, wo_ref,
-    win_ref, wout_ref, normed_ref, *refs,
+    win_ref, *refs,
 ):
     lines, depth, inner, inner_all, heads, turned = dims
+    wout_ref = None if turned else refs[0]
+    refs = refs[0 if turned else 1 :]
+    normed_ref, refs = refs[0], refs[1:]
     outs = refs[:4] if turned else ()
     mine, zsend, zrecv, xsend, xrecv, takes, puts, qsend, qrecv = refs[len(outs):]
     trank, drank = lax.axis_index("tensor"), lax.axis_index("dp")
@@ -1145,7 +1251,6 @@
         ]
         pieces += [(w_ref, inner_all + off + k * cut, win_ref, inner + k * cut, cut) for k in range(2)]
         pieces += [(w_ref, off + k * cut, win_ref, k * cut, cut) for k in range(2)]
-        pieces += [(wo_ref, k * LANES, wout_ref, k * LANES, LANES) for k in range(inner // LANES)]
     else:
         pieces = [
             (w_ref, inner_all + off, win_ref, inner, inner),
@@ -1304,14 +1409,15 @@
     anywhere = pl.BlockSpec(memory_space=pl.ANY)
     rows = 2 * inner + 2 * LANES + 2 * heads
     width = 2 * inner + 3 * LANES
-    count = 6 + inner // LANES if turned else 5
+    count = 6 if turned else 5
     outs = (
-        jax.ShapeDtypeStruct((rows, model) if turned else (model, width), BF16),
-        jax.ShapeDtypeStruct((model, inner), BF16),
-        jax.ShapeDtypeStruct((tokens, model), BF16),
-    ) + (half,) * (4 if turned else 0)
+        (jax.ShapeDtypeStruct((rows, model) if turned else (model, width), BF16),)
+        + (() if turned else (jax.ShapeDtypeStruct((model, inner), BF16),))
+        + (jax.ShapeDtypeStruct((tokens, model), BF16),)
+        + (half,) * (4 if turned else 0)
+    )
     dma = pltpu.SemaphoreType.DMA
-    held = (rows + depth * (inner // LANES), LANES) if turned else (depth, width + inner)
+    held = (rows, LANES) if turned else (depth, width + inner)
     fars = max(1, lines - 1)
     return pl.pallas_call(
         lambda *refs: gather_kernel((lines, depth, inner, inner_all, heads, turned), *refs),
@@ -1356,10 +1462,12 @@
             lax.dynamic_slice_in_dim(in_weight, base_dt + trank * heads, heads, 1),
             ((0, 0), (0, LANES - heads)),
         )
-    w_in, w_out, normed, *sorted_parts = gather_weights(
+    w_in, *rest = gather_weights(
         hidden_in, cotangent, norm_gain.reshape(1, -1), weight_in, own_step,
         out_weight, lines, inner_all, heads, turned,
     )
+    w_out, rest = (out_weight, rest) if turned else (rest[0], rest[1:])
+    normed, *sorted_parts = rest
     if not turned:
         pair = lax.dynamic_update_slice_in_dim(
             jnp.zeros((2 * heads, model), BF16),
@@ -1385,13 +1493,12 @@
 
     params = (conv_weight, conv_bias.reshape(-1, LANES), row(dt_bias), row(log_decay), row(skip_gain))
 
-    early = 4
-    *held, sums, mine, far = mixer_forward(
-        doc_ids, normed, cotangent, w_in, w_out, params, row(gate_gain), heads, early
+    *held, sums, mine, far, w_full = mixer_forward(
+        doc_ids, normed, cotangent, w_in, w_out, params, row(gate_gain), heads, lines, turned
     )
     delta, layer_out, grad_in, g_out, flat = mixer_backward(
-        doc_ids, hidden_in, held, sums, params, row(gate_gain), row(norm_gain), sorted_parts, w_in,
-        mine, far, heads, lines, depth, early,
+        doc_ids, hidden_in, cotangent, held, sums, params, row(gate_gain), row(norm_gain), sorted_parts, w_in,
+        mine, far, w_full, heads, lines, depth,
     )
     layer_out, grad_input, g_norm, grad_in_weight, taps, bias, dt, decay, skip, gain = finish(
         cotangent, delta, layer_out, grad_in, flat, in_weight.shape[1], inner_all, head_all, turned

time: 213 us -> 206 us (0.967)
  Pallas kernels: 211 us -> 203 us
    pallas_call x1, Pallas kernels: 51.1 us -> 38 us  [gather_weights(): pl.pallas_call(lambda *refs: gather_kernel((lines, depth, inner, inner_al...]
    pallas_call x1, Pallas kernels: 42.6 us -> 46.6 us  [mixer_forward(): pl.pallas_call(lambda *refs: forward_kernel((inner, heads, lines, depth,...]
where the time goes in v3:
time: 206 us; the launch traced here: 204 us
  Pallas kernels  203 us (99%)
    pallas_call x1, Pallas kernels, mixer_backward(): pl.pallas_call(lambda *refs: backward_kernel((inner, heads, inner_all, li...  104 us
    pallas_call x1, Pallas kernels, mixer_forward(): pl.pallas_call(lambda *refs: forward_kernel((inner, heads, lines, depth,...  46.6 us
    pallas_call x1, Pallas kernels, gather_weights(): pl.pallas_call(lambda *refs: gather_kernel((lines, depth, inner, inner_al...  38 us
    pallas_call x1, Pallas kernels, finish(): pl.pallas_call(lambda *refs: finish_kernel((inner_all, heads, turned), *r...  13.6 us

profile of v3, /device:TPU:0, one launch (start us, length us, event | category | flops | bytes accessed | tf_op | source)
XLA Modules:
  0.0 204.0 jit_solution(12725850608630473008)
XLA Ops:
  0.6 38.0 %gather_weights.1 = (bf16[1296,1024]{1,0:T(8,128)(2,1)}, bf16[2048,1024]{1,0:T(8,128)(2,1)}, bf16[2048,512]{1,0:T(8,128)(2,1)}, bf16[2048,512]{1,0:T(8,128)(2,1)...) custom-call(bf16[2048,1024]{1,0:T(8,128)(2,1)} %refs_1_.3, bf16[2048,1024]{1,0:T(8,128)(2,1)} %refs_0_.7, ...), custom_call_target="tpu_custom_call" | custom-call | flops 51749998592 | bytes 1048576 | tf_op jit(solution)/shard_map/gather_weights/pallas_call | solution.py:1422
  38.6 46.6 %mixer_forward.1 = (f32[2048,512]{1,0:T(8,128)}, f32[2048,768]{1,0:T(8,128)}, f32[2048,768]{1,0:T(8,128)}, f32[2048,512]{1,0:T(8,128)}, f32[8,2048]{1,0:T(8,128)...) custom-call(s32[1,2048]{1,0:T(1,128)} %refs_0_.6, ...), custom_call_target="tpu_custom_call" | custom-call | flops 46000001024 | bytes 1048576 | tf_op jit(solution)/shard_map/mixer_forward/pallas_call | solution.py:432
  85.3 104.4 %mixer_backward.1 = (bf16[2048,1024]{1,0:T(8,128)(2,1)}, bf16[2048,1024]{1,0:T(8,128)(2,1)}, f32[128,4480]{1,0:T(8,128)}, f32[128,512]{1,0:T(8,128)}, f32[136,128]{1,0:T(8,128)}) custom-call(s32[1,2048]{1,0:T(1,128)} %refs_0_.6, bf16[2048,1024]{1,0:T(8,128)(2,1)} %refs_1_.3, f32[2048,512]{1,0:T(8,128)} %get-tuple-element.44.refs_2_.refs_4_, ...), custom_call_target="tpu_custom_call" | custom-call | flops 103499997184 | bytes 1048576 | tf_op jit(solution)/shard_map/mixer_backward/pallas_call | solution.py:1085
  189.7 0.0 copy-start
  189.7 13.6 %finish.1 = (bf16[2048,1024]{1,0:T(8,128)(2,1)}, f32[2048,1024]{1,0:T(8,128)}, f32[1,1024]{1,0:T(1,128)}, f32[4384,128]{1,0:T(8,128)}, f32[4,2304]{1,0:T(4,128)}...) custom-call(bf16[2048,1024]{1,0:T(8,128)(2,1)} %refs_0_.7, ...), custom_call_target="tpu_custom_call" | custom-call | flops 10350000128 | bytes 1048576 | tf_op jit(solution)/shard_map/finish/pallas_call | solution.py:1208
  203.3 0.0 copy-done
  203.3 0.7 copy.24
Async XLA Ops:
  189.7 13.6 %copy-start = (f32[128,512]{1,0:T(8,128)S(1)}, f32[128,512]{1,0:T(8,128)}, u32[]{:S(2)}) copy-start(f32[128,512]{1,0:T(8,128)} %get-tuple-element.94) | copy-start | bytes 786436

commit v4 on v3

--- a/solution.py
+++ b/solution.py
@@ -473,7 +473,7 @@
     ax_out, ax_in, ax_sem, az_in, az_sem, atotal,
     sx_out, sx_in, sx_sem, sz_in, sz_sem, stotal, shere,
     vx_out, vx_in, vx_sem, vz_in, vz_sem, vtotal, vhere, vbuf,
-    gates, g_sem, values, v_sem, shared, shared_low, s_sem, put_sem, flat, flat_in, f_sem,
+    gates, g_sem, values, v_sem, shared, shared_low, shared_all, s_sem, put_sem, flat, flat_in, f_sem,
 ):
     inner, heads, inner_all, lines, depth = dims
     pairs = heads // 2
@@ -488,6 +488,7 @@
     half = SPAN // 2
     model = w.shape[1]
     blocks = lines * depth // LANES
+    turned = depth % LANES == 0
     rank, drank = lax.axis_index("tensor"), lax.axis_index("dp")
     line, side = drank // 2, drank % 2
     core = rank % 2
@@ -818,13 +819,6 @@
         block = lax.rem(i - mid + 1, blocks)
         ax_out[lot(block, LANES)] = out_grads(naway, caway, block).astype(BF16)
         ax_copy(block).start()
-        @pl.when(i < count - 1)
-        def _():
-            for k in (c + mid, c):
-                oy_copy(k).wait()
-
-        finish_out(c + mid)
-        finish_out(c)
         scan_step(False)
 
     @pl.when(i > 0)
@@ -832,7 +826,7 @@
         join(c + 1)
 
     order = tuple(range(1, blocks)) + (0,)
-    for k in range(blocks - 1):
+    for k in range(blocks - 2):
         @pl.when(i == mid + 1 + k)
         def _():
             a_block(order[k])
@@ -844,20 +838,29 @@
         own = jnp.where(core == 0, both_cores[0:heads], both_cores[heads:])
         w_step[...] = jnp.concatenate([own, jnp.zeros((LANES - heads, model), F32)], 0).astype(BF16)
 
-    rows_now = lot(c, SPAN)
-    kept[...] = (
-        nn(dgate_all[rows_now], w[0:inner])
-        + nn(dall[rows_now, 0:chan], w[inner : inner + chan])
-        + nn(dall[rows_now, chan:], w_step[...])
-    )
-    h_out[lot(c % 2, half)] = kept[lot(1 - core, half)].astype(BF16)
-    h_copy(c).start()
-    value = hid_ref[...].astype(F32)
-    unit = value * lax.rsqrt(jnp.mean(value * value, -1, keepdims=True) + EPS)
-    gnorm[...] += fold(kept[...] * unit)
+    def share_span():
+        rows_now = lot(c, SPAN)
+        kept[...] = (
+            nn(dgate_all[rows_now], w[0:inner])
+            + nn(dall[rows_now, 0:chan], w[inner : inner + chan])
+            + nn(dall[rows_now, chan:], w_step[...])
+        )
+        h_out[lot(c % 2, half)] = kept[lot(1 - core, half)].astype(BF16)
+        h_copy(c).start()
+        value = hid_ref[...].astype(F32)
+        unit = value * lax.rsqrt(jnp.mean(value * value, -1, keepdims=True) + EPS)
+        gnorm[...] += fold(kept[...] * unit)
+
+    @pl.when(i < count - 1)
+    def _():
+        share_span()
 
     @pl.when(i == count - 1)
     def _():
+        sx_out[...] = tn(naway[...], dall[:, inner:]).astype(BF16)
+        for k in order:
+            sx_copy(k).start()
+        share_span()
         chan_all = inner_all + 2 * LANES
         tap_rows, own_rows = chan_all // LANES, inner // LANES
         flat[...] = jnp.zeros(flat.shape, F32)
@@ -907,20 +910,26 @@
                 flat_in[last] = held
 
         flat_copy(0).start()
-        sx_out[...] = tn(naway[...], dall[:, inner:]).astype(BF16)
-        for k in order:
-            sx_copy(k).start()
-        flat_step(0)
         vx_out[LANES:] = tn(naway[:, LANES:], dall[:, 0:inner]).astype(BF16)
         for k in order[:-1]:
             vx_copy(k).start()
         vx_out[0:LANES] = tn(naway[:, 0:LANES], dall[:, 0:inner]).astype(BF16)
         vx_copy(0).start()
-        flat_step(1)
+        a_block(order[-2])
+        flat_step(0)
         join(0)
+        for k in range(count):
+            if k % mid:
+                oy_copy(k).wait()
+
+        def out_rows(k, carry):
+            finish_out(k)
+            return carry
+
+        lax.fori_loop(0, count, out_rows, 0)
 
         a_block(order[-1])
-        for k in range(2, len(hops) - 2):
+        for k in range(1, len(hops) - 2):
             flat_step(k)
         gain_row = ngain_ref[...]
 
@@ -993,20 +1002,26 @@
 
         def put(source, k, first, owner, index):
             column = pl.multiple_of(first + owner * inner, LANES)
-            return pltpu.make_async_copy(source.at[k], gin_ref.at[:, pl.ds(column, inner)], put_sem.at[index])
+            columns = pl.ds(column, inner)
+            dst = gin_ref.at[columns] if turned else gin_ref.at[:, columns]
+            return pltpu.make_async_copy(source.at[k], dst, put_sem.at[index])
+
+        def shown(v):
+            return jnp.transpose(v) if turned else v
 
         owners = (rank, rank + 1 - 2 * core, (rank + 2) % 4, (rank + 3 - 2 * core) % 4)
         gate_near.wait_recv()
         gate_pass.wait_recv()
         gate_puts = [put(vbuf, k, 0, owners[k], k) for k in range(4)]
         for k in range(4):
-            vbuf[k] = gates[k].astype(F32)
+            vbuf[k] = shown(gates[k].astype(F32))
             gate_puts[k].start()
         shared_far.wait_recv()
-        shared[1] = shared_low[0].astype(F32) + shared_low[1].astype(F32)
+        shared_all[...] = shown(shared_low[0].astype(F32) + shared_low[1].astype(F32))
+        shared_columns = pl.ds(2 * inner_all, 3 * LANES)
         puts = [
             pltpu.make_async_copy(
-                shared.at[1], gin_ref.at[:, pl.ds(2 * inner_all, 3 * LANES)], put_sem.at[8]
+                shared_all, gin_ref.at[shared_columns] if turned else gin_ref.at[:, shared_columns], put_sem.at[8]
             )
         ]
         puts[0].start()
@@ -1014,7 +1029,7 @@
             copy.wait()
 
         def put_values(k):
-            vbuf[k] = values[k].astype(F32)
+            vbuf[k] = shown(values[k].astype(F32))
             puts.append(put(vbuf, k, inner_all, owners[k], 4 + k))
             puts[-1].start()
 
@@ -1060,6 +1075,8 @@
     width = inner + chan + LANES
     wide = width - inner
     inner_all = ggain.shape[1]
+    turned = depth % LANES == 0
+    columns = 2 * inner_all + 3 * LANES
     count = tokens // SPAN
     mid = count // 2
     half = SPAN // 2
@@ -1087,7 +1104,7 @@
         out_shape=(
             jax.ShapeDtypeStruct((tokens, model), BF16),
             jax.ShapeDtypeStruct((tokens, model), BF16),
-            jax.ShapeDtypeStruct((depth, 2 * inner_all + 3 * LANES), F32),
+                jax.ShapeDtypeStruct((columns, depth) if turned else (depth, columns), F32),
             jax.ShapeDtypeStruct((depth, inner), F32),
             jax.ShapeDtypeStruct((rows, LANES), F32),
         ),
@@ -1126,9 +1143,10 @@
             vmem((depth, 3 * LANES), F32), vmem((blocks * LANES, 3 * LANES), F32),
             vmem((blocks * LANES, inner), BF16), vmem((blocks * LANES, inner), BF16),
             dma((2, blocks)), vmem((fars, depth, inner), BF16), dma((2, fars)), vmem((depth, inner), F32),
-            vmem((blocks * LANES, inner), F32), vmem((4, depth, inner), F32),
+            vmem((blocks * LANES, inner), F32), vmem((4, inner, depth) if turned else (4, depth, inner), F32),
             vmem((4, depth, inner), BF16), dma((2, 3)), vmem((4, depth, inner), BF16), dma((2, 3)),
-            vmem((2, depth, 3 * LANES), F32), vmem((2, depth, 3 * LANES), BF16), dma((2, 2)), dma((11,)),
+            vmem((2, depth, 3 * LANES), F32), vmem((2, depth, 3 * LANES), BF16),
+            vmem((3 * LANES, depth) if turned else (depth, 3 * LANES), F32), dma((2, 2)), dma((11,)),
             vmem((rows, LANES), F32), vmem((2 * hops + 1, rows, LANES), F32), dma((2, hops)),
         ],
         compiler_params=pltpu.CompilerParams(
@@ -1149,10 +1167,7 @@
     inner_all, heads, turned = dims
     grad_ref[...] = cot_ref[...].astype(F32) + delta_ref[...].astype(F32)
     out_ref[...] = layer_ref[...]
-    if turned:
-        win_ref[...] = jnp.transpose(gin_ref[...])
-    else:
-        win_ref[...] = gin_ref[:, 0 : win_ref.shape[1]]
+    win_ref[...] = gin_ref[...] if turned else gin_ref[:, 0 : win_ref.shape[1]]
 
     @pl.when(pl.program_id(0) == 0)
     def _():
@@ -1188,8 +1203,8 @@
 
 def finish(cotangent, delta, layer_out, grad_in, flat, columns, inner_all, heads, turned):
     tokens, model = cotangent.shape
-    depth = grad_in.shape[0]
-    steps = 8
+    depth = grad_in.shape[1] if turned else grad_in.shape[0]
+    steps = 2
     chan_all = inner_all + 2 * LANES
 
     def tok(v, size):
@@ -1200,9 +1215,8 @@
 
     small = [(1, model), (4, chan_all), (chan_all // LANES, LANES), (1, heads), (1, heads), (1, heads), (1, inner_all)]
     if turned:
-        cut = grad_in.shape[1] // (steps - 1)
-        rows = pl.BlockSpec((depth, cut), lambda i: (0, i - i // (steps - 1)))
-        shown = pl.BlockSpec((cut, depth), lambda i: (i - i // (steps - 1), 0))
+        cut = grad_in.shape[0] // steps
+        rows = shown = pl.BlockSpec((cut, grad_in.shape[1]), lambda i: (i, 0))
     else:
         rows, shown = full(grad_in.shape), full((depth, columns))
     return pl.pallas_call(
@@ -1250,7 +1264,7 @@
             (w_ref, steps, win_ref, 2 * inner + 2 * LANES, chip),
         ]
         pieces += [(w_ref, inner_all + off + k * cut, win_ref, inner + k * cut, cut) for k in range(2)]
-        pieces += [(w_ref, off + k * cut, win_ref, k * cut, cut) for k in range(2)]
+        pieces += [(w_ref, off + k * LANES, win_ref, k * LANES, LANES) for k in range(inner // LANES)]
     else:
         pieces = [
             (w_ref, inner_all + off, win_ref, inner, inner),
@@ -1409,7 +1423,7 @@
     anywhere = pl.BlockSpec(memory_space=pl.ANY)
     rows = 2 * inner + 2 * LANES + 2 * heads
     width = 2 * inner + 3 * LANES
-    count = 6 if turned else 5
+    count = 4 + inner // LANES if turned else 5
     outs = (
         (jax.ShapeDtypeStruct((rows, model) if turned else (model, width), BF16),)
         + (() if turned else (jax.ShapeDtypeStruct((model, inner), BF16),))

time: 206 us -> 202 us (0.981)
  Pallas kernels: 203 us -> 199 us
    pallas_call x1, Pallas kernels: 13.6 us -> 9.74 us  [finish(): pl.pallas_call(lambda *refs: finish_kernel((inner_all, heads, turned), *r...]
where the time goes in v4:
time: 202 us; the launch traced here: 200 us
  Pallas kernels  199 us (99%)
    pallas_call x1, Pallas kernels, mixer_backward(): pl.pallas_call(lambda *refs: backward_kernel((inner, heads, inner_all, li...  103 us
    pallas_call x1, Pallas kernels, mixer_forward(): pl.pallas_call(lambda *refs: forward_kernel((inner, heads, lines, depth,...  47.3 us
    pallas_call x1, Pallas kernels, gather_weights(): pl.pallas_call(lambda *refs: gather_kernel((lines, depth, inner, inner_al...  38.4 us
    pallas_call x1, Pallas kernels, finish(): pl.pallas_call(lambda *refs: finish_kernel((inner_all, heads, turned), *r...  9.74 us

profile of v4, /device:TPU:0, one launch (start us, length us, event | category | flops | bytes accessed | tf_op | source)
XLA Modules:
  0.0 200.2 jit_solution(14126516506209469840)
XLA Ops:
  0.6 38.4 %gather_weights.1 = (bf16[1296,1024]{1,0:T(8,128)(2,1)}, bf16[2048,1024]{1,0:T(8,128)(2,1)}, bf16[2048,512]{1,0:T(8,128)(2,1)}, bf16[2048,512]{1,0:T(8,128)(2,1)...) custom-call(bf16[2048,1024]{1,0:T(8,128)(2,1)} %refs_1_.3, bf16[2048,1024]{1,0:T(8,128)(2,1)} %refs_0_.7, ...), custom_call_target="tpu_custom_call" | custom-call | flops 51749998592 | bytes 1048576 | tf_op jit(solution)/shard_map/gather_weights/pallas_call | solution.py:1436
  39.1 47.3 %mixer_forward.1 = (f32[2048,512]{1,0:T(8,128)}, f32[2048,768]{1,0:T(8,128)}, f32[2048,768]{1,0:T(8,128)}, f32[2048,512]{1,0:T(8,128)}, f32[8,2048]{1,0:T(8,128)...) custom-call(s32[1,2048]{1,0:T(1,128)} %refs_0_.6, ...), custom_call_target="tpu_custom_call" | custom-call | flops 46000001024 | bytes 1048576 | tf_op jit(solution)/shard_map/mixer_forward/pallas_call | solution.py:432
  86.4 103.4 %mixer_backward.1 = (bf16[2048,1024]{1,0:T(8,128)(2,1)}, bf16[2048,1024]{1,0:T(8,128)(2,1)}, f32[4480,128]{1,0:T(8,128)}, f32[128,512]{1,0:T(8,128)}, f32[136,128]{1,0:T(8,128)}) custom-call(s32[1,2048]{1,0:T(1,128)} %refs_0_.6, bf16[2048,1024]{1,0:T(8,128)(2,1)} %refs_1_.3, f32[2048,512]{1,0:T(8,128)} %get-tuple-element.44.refs_2_.refs_4_, ...), custom_call_target="tpu_custom_call" | custom-call | flops 103499997184 | bytes 1048576 | tf_op jit(solution)/shard_map/mixer_backward/pallas_call | solution.py:1102
  189.8 0.0 copy-start
  189.8 9.7 %finish.1 = (bf16[2048,1024]{1,0:T(8,128)(2,1)}, f32[2048,1024]{1,0:T(8,128)}, f32[1,1024]{1,0:T(1,128)}, f32[4384,128]{1,0:T(8,128)}, f32[4,2304]{1,0:T(4,128)}...) custom-call(bf16[2048,1024]{1,0:T(8,128)(2,1)} %refs_0_.7, ...), custom_call_target="tpu_custom_call" | custom-call | flops 10350000128 | bytes 1048576 | tf_op jit(solution)/shard_map/finish/pallas_call | solution.py:1222
  199.5 0.0 copy-done
  199.5 0.7 copy.24
Async XLA Ops:
  189.8 9.8 %copy-start = (f32[128,512]{1,0:T(8,128)S(1)}, f32[128,512]{1,0:T(8,128)}, u32[]{:S(2)}) copy-start(f32[128,512]{1,0:T(8,128)} %get-tuple-element.94) | copy-start | bytes 786436
